TPU v7x, 512 devices: a whole 4x8x8 slice. The times are simulated.
512 devices in a mesh: row: 16 (over x, y_hi, core), col: 8 (over z), tp: 4 (over y_lo).
Axes of the slice: x: 4, y: 8 (y_hi: 2, y_lo: 4; y = y_hi * 4 + y_lo), z: 8, core: 2. Of those that a mesh axis runs over, the one named last changes fastest.
Arguments:
- latent: bfloat16 [256, 128, 1024], P('row', 'col'), may hold values from -6 to 6
- norm_gain: float32 [1024], replicated, may hold values from 0.1 to 1.9
- qkv_weight: bfloat16 [1024, 3, 1024], P(None, None, 'tp'), may hold values from -4 to 4
- out_weight: bfloat16 [1024, 1024], P('tp'), may hold values from -0.1875 to 0.1875
- cotangent: bfloat16 [256, 128, 1024], P('row', 'col'), may hold values from -6 to 6
Outputs:
- latent_grad: float32 [256, 128, 1024], P(('row', 'tp'), 'col')
All inputs are finite; a program needn't handle non-finite values.
Results may differ from a plain program's by a relative error of at most 0.009.
Values may be sent and summed in bfloat16 or wider, within the bound.
No kernel may reach another device: no remote copies, remote signals or barrier semaphores. Data moves between devices by JAX's collectives and lax.ppermute only.
A program may use at most 64 MiB of HBM per device.

v0:
```python
import jax
import jax.numpy as jnp
from jax import lax
from jax.sharding import PartitionSpec as P

HEAD_DIM = 64
RADIUS = 3


block_side = 8


def passed_along(block, axis, distance):
    devices = range(lax.axis_size(axis))
    route = [(i - distance, i) for i in devices if i - distance in devices]
    return lax.ppermute(block, axis, route)


def extended_2(block, sides, width):
    for axis, dim in sides:
        count = lax.axis_size(axis)
        forward = [(i, i + 1) for i in range(count - 1)]
        backward = [(target, source) for source, target in forward]
        low = lax.ppermute(
            lax.slice_in_dim(block, block.shape[dim] - width, None, axis=dim), axis, forward
        )
        high = lax.ppermute(lax.slice_in_dim(block, 0, width, axis=dim), axis, backward)
        block = jnp.concatenate([low, block, high], axis=dim)
    return block


def to_regions(field, block_rows, block_cols):
    region_side = block_side + 2 * RADIUS
    grow = block_side - 2 * RADIUS
    padded = jnp.pad(field, ((0, grow), (0, grow), (0, 0)))
    wide_cols = padded.shape[1]
    channels = padded.shape[2]
    span_rows = block_rows * block_side
    upper = padded[:span_rows].reshape(block_rows, block_side, wide_cols, channels)
    lower = padded[block_side : span_rows + block_side].reshape(
        block_rows, block_side, wide_cols, channels
    )[:, : 2 * RADIUS]
    banded = jnp.concatenate([upper, lower], axis=1)
    span_cols = block_cols * block_side
    left_part = banded[:, :, :span_cols].reshape(
        block_rows, region_side, block_cols, block_side, channels
    )
    right_part = banded[:, :, block_side : span_cols + block_side].reshape(
        block_rows, region_side, block_cols, block_side, channels
    )[:, :, :, : 2 * RADIUS]
    tiles = jnp.concatenate([left_part, right_part], axis=3).transpose(0, 2, 1, 3, 4)
    return tiles.reshape(block_rows, block_cols, region_side * region_side, channels)


def fold_lead(grads):
    block_count = grads.shape[0]
    middle = grads[:, RADIUS : RADIUS + block_side]
    top_rim = grads[:, :RADIUS]
    bottom_rim = grads[:, RADIUS + block_side :]
    middle = middle.at[1:, :RADIUS].add(bottom_rim[:-1])
    middle = middle.at[:-1, block_side - RADIUS :].add(top_rim[1:])
    rest = grads.shape[2:]
    return jnp.concatenate(
        [top_rim[0], middle.reshape((block_count * block_side,) + rest), bottom_rim[-1]], axis=0
    )


def from_regions(grads, block_rows, block_cols):
    region_side = block_side + 2 * RADIUS
    channels = grads.shape[-1]
    shaped = grads.reshape(block_rows, block_cols, region_side, region_side, channels).transpose(
        1, 3, 0, 2, 4
    )
    folded = fold_lead(shaped).transpose(1, 2, 0, 3)
    return fold_lead(folded)


def window_mask():
    region_side = block_side + 2 * RADIUS
    spots = jnp.arange(block_side, dtype=jnp.int32)[:, None]
    cells = jnp.arange(region_side, dtype=jnp.int32)[None, :]
    near = (cells >= spots) & (cells <= spots + 2 * RADIUS)
    both = near[:, None, :, None] & near[None, :, None, :]
    return both.reshape(block_side * block_side, region_side * region_side)


def core(query_blocks, upstream_blocks, key_regions, value_regions, allowed):
    scale = HEAD_DIM ** (-0.5)
    highest = lax.Precision.HIGHEST
    raw = jnp.einsum(
        "nqhd,nkhd->nhqk", query_blocks, key_regions, preferred_element_type=jnp.float32
    )
    scores = jnp.where(allowed[:, None], raw * scale, -1e30)
    peak = jnp.max(scores, axis=-1, keepdims=True)
    exponent = jnp.exp(scores - peak)
    weights = exponent / jnp.sum(exponent, axis=-1, keepdims=True)
    value_dots = jnp.einsum(
        "nqhd,nkhd->nhqk", upstream_blocks, value_regions, preferred_element_type=jnp.float32
    )
    centre = jnp.sum(weights * value_dots, axis=-1, keepdims=True)
    score_grads = weights * (value_dots - centre)
    query_grad = (
        jnp.einsum(
            "nhqk,nkhd->nqhd", score_grads, key_regions.astype(jnp.float32), precision=highest
        )
        * scale
    )
    key_grad = (
        jnp.einsum(
            "nhqk,nqhd->nkhd", score_grads, query_blocks.astype(jnp.float32), precision=highest
        )
        * scale
    )
    value_grad = jnp.einsum(
        "nhqk,nqhd->nkhd", weights, upstream_blocks.astype(jnp.float32), precision=highest
    )
    return (query_grad, key_grad, value_grad)


def attend(query, grad_out, neighbours, valid_cells):
    tile_rows, tile_cols, head_cols = query.shape
    head_count = head_cols // HEAD_DIM
    block_rows = tile_rows // block_side
    block_cols = tile_cols // block_side
    block_count = block_rows * block_cols
    cells = block_side * block_side

    def to_blocks(field):
        shaped = field.reshape(block_rows, block_side, block_cols, block_side, head_count, HEAD_DIM)
        return shaped.transpose(0, 2, 1, 3, 4, 5).reshape(block_count, cells, head_count, HEAD_DIM)

    query_blocks = to_blocks(query)
    upstream_blocks = to_blocks(grad_out)
    regions = to_regions(neighbours, block_rows, block_cols)
    region_cells = regions.shape[2]
    regions = regions.reshape(block_count, region_cells, 2 * head_cols)
    key_regions = regions[..., :head_cols].reshape(block_count, region_cells, head_count, HEAD_DIM)
    value_regions = regions[..., head_cols:].reshape(
        block_count, region_cells, head_count, HEAD_DIM
    )
    valid_regions = to_regions(valid_cells[:, :, None], block_rows, block_cols)[..., 0]
    valid_regions = valid_regions.reshape(block_count, region_cells)
    allowed = window_mask()[None] & valid_regions[:, None, :]
    query_grad, key_grad, value_grad = core(
        query_blocks, upstream_blocks, key_regions, value_regions, allowed
    )
    query_grad = query_grad.reshape(block_rows, block_cols, block_side, block_side, head_cols)
    query_grad = query_grad.transpose(0, 2, 1, 3, 4).reshape(tile_rows, tile_cols, head_cols)
    pair_grad = jnp.concatenate(
        [
            key_grad.reshape(block_count, region_cells, head_cols),
            value_grad.reshape(block_count, region_cells, head_cols),
        ],
        axis=-1,
    )
    spread = from_regions(
        pair_grad.reshape(block_rows, block_cols, region_cells, 2 * head_cols),
        block_rows,
        block_cols,
    )
    return (query_grad, spread)


def fold_rows(extended):
    upper = extended[:RADIUS]
    lower = extended[-RADIUS:]
    middle = extended[RADIUS:-RADIUS]
    from_below = passed_along(upper.astype(jnp.bfloat16), "row", -1).astype(upper.dtype)
    from_above = passed_along(lower.astype(jnp.bfloat16), "row", 1).astype(lower.dtype)
    middle = middle.at[:RADIUS].add(from_above)
    return middle.at[-RADIUS:].add(from_below)


def fold_cols(extended):
    left_rim = extended[:, :RADIUS]
    right_rim = extended[:, -RADIUS:]
    middle = extended[:, RADIUS:-RADIUS]
    from_right = passed_along(left_rim.astype(jnp.bfloat16), "col", -1).astype(left_rim.dtype)
    from_left = passed_along(right_rim.astype(jnp.bfloat16), "col", 1).astype(right_rim.dtype)
    middle = middle.at[:, :RADIUS].add(from_left)
    return middle.at[:, -RADIUS:].add(from_right)


def inside_mask(count, place, total):
    position = place * count - RADIUS + jnp.arange(count + 2 * RADIUS, dtype=jnp.int32)
    return (position >= 0) & (position < count * total)


def per_device(latent, norm_gain, qkv_weight, out_weight, cotangent):
    tile_rows, tile_cols, model_width = latent.shape
    head_cols = out_weight.shape[0]
    token_count = tile_rows * tile_cols
    own_tokens = token_count // lax.axis_size("tp")
    latent_f32 = latent.astype(jnp.float32)
    inverse = lax.rsqrt(jnp.mean(latent_f32 * latent_f32, axis=-1, keepdims=True) + 1e-06)
    unit = latent_f32 * inverse
    normed = (unit * norm_gain).astype(jnp.bfloat16).reshape(token_count, model_width)
    projection = qkv_weight.reshape(model_width, 3 * head_cols)
    projected = jnp.dot(normed, projection, preferred_element_type=jnp.float32).astype(jnp.bfloat16)
    projected = projected.reshape(token_count, 3, head_cols)
    query = projected[:, 0].reshape(tile_rows, tile_cols, head_cols)
    pairs = jnp.concatenate([projected[:, 1], projected[:, 2]], axis=-1).reshape(
        tile_rows, tile_cols, 2 * head_cols
    )
    neighbours = extended_2(pairs, (("row", 0), ("col", 1)), RADIUS)
    upstream_flat = cotangent.reshape(token_count, model_width)
    grad_out = lax.dot_general(
        upstream_flat, out_weight, (((1,), (1,)), ((), ())), preferred_element_type=jnp.float32
    ).astype(jnp.bfloat16)
    grad_out = grad_out.reshape(tile_rows, tile_cols, head_cols)
    row_mask = inside_mask(tile_rows, lax.axis_index("row"), lax.axis_size("row"))
    col_mask = inside_mask(tile_cols, lax.axis_index("col"), lax.axis_size("col"))
    valid_cells = row_mask[:, None] & col_mask[None, :]
    query_grad, spread = attend(query, grad_out, neighbours, valid_cells)
    gathered = fold_cols(fold_rows(spread))
    stacked = jnp.stack([query_grad, gathered[..., :head_cols], gathered[..., head_cols:]], axis=2)
    stacked = stacked.astype(jnp.bfloat16).reshape(token_count, 3 * head_cols)
    first_row = lax.axis_index("tp") * own_tokens
    full_term = lax.dot_general(
        stacked, projection, (((1,), (1,)), ((), ())), preferred_element_type=jnp.float32
    )
    summed_full = lax.psum(full_term.astype(jnp.bfloat16), "tp").astype(jnp.float32)
    summed = lax.dynamic_slice_in_dim(summed_full, first_row, own_tokens, 0)
    own_unit = lax.dynamic_slice_in_dim(
        unit.reshape(token_count, model_width), first_row, own_tokens, 0
    )
    own_inverse = lax.dynamic_slice_in_dim(
        inverse.reshape(token_count, 1), first_row, own_tokens, 0
    )
    own_upstream = lax.dynamic_slice_in_dim(upstream_flat, first_row, own_tokens, 0).astype(
        jnp.float32
    )
    scaled = summed * norm_gain
    stat = jnp.mean(scaled * own_unit, axis=-1, keepdims=True)
    result = own_upstream + own_inverse * (scaled - own_unit * stat)
    return result.reshape(own_tokens // tile_cols, tile_cols, model_width)


def solution(mesh):
    placed = (P("row", "col", None), P(), P(None, None, "tp"), P("tp", None), P("row", "col", None))
    return jax.shard_map(
        per_device,
        mesh=mesh,
        in_specs=placed,
        out_specs=P(("row", "tp"), "col", None),
        check_vma=False,
    )
```

profile of v0, /device:TPU:6, one launch (start us, length us, event | category | flops | bytes accessed | tf_op | source)
XLA Modules:
  0.0 160.9 jit_solution(3580214283583071866)
XLA Ops:
  6.5 1.3 fusion.11
  7.8 1.8 %copy.40 = bf16[1024,3,256]{0,2,1:T(8,128)(2,1)S(1)} copy(bf16[1024,3,256]{2,0,1:T(8,128)(2,1)} %param.23) | data formatting | bytes 3145728 | tf_op args[2]
  9.7 1.4 multiply_convert_fusion
  11.0 0.6 convolution_convert_fusion.1
  11.7 0.2 copy.41
  12.1 7.4 %collective-permute-start.1 = (bf16[3,16,512]{2,1,0:T(8,128)(2,1)S(1)}, bf16[3,16,512]{2,1,0:T(8,128)(2,1)S(1)}, u32[]{:S(2)}, u32[]{:S(2)}) collective-permute-start(bf16[3,16,512]{2,1,0:T(8,128)(2,1)S(1)} %bitcast.130), channel_id=1, source_target_pairs={{32,0},{64,32},{96,64},{128,96},{160,128},{192,160},{224,192},{256... | collective-permute-start | bytes 147464 | tf_op jit(solution)/shard_map/ppermute | solution.py:27
  19.7 1.9 %collective-permute-start = (bf16[3,16,512]{2,1,0:T(8,128)(2,1)S(1)}, bf16[3,16,512]{2,1,0:T(8,128)(2,1)S(1)}, u32[]{:S(2)}, u32[]{:S(2)}) collective-permute-start(bf16[3,16,512]{2,1,0:T(8,128)(2,1)S(1)} %bitcast.131), channel_id=1, source_target_pairs={{0,32},{32,64},{64,96},{96,128},{128,160},{160,192},{192,224},{224... | collective-permute-start | bytes 147464 | tf_op jit(solution)/shard_map/ppermute | solution.py:24
  22.1 0.1 copy.52
  22.3 0.1 broadcast_and_fusion
  22.5 0.3 and.121
  22.8 0.3 convolution_convert_fusion.2
  23.2 0.7 and_reduce_fusion.1
  23.9 0.7 and_reduce_fusion
  24.6 0.2 reshape_reshape.8
  25.0 0.2 reshape_reshape_squeeze.3
  25.4 4.5 %collective-permute-done = bf16[3,16,512]{2,1,0:T(8,128)(2,1)S(1)} collective-permute-done((bf16[3,16,512]{2,1,0:T(8,128)(2,1)S(1)}, bf16[3,16,512]{2,1,0:T(8,128)(2,1)S(1)}, u32[]{:S(2)}, u32[]{:S(2)}) %collective-permute-start) | collective-permute-done | bytes 49184 | tf_op jit(solution)/shard_map/ppermute | solution.py:24
  30.0 4.3 %collective-permute-start.2 = (bf16[22,3,512]{2,1,0:T(4,128)(2,1)S(1)}, bf16[22,3,512]{2,1,0:T(4,128)(2,1)S(1)}, u32[]{:S(2)}, u32[]{:S(2)}) collective-permute-start(bf16[22,3,512]{2,1,0:T(4,128)(2,1)S(1)} %get-tuple-element.121), channel_id=1, source_target_pairs={{0,4},{4,8},{8,12},{12,16},{16,20},{20,24},{24,28},{1,5},{5,9},{9,... | collective-permute-start | bytes 202760 | tf_op jit(solution)/shard_map/ppermute | solution.py:24
  34.3 1.5 collective-permute-start.3
  35.7 0.6 fusion.45
  36.4 4.7 %collective-permute-done.3 = bf16[22,3,512]{2,1,0:T(4,128)(2,1)S(1)} collective-permute-done((bf16[22,3,512]{2,1,0:T(4,128)(2,1)S(1)}, bf16[22,3,512]{2,1,0:T(4,128)(2,1)S(1)}, u32[]{:S(2)}, u32[]{:S(2)}) %collective-permute-start.3) | collective-permute-done | bytes 67616 | tf_op jit(solution)/shard_map/ppermute | solution.py:27
  41.0 0.4 fusion.16
  41.6 0.1 maximum_bitcast_fusion.2
  41.7 0.8 copy.48
  42.6 0.3 reshape_reshape.7
  42.9 0.3 fusion.41
  43.2 0.3 copy.56
  43.5 0.3 copy.49
  43.8 0.4 fusion.46
  44.2 0.4 fusion.13
  44.6 2.0 %convolution_bitcast_fusion = f32[4,196,4,64]{1,3,2,0:T(8,128)} fusion(bf16[4,64,4,64]{3,1,2,0:T(8,128)(2,1)S(1)} %bitcast.128, f32[4,4,64,196]{3,2,1,0:T(8,128)S(1)} %get-tuple-element.134, f32[4,4,64]{2,1,0:T(4,128)S(1)} %fusion.13, f32[4,4,64]{2,1,0:T(4,128)S(1)} %get-tuple-element.133), kind=kOutput, calls=%fused_computation.2 | convolution fusion | flops 154542080 | bytes 1744896 | tf_op jit(solution)/shard_map/nhqk,nqhd->nkhd/dot_general | solution.py:114
  46.6 1.3 multiply_reduce_fusion
  47.9 2.0 %copy.62 = f32[4,196,4,64]{3,2,0,1:T(4,128)S(1)} copy(f32[4,196,4,64]{1,3,2,0:T(8,128)} %convolution_bitcast_fusion) | data formatting | bytes 1605632 | tf_op jit(solution)/shard_map/nhqk,nqhd->nkhd/transpose | solution.py:114
  49.9 2.1 %concatenate.74 = f32[2,2,14,14,256]{4,1,0,3,2:T(2,128)} reshape(f32[4,196,4,64]{3,2,0,1:T(4,128)S(1)} %copy.62) | data formatting | bytes 1605632 | tf_op jit(solution)/shard_map/concatenate | solution.py:149
  52.1 2.4 %copy.64 = f32[2,2,14,14,256]{4,3,2,0,1:T(8,128)} copy(f32[2,2,14,14,256]{4,1,0,3,2:T(2,128)} %concatenate.74) | data formatting | bytes 1605632 | tf_op jit(solution)/shard_map/concatenate | solution.py:149
  54.4 1.4 fusion.1
  55.8 1.1 copy.60
  56.9 1.2 concatenate.73
  58.1 0.2 copy.63
  58.3 1.0 copy-done.5
  59.3 0.2 maximum_bitcast_fusion
  59.6 0.2 slice.445
  59.8 0.5 scatter-add.26
  60.4 2.8 %slice_bitcast_fusion.1 = (f32[3,2,14,512]{3,0,2,1:T(4,128)S(1)}, f32[1,3,2,14,512]{4,1,3,2,0:T(4,128)}, f32[3,2,14,512]{3,0,2,1:T(4,128)}) fusion(f32[2,14,2,14,512]{4,1,3,2,0:T(8,128)S(1)} %maximum_bitcast_fusion, f32[2,8,2,14,512]{4,1,3,2,0:T(8,128)S(1)} %scatter-add.26, s32[]{:T(128)} %bitcast.35, s32[]{:T(128)} %bitcast.36, pred[]{:T(512)} %and_reduce_fusion.1), kind=kLoop, calls=%fused_computation.60 | loop fusion | flops 86016 | bytes 1204233 | tf_op jit(solution)/shard_map/squeeze | solution.py:64
  63.2 2.7 %scatter-add.29 = f32[2,8,2,14,512]{4,1,3,2,0:T(8,128)S(1)} dynamic-update-slice(f32[2,8,2,14,512]{4,1,3,2,0:T(8,128)S(1)} %scatter-add.26, f32[1,3,2,14,512]{4,1,3,2,0:T(4,128)} %get-tuple-element.102, s32[]{:T(128)} %bitcast.35, s32[]{:T(128)} %bitcast.36, s32[]{:T(128)} %constant.247.clone.1, s32[]{:T(128)} %constant.247.clone.1, s32[]{:T(128)} %constant.247.clone.1) | dynamic-update-slice | bytes 344068 | tf_op jit(solution)/shard_map/scatter-add | solution.py:61
  65.9 0.3 fusion.37
  66.2 0.3 maximum_bitcast_fusion.1
  66.5 2.8 %collective-permute-start.5 = (bf16[3,22,512]{2,1,0:T(8,128)(2,1)S(1)}, bf16[3,22,512]{2,1,0:T(8,128)(2,1)S(1)}, u32[]{:S(2)}, u32[]{:S(2)}) collective-permute-start(bf16[3,22,512]{2,1,0:T(8,128)(2,1)S(1)} %get-tuple-element.106), channel_id=1, source_target_pairs={{32,0},{64,32},{96,64},{128,96},{160,128},{192,160},{224,192},{256... | collective-permute-start | bytes 202760 | tf_op jit(solution)/shard_map/ppermute | solution.py:16
  69.3 1.9 %collective-permute-start.4 = (bf16[3,22,512]{2,1,0:T(8,128)(2,1)S(1)}, bf16[3,22,512]{2,1,0:T(8,128)(2,1)S(1)}, u32[]{:S(2)}, u32[]{:S(2)}) collective-permute-start(bf16[3,22,512]{2,1,0:T(8,128)(2,1)S(1)} %get-tuple-element.107), channel_id=1, source_target_pairs={{0,32},{32,64},{64,96},{96,128},{128,160},{160,192},{192,224},{224... | collective-permute-start | bytes 202760 | tf_op jit(solution)/shard_map/ppermute | solution.py:16
  71.4 2.0 %fusion.28 = f32[2,8,22,512]{3,2,1,0:T(8,128)S(1)} fusion(f32[2,8,22,512]{3,2,1,0:T(8,128)S(1)} %fusion.31, s32[]{:T(128)} %bitcast.35, s32[]{:T(128)} %bitcast.36, f32[2,14,22,512]{3,2,1,0:T(8,128)S(1)} %maximum_bitcast_fusion.1, pred[]{:T(512)} %and_reduce_fusion), kind=kLoop, calls=%fused_computation.62 | loop fusion | flops 67584 | bytes 442377 | tf_op jit(solution)/shard_map/scatter-add | solution.py:61
  73.3 6.8 %collective-permute-done.4 = bf16[3,22,512]{2,1,0:T(8,128)(2,1)S(1)} collective-permute-done((bf16[3,22,512]{2,1,0:T(8,128)(2,1)S(1)}, bf16[3,22,512]{2,1,0:T(8,128)(2,1)S(1)}, u32[]{:S(2)}, u32[]{:S(2)}) %collective-permute-start.4) | collective-permute-done | bytes 67616 | tf_op jit(solution)/shard_map/ppermute | solution.py:16
  80.4 4.5 %collective-permute-start.6 = (bf16[16,3,512]{2,1,0:T(4,128)(2,1)S(1)}, bf16[16,3,512]{2,1,0:T(4,128)(2,1)S(1)}, u32[]{:S(2)}, u32[]{:S(2)}) collective-permute-start(bf16[16,3,512]{2,1,0:T(4,128)(2,1)S(1)} %get-tuple-element.115), channel_id=1, source_target_pairs={{0,4},{4,8},{8,12},{12,16},{16,20},{20,24},{24,28},{1,5},{5,9},{9,... | collective-permute-start | bytes 147464 | tf_op jit(solution)/shard_map/ppermute | solution.py:16
  84.9 1.0 fusion.10
  86.0 0.2 copy.57
  86.2 0.2 reshape.571
  86.5 1.3 collective-permute-start.7
  87.8 0.4 scatter-add.36
  88.2 6.0 %collective-permute-done.7 = bf16[16,3,512]{2,1,0:T(4,128)(2,1)S(1)} collective-permute-done((bf16[16,3,512]{2,1,0:T(4,128)(2,1)S(1)}, bf16[16,3,512]{2,1,0:T(4,128)(2,1)S(1)}, u32[]{:S(2)}, u32[]{:S(2)}) %collective-permute-start.7) | collective-permute-done | bytes 49184 | tf_op jit(solution)/shard_map/ppermute | solution.py:16
  94.2 0.3 scatter-add.39
  94.7 0.3 copy.66
  95.1 0.9 copy-done.2
  96.0 1.4 convolution_convert_fusion
  97.6 53.6 %all-reduce.4.cloned.1.call-done = bf16[256,1024]{1,0:T(8,128)(2,1)} async-done(((bf16[256,1024]{1,0:T(8,128)(2,1)}), bf16[256,1024]{1,0:T(8,128)(2,1)}) %all-reduce.4.cloned.1.call-update) | async-done | bytes 524304 | tf_op jit(solution)/shard_map/psum | solution.py:222
  151.2 1.0 multiply_reduce_fusion.1
  152.3 1.8 %multiply_add_fusion = f32[64,1024]{1,0:T(8,128)} fusion(f32[256,1024]{1,0:T(8,128)S(1)} %bitcast.106, s32[]{:T(128)S(6)} %select_n.10, f32[64]{0:T(128)S(1)} %broadcast_multiply_fusion, f32[1024]{0:T(1024)S(1)} %copy-done.12, f32[64]{0:T(128)S(1)} %fusion.36, bf16[256,1024]{1,0:T(8,128)(2,1)} %bitcast.122, bf16[256,1024]{1,0:T(8,128)(2,1)} %all-reduce.4.cloned.1.call-done), kind=kLoop, calls=%fused_computation.54 | loop fusion | flops 458752 | bytes 791044 | tf_op jit(solution)/shard_map/add | solution.py:235
  (84 shorter events, 2.7 us)
Async XLA Ops:
  6.5 16.2 %copy-start = (bf16[256,1024]{1,0:T(8,128)(2,1)S(1)}, bf16[256,1024]{1,0:T(8,128)(2,1)}, u32[]{:S(2)}) copy-start(bf16[256,1024]{1,0:T(8,128)(2,1)} %param.24) | copy-start | bytes 1572868
  6.5 144.7 %all-reduce.4.cloned.1.call-start = ((), (), s32[]{:S(2)}) async-start(), calls=%async_computation | async-start | bytes 1048576 | tf_op jit(solution)/shard_map/psum | solution.py:222
  7.8 1.8 %copy-start.9 = (bf16[16,16,1024]{2,1,0:T(8,128)(2,1)S(1)}, bf16[16,16,1024]{2,1,0:T(8,128)(2,1)}, u32[]{:S(2)}) copy-start(bf16[16,16,1024]{2,1,0:T(8,128)(2,1)} %param.21) | copy-start | bytes 1572868
  7.8 1.8 %copy-start.12 = (f32[1024]{0:T(1024)S(1)}, f32[1024]{0:T(1024)}, u32[]{:S(2)}) copy-start(f32[1024]{0:T(1024)} %param.22) | copy-start | bytes 12292
  9.6 2.0 %copy-start.1 = (bf16[1024,3,256]{0,2,1:T(8,128)(2,1)}, bf16[1024,3,256]{0,2,1:T(8,128)(2,1)S(1)}, u32[]{:S(2)}) copy-start(bf16[1024,3,256]{0,2,1:T(8,128)(2,1)S(1)} %copy.40) | copy-start | bytes 4718596
  11.8 11.0 %copy-start.11 = (bf16[16,16,1024]{2,1,0:T(8,128)(2,1)S(1)}, bf16[16,16,1024]{2,1,0:T(8,128)(2,1)}, u32[]{:S(2)}) copy-start(bf16[16,16,1024]{2,1,0:T(8,128)(2,1)} %param.25) | copy-start | bytes 1572868
  11.9 11.3 %copy-start.14 = (s32[5]{0:T(128)S(1)}, s32[5]{0:T(128)}, u32[]{:S(2)}) copy-start(s32[5]{0:T(128)} %constant.268.clone.1) | copy-start | bytes 64
  11.9 12.0 %copy-start.13 = (s32[4]{0:T(128)S(1)}, s32[4]{0:T(128)}, u32[]{:S(2)}) copy-start(s32[4]{0:T(128)} %constant.270.clone.1) | copy-start | bytes 52
  12.1 13.2 %collective-permute-start.1 = (bf16[3,16,512]{2,1,0:T(8,128)(2,1)S(1)}, bf16[3,16,512]{2,1,0:T(8,128)(2,1)S(1)}, u32[]{:S(2)}, u32[]{:S(2)}) collective-permute-start(bf16[3,16,512]{2,1,0:T(8,128)(2,1)S(1)} %bitcast.130), channel_id=1, source_target_pairs={{32,0},{64,32},{96,64},{128,96},{160,128},{192,160},{224,192},{256... | collective-permute-start | bytes 147464 | tf_op jit(solution)/shard_map/ppermute | solution.py:27
  19.7 10.2 %collective-permute-start = (bf16[3,16,512]{2,1,0:T(8,128)(2,1)S(1)}, bf16[3,16,512]{2,1,0:T(8,128)(2,1)S(1)}, u32[]{:S(2)}, u32[]{:S(2)}) collective-permute-start(bf16[3,16,512]{2,1,0:T(8,128)(2,1)S(1)} %bitcast.131), channel_id=1, source_target_pairs={{0,32},{32,64},{64,96},{96,128},{128,160},{160,192},{192,224},{224... | collective-permute-start | bytes 147464 | tf_op jit(solution)/shard_map/ppermute | solution.py:24
  30.0 6.4 %collective-permute-start.2 = (bf16[22,3,512]{2,1,0:T(4,128)(2,1)S(1)}, bf16[22,3,512]{2,1,0:T(4,128)(2,1)S(1)}, u32[]{:S(2)}, u32[]{:S(2)}) collective-permute-start(bf16[22,3,512]{2,1,0:T(4,128)(2,1)S(1)} %get-tuple-element.121), channel_id=1, source_target_pairs={{0,4},{4,8},{8,12},{12,16},{16,20},{20,24},{24,28},{1,5},{5,9},{9,... | collective-permute-start | bytes 202760 | tf_op jit(solution)/shard_map/ppermute | solution.py:24
  34.3 6.8 %collective-permute-start.3 = (bf16[22,3,512]{2,1,0:T(4,128)(2,1)S(1)}, bf16[22,3,512]{2,1,0:T(4,128)(2,1)S(1)}, u32[]{:S(2)}, u32[]{:S(2)}) collective-permute-start(bf16[22,3,512]{2,1,0:T(4,128)(2,1)S(1)} %get-tuple-element.122), channel_id=1, source_target_pairs={{4,0},{8,4},{12,8},{16,12},{20,16},{24,20},{28,24},{5,1},{9,5},{13... | collective-permute-start | bytes 202760 | tf_op jit(solution)/shard_map/ppermute | solution.py:27
  43.8 0.8 copy-start.7
  44.2 10.3 %copy-start.3 = (f32[4,4,64,196]{3,2,1,0:T(8,128)}, f32[4,4,64,196]{3,2,1,0:T(8,128)S(1)}, u32[]{:S(2)}) copy-start(f32[4,4,64,196]{3,2,1,0:T(8,128)S(1)} %get-tuple-element.134) | copy-start | bytes 2408452
  52.1 2.4 %copy-start.15 = (f32[4,4,64,196]{3,2,1,0:T(8,128)S(1)}, f32[4,4,64,196]{3,2,1,0:T(8,128)}, u32[]{:S(2)}) copy-start(f32[4,4,64,196]{3,2,1,0:T(8,128)} %get-tuple-element.136) | copy-start | bytes 2408452
  58.1 1.2 copy-start.5
  63.2 2.8 %copy-start.10 = (f32[3,2,14,512]{3,0,2,1:T(4,128)S(1)}, f32[3,2,14,512]{3,0,2,1:T(4,128)}, u32[]{:S(2)}) copy-start(f32[3,2,14,512]{3,0,2,1:T(4,128)} %get-tuple-element.103) | copy-start | bytes 516100
  66.5 13.7 %collective-permute-start.5 = (bf16[3,22,512]{2,1,0:T(8,128)(2,1)S(1)}, bf16[3,22,512]{2,1,0:T(8,128)(2,1)S(1)}, u32[]{:S(2)}, u32[]{:S(2)}) collective-permute-start(bf16[3,22,512]{2,1,0:T(8,128)(2,1)S(1)} %get-tuple-element.106), channel_id=1, source_target_pairs={{32,0},{64,32},{96,64},{128,96},{160,128},{192,160},{224,192},{256... | collective-permute-start | bytes 202760 | tf_op jit(solution)/shard_map/ppermute | solution.py:16
  69.3 10.8 %collective-permute-start.4 = (bf16[3,22,512]{2,1,0:T(8,128)(2,1)S(1)}, bf16[3,22,512]{2,1,0:T(8,128)(2,1)S(1)}, u32[]{:S(2)}, u32[]{:S(2)}) collective-permute-start(bf16[3,22,512]{2,1,0:T(8,128)(2,1)S(1)} %get-tuple-element.107), channel_id=1, source_target_pairs={{0,32},{32,64},{64,96},{96,128},{128,160},{160,192},{192,224},{224... | collective-permute-start | bytes 202760 | tf_op jit(solution)/shard_map/ppermute | solution.py:16
  71.3 13.6 %copy-start.4 = (f32[4,4,64,196]{3,2,1,0:T(8,128)S(1)}, f32[4,4,64,196]{3,2,1,0:T(8,128)}, u32[]{:S(2)}) copy-start(f32[4,4,64,196]{3,2,1,0:T(8,128)} %copy-done.3) | copy-start | bytes 2408452
  71.3 13.6 %copy-start.8 = (bf16[4,196,256]{1,2,0:T(8,128)(2,1)S(1)}, bf16[4,196,256]{1,2,0:T(8,128)(2,1)}, u32[]{:S(2)}) copy-start(bf16[4,196,256]{1,2,0:T(8,128)(2,1)} %copy-done.7) | copy-start | bytes 1204228
  71.3 13.6 %copy-start.16 = (f32[4,4,64,196]{3,2,1,0:T(8,128)S(1)}, f32[4,4,64,196]{3,2,1,0:T(8,128)}, u32[]{:S(2)}) copy-start(f32[4,4,64,196]{3,2,1,0:T(8,128)} %get-tuple-element.136) | copy-start | bytes 2408452
  80.4 7.4 %collective-permute-start.6 = (bf16[16,3,512]{2,1,0:T(4,128)(2,1)S(1)}, bf16[16,3,512]{2,1,0:T(4,128)(2,1)S(1)}, u32[]{:S(2)}, u32[]{:S(2)}) collective-permute-start(bf16[16,3,512]{2,1,0:T(4,128)(2,1)S(1)} %get-tuple-element.115), channel_id=1, source_target_pairs={{0,4},{4,8},{8,12},{12,16},{16,20},{20,24},{24,28},{1,5},{5,9},{9,... | collective-permute-start | bytes 147464 | tf_op jit(solution)/shard_map/ppermute | solution.py:16
  86.5 7.7 %collective-permute-start.7 = (bf16[16,3,512]{2,1,0:T(4,128)(2,1)S(1)}, bf16[16,3,512]{2,1,0:T(4,128)(2,1)S(1)}, u32[]{:S(2)}, u32[]{:S(2)}) collective-permute-start(bf16[16,3,512]{2,1,0:T(4,128)(2,1)S(1)} %get-tuple-element.114), channel_id=1, source_target_pairs={{4,0},{8,4},{12,8},{16,12},{20,16},{24,20},{28,24},{5,1},{9,5},{13... | collective-permute-start | bytes 147464 | tf_op jit(solution)/shard_map/ppermute | solution.py:16
  94.6 1.4 copy-start.2
  96.0 55.2 %copy-start.6 = (f32[16,16,1024]{2,1,0:T(8,128)S(1)}, f32[16,16,1024]{2,1,0:T(8,128)}, u32[]{:S(2)}) copy-start(f32[16,16,1024]{2,1,0:T(8,128)} %get-tuple-element.113) | copy-start | bytes 3145732
Sparse Core Ops, SparseCore 0:
  97.5 53.6 all-reduce.3
where the time goes:
time: 162 us; the launch traced here: 161 us
  waiting for transfers between devices  75.6 us (47%)
  starting transfers between devices  25.7 us (16%)
  local copies, waits for them, and re-layouts  22.6 us (14%)
  other arithmetic  14.5 us (9%)
  between operations  14.2 us (9%)
  matrix products  8.37 us (5%)
    psum x1, waiting for transfers between devices, per_device(): lax.psum(full_term.astype(jnp.bfloat16), 'tp').astype(jnp.float32)  53.6 us
    ppermute x4, waiting for transfers between devices, passed_along(): return lax.ppermute(block, axis, route)  12.8 us
    ppermute x4, starting transfers between devices, passed_along(): return lax.ppermute(block, axis, route)  10.6 us
    ppermute x2, starting transfers between devices, extended_2(): lax.ppermute(lax.slice_in_dim(block, 0, width, axis=dim), axis, backward)  8.91 us
    ppermute x2, starting transfers between devices, extended_2(): lax.ppermute(lax.slice_in_dim(block, block.shape[dim] - width, None, axis...  6.2 us
    concatenate x4, local copies, waits for them, and re-layouts, attend(): jnp.concatenate([key_grad.reshape(block_count, region_cells, head_cols),...  5.89 us
    ppermute x2, waiting for transfers between devices, extended_2(): lax.ppermute(lax.slice_in_dim(block, 0, width, axis=dim), axis, backward)  4.67 us
    ppermute x2, waiting for transfers between devices, extended_2(): lax.ppermute(lax.slice_in_dim(block, block.shape[dim] - width, None, axis...  4.54 us
  transfers between devices with their start and end apart: 9, of which 5 were waited for; matrix products, arithmetic and copies ran while one was open for 5% of the time, Pallas kernels for 0%

commit v1 on v0

v1 whole, which is shorter than its diff:
```python
import jax
import jax.numpy as jnp
import numpy as np
from jax import lax
from jax.experimental import pallas as pl
from jax.experimental.pallas import tpu as pltpu
from jax.sharding import PartitionSpec as P

HEAD_DIM = 64
RADIUS = 3
REACH = 2 * RADIUS
SIDE = 16
WIDE = SIDE + 2 * REACH
TALL = SIDE + 2 * RADIUS
KV_ROWS = REACH * SIDE
QG_ROWS = RADIUS * SIDE
KV_EDGE = 176
QG_EDGE = 80
KEYS = WIDE * SIDE + 2 * KV_EDGE
QUERIES = TALL * SIDE + 2 * QG_EDGE
FAR = 1000.0
bf16 = jnp.bfloat16
f32 = jnp.float32
VMEM = pl.BlockSpec(memory_space=pltpu.VMEM)
SMEM = pl.BlockSpec(memory_space=pltpu.SMEM)
PARAMS = pltpu.CompilerParams(vmem_limit_bytes=56 * 1024 * 1024)


def nt(a, b):
    return lax.dot_general(a, b, (((1,), (1,)), ((), ())), preferred_element_type=f32)


def nn(a, b):
    return jnp.dot(a, b, preferred_element_type=f32)


def edge_picks():
    def pick(out_rows, in_rows, count, lines, first):
        table = np.zeros((out_rows, in_rows), np.float32)
        for line in range(lines):
            for step in range(count):
                table[line * count + step, line * SIDE + first + step] = 1.0
        return table

    kv_low = pick(KV_EDGE, WIDE * SIDE, REACH, WIDE, 0)
    kv_high = pick(KV_EDGE, WIDE * SIDE, REACH, WIDE, SIDE - REACH)
    qg_low = pick(QG_EDGE, TALL * SIDE, RADIUS, TALL, 0)
    qg_high = pick(QG_EDGE, TALL * SIDE, RADIUS, TALL, SIDE - RADIUS)
    return [jnp.asarray(t, bf16) for t in (kv_low, kv_high, qg_low, qg_high)]


def places():
    def coords(lines, reach, edge_rows):
        ys, xs = [], []
        for line in range(lines):
            for x in range(SIDE):
                ys.append(line - reach)
                xs.append(x)
        for first in (-reach, SIDE):
            begin = len(ys)
            for line in range(lines):
                for step in range(reach):
                    ys.append(line - reach)
                    xs.append(first + step)
            while len(ys) < begin + edge_rows:
                ys.append(FAR)
                xs.append(FAR)
        return np.asarray(ys, np.float32), np.asarray(xs, np.float32)

    key_y, key_x = coords(WIDE, REACH, KV_EDGE)
    query_y, query_x = coords(TALL, RADIUS, QG_EDGE)
    keys = np.stack([key_y, key_x], axis=1)
    queries = np.stack([query_y, query_x], axis=0)
    queries = np.where(queries == FAR, -FAR, queries)
    return jnp.asarray(keys), jnp.asarray(queries)


def project_kernel(latent, gain, weight, out_weight, cotangent, kv, qg, upper, lower):
    tokens = latent[...].astype(f32)
    inverse = lax.rsqrt(jnp.mean(tokens * tokens, axis=-1, keepdims=True) + 1e-06)
    normed = (tokens * inverse * gain[...]).astype(bf16)
    width = out_weight.shape[0]
    grad_out = nt(cotangent[...], out_weight[...]).astype(bf16)
    query = nn(normed, weight[0]).astype(bf16)
    qg[:, :width] = query * jnp.asarray(HEAD_DIM ** (-0.5), bf16)
    kv[:, :width] = nn(normed, weight[1]).astype(bf16)
    kv[:, width:] = nn(normed, weight[2]).astype(bf16)
    qg[:, width:] = grad_out
    count = latent.shape[0]
    upper[:KV_ROWS] = kv[:KV_ROWS]
    upper[KV_ROWS:] = qg[:QG_ROWS]
    lower[:KV_ROWS] = kv[count - KV_ROWS :]
    lower[KV_ROWS:] = qg[count - QG_ROWS :]


def edges_kernel(kv, qg, above, below, kv_low, kv_high, qg_low, qg_high, left, right):
    kv_all = jnp.concatenate([above[:KV_ROWS], kv[...], below[:KV_ROWS]], axis=0)
    qg_all = jnp.concatenate([above[KV_ROWS:], qg[...], below[KV_ROWS:]], axis=0)
    left[:KV_EDGE] = nn(kv_low[...], kv_all).astype(bf16)
    left[KV_EDGE:] = nn(qg_low[...], qg_all).astype(bf16)
    right[:KV_EDGE] = nn(kv_high[...], kv_all).astype(bf16)
    right[KV_EDGE:] = nn(qg_high[...], qg_all).astype(bf16)


def attend_kernel(
    limits, kv, qg, above, below, from_left, from_right, keys, queries, weight, partial, bias
):
    width = kv.shape[1] // 2
    count = kv.shape[0]
    key_y, key_x = keys[:, 0:1], keys[:, 1:2]
    query_y, query_x = queries[0:1, :], queries[1:2, :]
    top, bottom = limits[0].astype(f32), limits[1].astype(f32)
    left, right = limits[2].astype(f32), limits[3].astype(f32)
    inside = (key_y >= top) & (key_y <= bottom) & (key_x >= left) & (key_x <= right)
    key_y = jnp.where(inside, key_y, FAR)
    near = (jnp.abs(key_y - query_y) <= RADIUS) & (jnp.abs(key_x - query_x) <= RADIUS)
    bias[...] = jnp.where(near, 0.0, -1e30)

    kv_all = jnp.concatenate(
        [above[:KV_ROWS], kv[...], below[:KV_ROWS], from_left[:KV_EDGE], from_right[:KV_EDGE]],
        axis=0,
    )
    qg_all = jnp.concatenate(
        [above[KV_ROWS:], qg[...], below[KV_ROWS:], from_left[KV_EDGE:], from_right[KV_EDGE:]],
        axis=0,
    )
    key, value = kv_all[:, :width], kv_all[:, width:]
    query, upstream = qg_all[:, :width], qg_all[:, width:]
    key_t = key.astype(f32).T.astype(bf16)
    lanes = lax.broadcasted_iota(jnp.int32, (1, width), 1) // HEAD_DIM
    own = slice(KV_ROWS, KV_ROWS + count)
    key_grad = jnp.zeros((count, width), f32)
    value_grad = jnp.zeros((count, width), f32)
    query_parts = []
    for head in range(width // HEAD_DIM):
        mine = lanes == head
        query_h = jnp.where(mine, query, jnp.zeros_like(query))
        upstream_h = jnp.where(mine, upstream, jnp.zeros_like(upstream))
        scores = nt(key, query_h) + bias[...]
        dots = nt(value, upstream_h)
        exponent = jnp.exp(scores - jnp.max(scores, axis=0, keepdims=True))
        scale = 1.0 / jnp.sum(exponent, axis=0, keepdims=True)
        weights = exponent * scale
        centre = jnp.sum(weights * dots, axis=0, keepdims=True)
        score_grads = (weights * (dots - centre)).astype(bf16)
        value_grad += nn(weights[own].astype(bf16), upstream_h)
        key_grad += nn(score_grads[own], query_h)
        query_parts.append(nn(key_t[head * HEAD_DIM : (head + 1) * HEAD_DIM], score_grads))
    query_grad = jnp.concatenate(query_parts, axis=0).T[QG_ROWS : QG_ROWS + count]
    query_grad = query_grad * (HEAD_DIM ** (-0.5))
    total = nt(query_grad.astype(bf16), weight[0])
    total += nt(key_grad.astype(bf16), weight[1])
    total += nt(value_grad.astype(bf16), weight[2])
    partial[...] = total.astype(bf16)


def finish_kernel(place, received, latent, gain, cotangent, result):
    count = received.shape[1]
    first = pl.multiple_of(place[0] * count, count)
    tokens = latent[pl.ds(first, count), :].astype(f32)
    upstream = cotangent[pl.ds(first, count), :].astype(f32)
    summed = received[0].astype(f32)
    for part in range(1, received.shape[0]):
        summed += received[part].astype(f32)
    inverse = lax.rsqrt(jnp.mean(tokens * tokens, axis=-1, keepdims=True) + 1e-06)
    unit = tokens * inverse
    scaled = summed * gain[...]
    stat = jnp.mean(scaled * unit, axis=-1, keepdims=True)
    result[...] = upstream + inverse * (scaled - unit * stat)


def moved(block, axis, distance):
    count = lax.axis_size(axis)
    route = [(i, i + distance) for i in range(count) if 0 <= i + distance < count]
    return lax.ppermute(block, axis, route)


def per_device(latent, norm_gain, qkv_weight, out_weight, cotangent):
    tile_rows, tile_cols, model_width = latent.shape
    head_cols = out_weight.shape[0]
    count = tile_rows * tile_cols
    tp = lax.axis_size("tp")
    flat_latent = latent.reshape(count, model_width)
    flat_cotangent = cotangent.reshape(count, model_width)
    gain = norm_gain.reshape(1, model_width)
    weight = qkv_weight.transpose(1, 0, 2)
    shape = jax.ShapeDtypeStruct
    edge = shape((KV_ROWS + QG_ROWS, 2 * head_cols), bf16)
    kv, qg, upper, lower = pl.pallas_call(
        project_kernel,
        out_shape=[shape((count, 2 * head_cols), bf16)] * 2 + [edge] * 2,
        in_specs=[VMEM] * 5,
        out_specs=[VMEM] * 4,
        compiler_params=PARAMS,
        name="project",
    )(flat_latent, gain, weight, out_weight, flat_cotangent)
    above = moved(lower, "row", 1)
    below = moved(upper, "row", -1)
    side = shape((KV_EDGE + QG_EDGE, 2 * head_cols), bf16)
    leftward, rightward = pl.pallas_call(
        edges_kernel,
        out_shape=[side] * 2,
        in_specs=[VMEM] * 8,
        out_specs=[VMEM] * 2,
        compiler_params=PARAMS,
        name="edges",
    )(kv, qg, above, below, *edge_picks())
    from_left = moved(rightward, "col", 1)
    from_right = moved(leftward, "col", -1)
    row, col = lax.axis_index("row"), lax.axis_index("col")
    limits = jnp.stack(
        [
            -row * tile_rows,
            (lax.axis_size("row") - row) * tile_rows - 1,
            -col * tile_cols,
            (lax.axis_size("col") - col) * tile_cols - 1,
        ]
    ).astype(jnp.int32)
    partial = pl.pallas_call(
        attend_kernel,
        out_shape=shape((count, model_width), bf16),
        in_specs=[SMEM] + [VMEM] * 9,
        out_specs=VMEM,
        scratch_shapes=[pltpu.VMEM((KEYS, QUERIES), f32)],
        compiler_params=PARAMS,
        name="attend",
    )(limits, kv, qg, above, below, from_left, from_right, *places(), weight)
    own = count // tp
    received = lax.all_to_all(partial.reshape(tp, own, model_width), "tp", 0, 0)
    place = lax.axis_index("tp").astype(jnp.int32).reshape(1)
    result = pl.pallas_call(
        finish_kernel,
        out_shape=shape((own, model_width), f32),
        in_specs=[SMEM] + [VMEM] * 4,
        out_specs=VMEM,
        compiler_params=PARAMS,
        name="finish",
    )(place, received, flat_latent, gain, flat_cotangent)
    return result.reshape(own // tile_cols, tile_cols, model_width)


def solution(mesh):
    placed = (P("row", "col", None), P(), P(None, None, "tp"), P("tp", None), P("row", "col", None))
    return jax.shard_map(
        per_device,
        mesh=mesh,
        in_specs=placed,
        out_specs=P(("row", "tp"), "col", None),
        check_vma=False,
    )
```

time: 162 us -> 71.2 us (0.44)
  the two profiles are of different devices: /device:TPU:6 before, /device:TPU:194 now
where the time goes in v1:
time: 71.2 us; the launch traced here: 70.9 us
  waiting for transfers between devices  25.5 us (36%)
  starting transfers between devices  25.1 us (35%)
  Pallas kernels  17.4 us (24%)
  local copies, waits for them, and re-layouts  2.19 us (3%)
    ppermute x4, starting transfers between devices, moved(): return lax.ppermute(block, axis, route)  17.8 us
    all_to_all x1, waiting for transfers between devices, per_device(): received = lax.all_to_all(partial.reshape(tp, own, model_width), 'tp', 0, 0)  14.9 us
    ppermute x4, waiting for transfers between devices, moved(): return lax.ppermute(block, axis, route)  10.5 us
    pallas_call x1, Pallas kernels, per_device(): pl.pallas_call(attend_kernel, out_shape=shape((count, model_width), bf16)...  9.25 us
    all_to_all x1, starting transfers between devices, per_device(): received = lax.all_to_all(partial.reshape(tp, own, model_width), 'tp', 0, 0)  7.36 us
    pallas_call x1, Pallas kernels, per_device(): pl.pallas_call(project_kernel, out_shape=[shape((count, 2 * head_cols), b...  3.42 us
    pallas_call x1, Pallas kernels, per_device(): pl.pallas_call(edges_kernel, out_shape=[side] * 2, in_specs=[VMEM] * 8, o...  2.47 us
    pallas_call x1, Pallas kernels, per_device(): pl.pallas_call(finish_kernel, out_shape=shape((own, model_width), f32), i...  2.3 us
  transfers between devices with their start and end apart: 5, of which 5 were waited for; matrix products, arithmetic and copies ran while one was open for 1% of the time, Pallas kernels for 0%

profile of v1, /device:TPU:194, one launch (start us, length us, event | category | flops | bytes accessed | tf_op | source)
XLA Modules:
  0.0 70.9 jit_solution(3254573152183881729)
XLA Ops:
  0.0 3.4 %project.1 = (bf16[256,512]{1,0:T(8,128)(2,1)}, bf16[256,512]{1,0:T(8,128)(2,1)}, bf16[144,512]{1,0:T(8,128)(2,1)}, bf16[144,512]{1,0:T(8,128)(2,1)}) custom-call(bf16[256,1024]{1,0:T(8,128)(2,1)} %bitcast.14, f32[1,1024]{1,0:T(1,128)} %bitcast.18, bf16[3,1024,256]{2,1,0:T(8,128)(2,1)} %bitcast.11, bf16[256,1024]{1,0:T(8,128)(2,1)} %out_weight.1, ...), custom_call_target="tpu_custom_call" | custom-call | tf_op jit(solution)/shard_map/project/pallas_call | solution.py:189
  3.4 1.9 %collective-permute-start = (bf16[144,512]{1,0:T(8,128)(2,1)}, bf16[144,512]{1,0:T(8,128)(2,1)S(1)}, u32[]{:S(2)}, u32[]{:S(2)}) collective-permute-start(bf16[144,512]{1,0:T(8,128)(2,1)} %get-tuple-element.13), channel_id=1, source_target_pairs={{0,32},{32,64},{64,96},{96,128},{128,160},{160,192},{192,224},{224... | collective-permute-start | bytes 442376 | tf_op jit(solution)/shard_map/ppermute | solution.py:175
  5.3 8.4 %collective-permute-start.1 = (bf16[144,512]{1,0:T(8,128)(2,1)}, bf16[144,512]{1,0:T(8,128)(2,1)S(1)}, u32[]{:S(2)}, u32[]{:S(2)}) collective-permute-start(bf16[144,512]{1,0:T(8,128)(2,1)} %get-tuple-element.14), channel_id=1, source_target_pairs={{32,0},{64,32},{96,64},{128,96},{160,128},{192,160},{224,192},{256... | collective-permute-start | bytes 442376 | tf_op jit(solution)/shard_map/ppermute | solution.py:175
  13.8 1.2 %collective-permute-done.above = bf16[144,512]{1,0:T(8,128)(2,1)S(1)} collective-permute-done((bf16[144,512]{1,0:T(8,128)(2,1)}, bf16[144,512]{1,0:T(8,128)(2,1)S(1)}, u32[]{:S(2)}, u32[]{:S(2)}) %collective-permute-start) | collective-permute-done | bytes 147488 | tf_op jit(solution)/shard_map/ppermute | solution.py:175
  15.0 0.0 copy-start.1
  15.0 2.2 %collective-permute-done.1.below = bf16[144,512]{1,0:T(8,128)(2,1)S(1)} collective-permute-done((bf16[144,512]{1,0:T(8,128)(2,1)}, bf16[144,512]{1,0:T(8,128)(2,1)S(1)}, u32[]{:S(2)}, u32[]{:S(2)}) %collective-permute-start.1) | collective-permute-done | bytes 147488 | tf_op jit(solution)/shard_map/ppermute | solution.py:175
  17.2 0.0 copy-start.2
  17.2 0.0 copy-done.1
  17.2 0.7 copy-done.2
  17.8 2.5 %edges.1 = (bf16[256,512]{1,0:T(8,128)(2,1)}, bf16[256,512]{1,0:T(8,128)(2,1)}) custom-call(bf16[256,512]{1,0:T(8,128)(2,1)} %get-tuple-element.11.kv, bf16[256,512]{1,0:T(8,128)(2,1)} %get-tuple-element.12.qg, bf16[144,512]{1,0:T(8,128)(2,1)} %copy-done.1, bf16[144,512]{1,0:T(8,128)(2,1)} %copy-done.2, bf16[176,448]{1,0:T(8,128)(2,1)} %constant.35.clone.kv_low, ...), custom_call_target="tpu_custom_call" | custom-call | tf_op jit(solution)/shard_map/edges/pallas_call | solution.py:200
  20.3 5.5 %collective-permute-start.2 = (bf16[256,512]{1,0:T(8,128)(2,1)}, bf16[256,512]{1,0:T(8,128)(2,1)S(1)}, u32[]{:S(2)}, u32[]{:S(2)}) collective-permute-start(bf16[256,512]{1,0:T(8,128)(2,1)} %get-tuple-element.15), channel_id=1, source_target_pairs={{0,4},{4,8},{8,12},{12,16},{16,20},{20,24},{24,28},{1,5},{5,9},{9,... | collective-permute-start | bytes 786440 | tf_op jit(solution)/shard_map/ppermute | solution.py:175
  25.8 1.9 %collective-permute-start.3 = (bf16[256,512]{1,0:T(8,128)(2,1)}, bf16[256,512]{1,0:T(8,128)(2,1)S(1)}, u32[]{:S(2)}, u32[]{:S(2)}) collective-permute-start(bf16[256,512]{1,0:T(8,128)(2,1)} %get-tuple-element.16), channel_id=1, source_target_pairs={{4,0},{8,4},{12,8},{16,12},{20,16},{24,20},{28,24},{5,1},{9,5},{13... | collective-permute-start | bytes 786440 | tf_op jit(solution)/shard_map/ppermute | solution.py:175
  27.7 0.6 pad_add_fusion.limits
  28.3 1.7 %collective-permute-done.2.from_left = bf16[256,512]{1,0:T(8,128)(2,1)S(1)} collective-permute-done((bf16[256,512]{1,0:T(8,128)(2,1)}, bf16[256,512]{1,0:T(8,128)(2,1)S(1)}, u32[]{:S(2)}, u32[]{:S(2)}) %collective-permute-start.2) | collective-permute-done | bytes 262176 | tf_op jit(solution)/shard_map/ppermute | solution.py:175
  30.0 0.0 copy-start.3
  30.0 5.5 %collective-permute-done.3.from_right = bf16[256,512]{1,0:T(8,128)(2,1)S(1)} collective-permute-done((bf16[256,512]{1,0:T(8,128)(2,1)}, bf16[256,512]{1,0:T(8,128)(2,1)S(1)}, u32[]{:S(2)}, u32[]{:S(2)}) %collective-permute-start.3) | collective-permute-done | bytes 262176 | tf_op jit(solution)/shard_map/ppermute | solution.py:175
  35.5 0.0 copy-done.3
  35.5 0.0 copy-start.4
  35.5 0.7 %copy-done.4 = bf16[256,512]{1,0:T(8,128)(2,1)} copy-done((bf16[256,512]{1,0:T(8,128)(2,1)}, bf16[256,512]{1,0:T(8,128)(2,1)S(1)}, u32[]{:S(2)}) %copy-start.4) | copy-done | bytes 262168
  36.2 9.2 %attend.1 = bf16[256,1024]{1,0:T(8,128)(2,1)} custom-call(s32[4]{0:T(128)} %pad_add_fusion.limits, bf16[256,512]{1,0:T(8,128)(2,1)} %get-tuple-element.11.kv, bf16[256,512]{1,0:T(8,128)(2,1)} %get-tuple-element.12.qg, bf16[144,512]{1,0:T(8,128)(2,1)} %copy-done.1, bf16[144,512]{1,0:T(8,128)(2,1)} %copy-done.2, bf16[256,512]{1,0:T(8,128)(2,1)} %copy-done.3, ...), custom_call_target="tpu_custom_call" | custom-call | tf_op jit(solution)/shard_map/attend/pallas_call | solution.py:219
  45.4 7.4 %all-to-all-start = ((bf16[4,64,1024]{2,1,0:T(8,128)(2,1)}), bf16[4,64,1024]{2,1,0:T(8,128)(2,1)S(1)}, u32[]{:S(2)}, u32[]{:S(2)}) async-start(bf16[4,64,1024]{2,1,0:T(8,128)(2,1)} %bitcast.13), calls=%async_computation | async-start | bytes 1048576 | tf_op jit(solution)/shard_map/all_to_all | solution.py:229
  52.8 14.9 %all-to-all-done.received = bf16[4,64,1024]{2,1,0:T(8,128)(2,1)S(1)} async-done(((bf16[4,64,1024]{2,1,0:T(8,128)(2,1)}), bf16[4,64,1024]{2,1,0:T(8,128)(2,1)S(1)}, u32[]{:S(2)}, u32[]{:S(2)}) %all-to-all-start) | async-done | bytes 524320 | tf_op jit(solution)/shard_map/all_to_all | solution.py:229
  67.8 0.0 copy-start
  67.8 0.8 %copy-done = bf16[4,64,1024]{2,1,0:T(8,128)(2,1)} copy-done((bf16[4,64,1024]{2,1,0:T(8,128)(2,1)}, bf16[4,64,1024]{2,1,0:T(8,128)(2,1)S(1)}, u32[]{:S(2)}) %copy-start) | copy-done | bytes 524312
  68.6 2.3 %finish.1 = f32[64,1024]{1,0:T(8,128)} custom-call(s32[1]{0:T(128)} %bitcast.place, bf16[4,64,1024]{2,1,0:T(8,128)(2,1)} %copy-done, bf16[256,1024]{1,0:T(8,128)(2,1)} %bitcast.15, f32[1,1024]{1,0:T(1,128)} %bitcast.19, bf16[256,1024]{1,0:T(8,128)(2,1)} %bitcast.17), custom_call_target="tpu_custom_call" | custom-call | tf_op jit(solution)/shard_map/finish/pallas_call | solution.py:231
Async XLA Ops:
  3.4 11.6 %collective-permute-start = (bf16[144,512]{1,0:T(8,128)(2,1)}, bf16[144,512]{1,0:T(8,128)(2,1)S(1)}, u32[]{:S(2)}, u32[]{:S(2)}) collective-permute-start(bf16[144,512]{1,0:T(8,128)(2,1)} %get-tuple-element.13), channel_id=1, source_target_pairs={{0,32},{32,64},{64,96},{96,128},{128,160},{160,192},{192,224},{224... | collective-permute-start | bytes 442376 | tf_op jit(solution)/shard_map/ppermute | solution.py:175
  5.3 11.8 %collective-permute-start.1 = (bf16[144,512]{1,0:T(8,128)(2,1)}, bf16[144,512]{1,0:T(8,128)(2,1)S(1)}, u32[]{:S(2)}, u32[]{:S(2)}) collective-permute-start(bf16[144,512]{1,0:T(8,128)(2,1)} %get-tuple-element.14), channel_id=1, source_target_pairs={{32,0},{64,32},{96,64},{128,96},{160,128},{192,160},{224,192},{256... | collective-permute-start | bytes 442376 | tf_op jit(solution)/shard_map/ppermute | solution.py:175
  15.0 2.2 %copy-start.1 = (bf16[144,512]{1,0:T(8,128)(2,1)}, bf16[144,512]{1,0:T(8,128)(2,1)S(1)}, u32[]{:S(2)}) copy-start(bf16[144,512]{1,0:T(8,128)(2,1)S(1)} %collective-permute-done.above) | copy-start | bytes 442372
  17.2 0.7 copy-start.2
  20.3 9.7 %collective-permute-start.2 = (bf16[256,512]{1,0:T(8,128)(2,1)}, bf16[256,512]{1,0:T(8,128)(2,1)S(1)}, u32[]{:S(2)}, u32[]{:S(2)}) collective-permute-start(bf16[256,512]{1,0:T(8,128)(2,1)} %get-tuple-element.15), channel_id=1, source_target_pairs={{0,4},{4,8},{8,12},{12,16},{16,20},{20,24},{24,28},{1,5},{5,9},{9,... | collective-permute-start | bytes 786440 | tf_op jit(solution)/shard_map/ppermute | solution.py:175
  25.8 9.7 %collective-permute-start.3 = (bf16[256,512]{1,0:T(8,128)(2,1)}, bf16[256,512]{1,0:T(8,128)(2,1)S(1)}, u32[]{:S(2)}, u32[]{:S(2)}) collective-permute-start(bf16[256,512]{1,0:T(8,128)(2,1)} %get-tuple-element.16), channel_id=1, source_target_pairs={{4,0},{8,4},{12,8},{16,12},{20,16},{24,20},{28,24},{5,1},{9,5},{13... | collective-permute-start | bytes 786440 | tf_op jit(solution)/shard_map/ppermute | solution.py:175
  30.0 5.5 %copy-start.3 = (bf16[256,512]{1,0:T(8,128)(2,1)}, bf16[256,512]{1,0:T(8,128)(2,1)S(1)}, u32[]{:S(2)}) copy-start(bf16[256,512]{1,0:T(8,128)(2,1)S(1)} %collective-permute-done.2.from_left) | copy-start | bytes 786436
  35.5 0.7 %copy-start.4 = (bf16[256,512]{1,0:T(8,128)(2,1)}, bf16[256,512]{1,0:T(8,128)(2,1)S(1)}, u32[]{:S(2)}) copy-start(bf16[256,512]{1,0:T(8,128)(2,1)S(1)} %collective-permute-done.3.from_right) | copy-start | bytes 786436
  45.4 22.3 %all-to-all-start = ((bf16[4,64,1024]{2,1,0:T(8,128)(2,1)}), bf16[4,64,1024]{2,1,0:T(8,128)(2,1)S(1)}, u32[]{:S(2)}, u32[]{:S(2)}) async-start(bf16[4,64,1024]{2,1,0:T(8,128)(2,1)} %bitcast.13), calls=%async_computation | async-start | bytes 1048576 | tf_op jit(solution)/shard_map/all_to_all | solution.py:229
  67.8 0.8 %copy-start = (bf16[4,64,1024]{2,1,0:T(8,128)(2,1)}, bf16[4,64,1024]{2,1,0:T(8,128)(2,1)S(1)}, u32[]{:S(2)}) copy-start(bf16[4,64,1024]{2,1,0:T(8,128)(2,1)S(1)} %all-to-all-done.received) | copy-start | bytes 1572868

commit v2 on v1

v2 whole, which is shorter than its diff:
```python
import jax
import jax.numpy as jnp
import numpy as np
from jax import lax
from jax.experimental import pallas as pl
from jax.experimental.pallas import tpu as pltpu
from jax.sharding import PartitionSpec as P

HEAD_DIM = 64
RADIUS = 3
REACH = 2 * RADIUS
SIDE = 16
WIDE = SIDE + 2 * REACH
TALL = SIDE + 2 * RADIUS
KV_ROWS = REACH * SIDE
QG_ROWS = RADIUS * SIDE
KV_EDGE = 176
QG_EDGE = 80
MIDDLE = SIDE - 2 * RADIUS
MID_QUERIES = 224
OWN_FROM = 32
OWN_EDGE = 112
FAR = 1000.0
bf16 = jnp.bfloat16
f32 = jnp.float32
VMEM = pl.BlockSpec(memory_space=pltpu.VMEM)
SMEM = pl.BlockSpec(memory_space=pltpu.SMEM)
PARAMS = pltpu.CompilerParams(vmem_limit_bytes=56 * 1024 * 1024)


def nt(a, b):
    return lax.dot_general(a, b, (((1,), (1,)), ((), ())), preferred_element_type=f32)


def nn(a, b):
    return jnp.dot(a, b, preferred_element_type=f32)


def table(out_rows, in_rows, pairs):
    filled = np.zeros((out_rows, in_rows), np.float32)
    for target, source in pairs:
        filled[target, source] = 1.0
    return jnp.asarray(filled, bf16)


def strip_pairs(lines, count, first):
    return [
        (line * count + step, line * SIDE + first + step)
        for line in range(lines)
        for step in range(count)
    ]


def edge_picks():
    return [
        table(KV_EDGE, WIDE * SIDE, strip_pairs(WIDE, REACH, 0)),
        table(KV_EDGE, WIDE * SIDE, strip_pairs(WIDE, REACH, SIDE - REACH)),
        table(QG_EDGE, TALL * SIDE, strip_pairs(TALL, RADIUS, 0)),
        table(QG_EDGE, TALL * SIDE, strip_pairs(TALL, RADIUS, SIDE - RADIUS)),
    ]


def middle_picks():
    pairs = strip_pairs(TALL, MIDDLE, RADIUS)
    gather = table(MID_QUERIES, TALL * SIDE, pairs)
    own = [
        (source - QG_ROWS, target)
        for target, source in pairs
        if 0 <= source - QG_ROWS < SIDE * SIDE
    ]
    return gather, table(SIDE * SIDE, MID_QUERIES, own)


def side_spreads():
    key_pairs, query_pairs = [], []
    for part, first in enumerate((0, SIDE - REACH)):
        for target, source in strip_pairs(WIDE, REACH, first):
            if 0 <= source - KV_ROWS < SIDE * SIDE:
                key_pairs.append((source - KV_ROWS, part * OWN_EDGE + target - OWN_FROM))
    for part, first in enumerate((0, SIDE - RADIUS)):
        for target, source in strip_pairs(TALL, RADIUS, first):
            if 0 <= source - QG_ROWS < SIDE * SIDE:
                query_pairs.append((source - QG_ROWS, part * QG_EDGE + target))
    return (
        table(SIDE * SIDE, 2 * OWN_EDGE, key_pairs),
        table(SIDE * SIDE, 2 * QG_EDGE, query_pairs),
    )


def coords(lines, reach, first, count, total, pad):
    ys = [float(line - reach) for line in range(lines) for _ in range(count)]
    xs = [float(first + step) for _ in range(lines) for step in range(count)]
    spare = [pad] * (total - len(ys))
    return np.asarray([ys + spare, xs + spare], np.float32)


def middle_places(heads):
    keys = coords(WIDE, REACH, 0, SIDE, WIDE * SIDE, FAR)
    queries = coords(TALL, RADIUS, RADIUS, MIDDLE, MID_QUERIES, -FAR)
    return jnp.asarray(keys.T), jnp.asarray(np.tile(queries, (1, heads)))


def side_places(heads):
    spots = []
    for key_firsts, query_firsts in (
        ((0, -REACH), (0, -RADIUS)),
        ((SIDE - REACH, SIDE), (SIDE - RADIUS, SIDE)),
    ):
        keys = [coords(WIDE, REACH, f, REACH, KV_EDGE, FAR) for f in key_firsts]
        queries = [coords(TALL, RADIUS, f, RADIUS, QG_EDGE, -FAR) for f in query_firsts]
        spots.append(jnp.asarray(np.concatenate(keys, axis=1).T))
        spots.append(jnp.asarray(np.tile(np.concatenate(queries, axis=1), (1, heads))))
    return spots


def project_kernel(latent, gain, weight, out_weight, cotangent, kv, qg, upper, lower):
    tokens = latent[...].astype(f32)
    inverse = lax.rsqrt(jnp.mean(tokens * tokens, axis=-1, keepdims=True) + 1e-06)
    normed = (tokens * inverse * gain[...]).astype(bf16)
    width = out_weight.shape[0]
    grad_out = nt(cotangent[...], out_weight[...]).astype(bf16)
    query = nn(normed, weight[0]).astype(bf16)
    qg[:, :width] = query * jnp.asarray(HEAD_DIM ** (-0.5), bf16)
    kv[:, :width] = nn(normed, weight[1]).astype(bf16)
    kv[:, width:] = nn(normed, weight[2]).astype(bf16)
    qg[:, width:] = grad_out
    count = latent.shape[0]
    upper[:KV_ROWS] = kv[:KV_ROWS]
    upper[KV_ROWS:] = qg[:QG_ROWS]
    lower[:KV_ROWS] = kv[count - KV_ROWS :]
    lower[KV_ROWS:] = qg[count - QG_ROWS :]


def edges_kernel(kv, qg, above, below, kv_low, kv_high, qg_low, qg_high, left, right):
    kv_all = jnp.concatenate([above[:KV_ROWS], kv[...], below[:KV_ROWS]], axis=0)
    qg_all = jnp.concatenate([above[KV_ROWS:], qg[...], below[KV_ROWS:]], axis=0)
    left[:KV_EDGE] = nn(kv_low[...], kv_all).astype(bf16)
    left[KV_EDGE:] = nn(qg_low[...], qg_all).astype(bf16)
    right[:KV_EDGE] = nn(kv_high[...], kv_all).astype(bf16)
    right[KV_EDGE:] = nn(qg_high[...], qg_all).astype(bf16)


def window_bias(limits, keys, queries):
    key_y, key_x = keys[:, 0:1], keys[:, 1:2]
    top, bottom = limits[0].astype(f32), limits[1].astype(f32)
    left, right = limits[2].astype(f32), limits[3].astype(f32)
    inside = (key_y >= top) & (key_y <= bottom) & (key_x >= left) & (key_x <= right)
    key_y = jnp.where(inside, key_y, FAR)
    apart = jnp.maximum(jnp.abs(key_y - queries[0:1, :]), jnp.abs(key_x - queries[1:2, :]))
    return jnp.where(apart <= RADIUS, 0.0, -1e30)


def by_head(block):
    width = block.shape[1]
    lanes = lax.broadcasted_iota(jnp.int32, (1, width), 1) // HEAD_DIM
    return [jnp.where(lanes == head, block, jnp.zeros_like(block)) for head in range(width // HEAD_DIM)]


def attention(bias, kv, qg, own):
    width = kv.shape[1] // 2
    count = qg.shape[0]
    key, value = kv[:, :width], kv[:, width:]
    query = jnp.concatenate(by_head(qg[:, :width]), axis=0)
    upstream = jnp.concatenate(by_head(qg[:, width:]), axis=0)
    scores = nt(key, query) + bias
    dots = nt(value, upstream)
    exponent = jnp.exp(scores - jnp.max(scores, axis=0, keepdims=True))
    scale = 1.0 / jnp.sum(exponent, axis=0, keepdims=True)
    weights = exponent * scale
    centre = jnp.sum(weights * dots, axis=0, keepdims=True)
    score_grads = (weights * (dots - centre)).astype(bf16)
    value_grad = nn(weights[own].astype(bf16), upstream)
    key_grad = nn(score_grads[own], query)
    stacked = nn(key.astype(f32).T.astype(bf16), score_grads).T
    parts = [stacked[first : first + count] for first in range(0, stacked.shape[0], count)]
    lanes = lax.broadcasted_iota(jnp.int32, (1, width), 1) // HEAD_DIM
    query_grad = parts[0]
    for head in range(1, len(parts)):
        query_grad = jnp.where(lanes == head, parts[head], query_grad)
    return query_grad * (HEAD_DIM ** (-0.5)), key_grad, value_grad


def middle_kernel(
    limits, kv, qg, above, below, keys, queries, gather, spread, query_out, pair_out
):
    width = kv.shape[1] // 2
    count = kv.shape[0]
    kv_all = jnp.concatenate([above[:KV_ROWS], kv[...], below[:KV_ROWS]], axis=0)
    qg_all = jnp.concatenate([above[KV_ROWS:], qg[...], below[KV_ROWS:]], axis=0)
    qg_mid = nn(gather[...], qg_all).astype(bf16)
    bias = window_bias(limits, keys, queries)
    own = slice(KV_ROWS, KV_ROWS + count)
    query_grad, key_grad, value_grad = attention(bias, kv_all, qg_mid, own)
    query_out[...] = nn(spread[...], query_grad.astype(bf16)).astype(bf16)
    pair_out[:, :width] = key_grad
    pair_out[:, width:] = value_grad


def sides_kernel(
    limits, leftward, from_left, rightward, from_right, query_mid, pair_mid, left_keys,
    left_queries, right_keys, right_queries, key_spread, query_spread, weight, partial
):
    width = query_mid.shape[1]
    own = slice(OWN_FROM, OWN_FROM + OWN_EDGE)
    query_parts, pair_parts = [], []
    for mine, theirs, keys, queries in (
        (leftward, from_left, left_keys, left_queries),
        (rightward, from_right, right_keys, right_queries),
    ):
        kv = jnp.concatenate([mine[:KV_EDGE], theirs[:KV_EDGE]], axis=0)
        qg = jnp.concatenate([mine[KV_EDGE:], theirs[KV_EDGE:]], axis=0)
        bias = window_bias(limits, keys, queries)
        query_grad, key_grad, value_grad = attention(bias, kv, qg, own)
        query_parts.append(query_grad[:QG_EDGE])
        pair_parts.append(jnp.concatenate([key_grad, value_grad], axis=1))
    query_side = jnp.concatenate(query_parts, axis=0).astype(bf16)
    pair_side = jnp.concatenate(pair_parts, axis=0)
    coarse = pair_side.astype(bf16)
    fine = (pair_side - coarse.astype(f32)).astype(bf16)
    pair = pair_mid[...] + (nn(key_spread[...], coarse) + nn(key_spread[...], fine))
    query_grad = query_mid[...].astype(f32) + nn(query_spread[...], query_side)
    pair = pair.astype(bf16)
    total = nt(query_grad.astype(bf16), weight[0])
    total += nt(pair[:, :width], weight[1])
    total += nt(pair[:, width:], weight[2])
    partial[...] = total.astype(bf16)


def finish_kernel(place, received, latent, gain, cotangent, result):
    count = received.shape[1]
    first = pl.multiple_of(place[0] * count, count)
    tokens = latent[pl.ds(first, count), :].astype(f32)
    upstream = cotangent[pl.ds(first, count), :].astype(f32)
    summed = received[0].astype(f32)
    for part in range(1, received.shape[0]):
        summed += received[part].astype(f32)
    inverse = lax.rsqrt(jnp.mean(tokens * tokens, axis=-1, keepdims=True) + 1e-06)
    unit = tokens * inverse
    scaled = summed * gain[...]
    stat = jnp.mean(scaled * unit, axis=-1, keepdims=True)
    result[...] = upstream + inverse * (scaled - unit * stat)


def moved(block, axis, distance):
    count = lax.axis_size(axis)
    route = [(i, i + distance) for i in range(count) if 0 <= i + distance < count]
    return lax.ppermute(block, axis, route)


def per_device(latent, norm_gain, qkv_weight, out_weight, cotangent):
    tile_rows, tile_cols, model_width = latent.shape
    head_cols = out_weight.shape[0]
    count = tile_rows * tile_cols
    tp = lax.axis_size("tp")
    flat_latent = latent.reshape(count, model_width)
    flat_cotangent = cotangent.reshape(count, model_width)
    gain = norm_gain.reshape(1, model_width)
    weight = qkv_weight.transpose(1, 0, 2)
    shape = jax.ShapeDtypeStruct
    edge = shape((KV_ROWS + QG_ROWS, 2 * head_cols), bf16)
    row, col = lax.axis_index("row"), lax.axis_index("col")
    limits = jnp.stack(
        [
            -row * tile_rows,
            (lax.axis_size("row") - row) * tile_rows - 1,
            -col * tile_cols,
            (lax.axis_size("col") - col) * tile_cols - 1,
        ]
    ).astype(jnp.int32)
    kv, qg, upper, lower = pl.pallas_call(
        project_kernel,
        out_shape=[shape((count, 2 * head_cols), bf16)] * 2 + [edge] * 2,
        in_specs=[VMEM] * 5,
        out_specs=[VMEM] * 4,
        compiler_params=PARAMS,
        name="project",
    )(flat_latent, gain, weight, out_weight, flat_cotangent)
    above = moved(lower, "row", 1)
    below = moved(upper, "row", -1)
    side = shape((KV_EDGE + QG_EDGE, 2 * head_cols), bf16)
    leftward, rightward = pl.pallas_call(
        edges_kernel,
        out_shape=[side] * 2,
        in_specs=[VMEM] * 8,
        out_specs=[VMEM] * 2,
        compiler_params=PARAMS,
        name="edges",
    )(kv, qg, above, below, *edge_picks())
    from_left = moved(rightward, "col", 1)
    from_right = moved(leftward, "col", -1)
    heads = head_cols // HEAD_DIM
    query_mid, pair_mid = pl.pallas_call(
        middle_kernel,
        out_shape=[shape((count, head_cols), bf16), shape((count, 2 * head_cols), f32)],
        in_specs=[SMEM] + [VMEM] * 8,
        out_specs=[VMEM] * 2,
        compiler_params=PARAMS,
        name="middle",
    )(limits, kv, qg, above, below, *middle_places(heads), *middle_picks())
    partial = pl.pallas_call(
        sides_kernel,
        out_shape=shape((count, model_width), bf16),
        in_specs=[SMEM] + [VMEM] * 13,
        out_specs=VMEM,
        compiler_params=PARAMS,
        name="sides",
    )(
        limits, leftward, from_left, rightward, from_right, query_mid, pair_mid,
        *side_places(heads), *side_spreads(), weight,
    )
    own = count // tp
    received = lax.all_to_all(partial.reshape(tp, own, model_width), "tp", 0, 0)
    place = lax.axis_index("tp").astype(jnp.int32).reshape(1)
    result = pl.pallas_call(
        finish_kernel,
        out_shape=shape((own, model_width), f32),
        in_specs=[SMEM] + [VMEM] * 4,
        out_specs=VMEM,
        compiler_params=PARAMS,
        name="finish",
    )(place, received, flat_latent, gain, flat_cotangent)
    return result.reshape(own // tile_cols, tile_cols, model_width)


def solution(mesh):
    placed = (P("row", "col", None), P(), P(None, None, "tp"), P("tp", None), P("row", "col", None))
    return jax.shard_map(
        per_device,
        mesh=mesh,
        in_specs=placed,
        out_specs=P(("row", "tp"), "col", None),
        check_vma=False,
    )
```

time: 71.2 us -> 64.8 us (0.910)
  the two profiles are of different devices: /device:TPU:194 before, /device:TPU:195 now
where the time goes in v2:
time: 64.8 us; the launch traced here: 64.4 us
  waiting for transfers between devices  22.8 us (35%)
  starting transfers between devices  20.5 us (32%)
  Pallas kernels  18.3 us (28%)
  local copies, waits for them, and re-layouts  2.21 us (3%)
    ppermute x4, starting transfers between devices, moved(): return lax.ppermute(block, axis, route)  17 us
    all_to_all x1, waiting for transfers between devices, per_device(): received = lax.all_to_all(partial.reshape(tp, own, model_width), 'tp', 0, 0)  13.8 us
    ppermute x4, waiting for transfers between devices, moved(): return lax.ppermute(block, axis, route)  8.96 us
    pallas_call x1, Pallas kernels, per_device(): pl.pallas_call(sides_kernel, out_shape=shape((count, model_width), bf16),...  5.81 us
    pallas_call x1, Pallas kernels, per_device(): pl.pallas_call(middle_kernel, out_shape=[shape((count, head_cols), bf16),...  4.27 us
    all_to_all x1, starting transfers between devices, per_device(): received = lax.all_to_all(partial.reshape(tp, own, model_width), 'tp', 0, 0)  3.47 us
    pallas_call x1, Pallas kernels, per_device(): pl.pallas_call(project_kernel, out_shape=[shape((count, 2 * head_cols), b...  3.42 us
    pallas_call x1, Pallas kernels, per_device(): pl.pallas_call(edges_kernel, out_shape=[side] * 2, in_specs=[VMEM] * 8, o...  2.45 us
  transfers between devices with their start and end apart: 5, of which 3 were waited for; matrix products, arithmetic and copies ran while one was open for 1% of the time, Pallas kernels for 7%

profile of v2, /device:TPU:195, one launch (start us, length us, event | category | flops | bytes accessed | tf_op | source)
XLA Modules:
  0.0 64.4 jit_solution(4728090918219570761)
XLA Ops:
  0.0 3.4 %project.1 = (bf16[256,512]{1,0:T(8,128)(2,1)}, bf16[256,512]{1,0:T(8,128)(2,1)}, bf16[144,512]{1,0:T(8,128)(2,1)}, bf16[144,512]{1,0:T(8,128)(2,1)}) custom-call(bf16[256,1024]{1,0:T(8,128)(2,1)} %bitcast.14, f32[1,1024]{1,0:T(1,128)} %bitcast.18, bf16[3,1024,256]{2,1,0:T(8,128)(2,1)} %bitcast.11, bf16[256,1024]{1,0:T(8,128)(2,1)} %out_weight.1, ...), custom_call_target="tpu_custom_call" | custom-call | tf_op jit(solution)/shard_map/project/pallas_call | solution.py:270
  3.4 8.0 %collective-permute-start = (bf16[144,512]{1,0:T(8,128)(2,1)}, bf16[144,512]{1,0:T(8,128)(2,1)S(1)}, u32[]{:S(2)}, u32[]{:S(2)}) collective-permute-start(bf16[144,512]{1,0:T(8,128)(2,1)} %get-tuple-element.15), channel_id=1, source_target_pairs={{0,32},{32,64},{64,96},{96,128},{128,160},{160,192},{192,224},{224... | collective-permute-start | bytes 442376 | tf_op jit(solution)/shard_map/ppermute | solution.py:247
  11.4 1.9 %collective-permute-start.1 = (bf16[144,512]{1,0:T(8,128)(2,1)}, bf16[144,512]{1,0:T(8,128)(2,1)S(1)}, u32[]{:S(2)}, u32[]{:S(2)}) collective-permute-start(bf16[144,512]{1,0:T(8,128)(2,1)} %get-tuple-element.16), channel_id=1, source_target_pairs={{32,0},{64,32},{96,64},{128,96},{160,128},{192,160},{224,192},{256... | collective-permute-start | bytes 442376 | tf_op jit(solution)/shard_map/ppermute | solution.py:247
  13.4 0.6 collective-permute-done.above
  13.9 0.0 copy-start.1
  13.9 8.4 %collective-permute-done.1.below = bf16[144,512]{1,0:T(8,128)(2,1)S(1)} collective-permute-done((bf16[144,512]{1,0:T(8,128)(2,1)}, bf16[144,512]{1,0:T(8,128)(2,1)S(1)}, u32[]{:S(2)}, u32[]{:S(2)}) %collective-permute-start.1) | collective-permute-done | bytes 147488 | tf_op jit(solution)/shard_map/ppermute | solution.py:247
  22.3 0.0 copy-start.2
  22.3 0.0 copy-done.1
  22.3 0.6 copy-done.2
  23.0 2.5 %edges.1 = (bf16[256,512]{1,0:T(8,128)(2,1)}, bf16[256,512]{1,0:T(8,128)(2,1)}) custom-call(bf16[256,512]{1,0:T(8,128)(2,1)} %get-tuple-element.13.kv, bf16[256,512]{1,0:T(8,128)(2,1)} %get-tuple-element.14.qg, bf16[144,512]{1,0:T(8,128)(2,1)} %copy-done.1, bf16[144,512]{1,0:T(8,128)(2,1)} %copy-done.2, bf16[176,448]{1,0:T(8,128)(2,1)} %constant.51.clone.kv_low, ...), custom_call_target="tpu_custom_call" | custom-call | tf_op jit(solution)/shard_map/edges/pallas_call | solution.py:281
  25.4 1.9 %collective-permute-start.3 = (bf16[256,512]{1,0:T(8,128)(2,1)}, bf16[256,512]{1,0:T(8,128)(2,1)S(1)}, u32[]{:S(2)}, u32[]{:S(2)}) collective-permute-start(bf16[256,512]{1,0:T(8,128)(2,1)} %get-tuple-element.17.leftward), channel_id=1, source_target_pairs={{4,0},{8,4},{12,8},{16,12},{20,16},{24,20},{28,24},{5,1},{9,5},{13... | collective-permute-start | bytes 786440 | tf_op jit(solution)/shard_map/ppermute | solution.py:247
  27.3 5.2 %collective-permute-start.2 = (bf16[256,512]{1,0:T(8,128)(2,1)}, bf16[256,512]{1,0:T(8,128)(2,1)S(1)}, u32[]{:S(2)}, u32[]{:S(2)}) collective-permute-start(bf16[256,512]{1,0:T(8,128)(2,1)} %get-tuple-element.18.rightward), channel_id=1, source_target_pairs={{0,4},{4,8},{8,12},{12,16},{16,20},{20,24},{24,28},{1,5},{5,9},{9,... | collective-permute-start | bytes 786440 | tf_op jit(solution)/shard_map/ppermute | solution.py:247
  32.6 0.6 pad_add_fusion.limits
  33.2 4.3 %middle.1 = (bf16[256,256]{1,0:T(8,128)(2,1)}, f32[256,512]{1,0:T(8,128)}) custom-call(s32[4]{0:T(128)} %pad_add_fusion.limits, bf16[256,512]{1,0:T(8,128)(2,1)} %get-tuple-element.13.kv, bf16[256,512]{1,0:T(8,128)(2,1)} %get-tuple-element.14.qg, bf16[144,512]{1,0:T(8,128)(2,1)} %copy-done.1, bf16[144,512]{1,0:T(8,128)(2,1)} %copy-done.2, ...), custom_call_target="tpu_custom_call" | custom-call | tf_op jit(solution)/shard_map/middle/pallas_call | solution.py:292
  37.4 0.0 collective-permute-done.3.from_right
  37.4 0.0 copy-start.3
  37.4 0.0 collective-permute-done.2.from_left
  37.4 0.0 copy-start.4
  37.5 0.7 %copy-done.3 = bf16[256,512]{1,0:T(8,128)(2,1)} copy-done((bf16[256,512]{1,0:T(8,128)(2,1)}, bf16[256,512]{1,0:T(8,128)(2,1)S(1)}, u32[]{:S(2)}) %copy-start.3) | copy-done | bytes 262168
  38.1 0.1 copy-done.4
  38.2 5.8 %sides.1 = bf16[256,1024]{1,0:T(8,128)(2,1)} custom-call(s32[4]{0:T(128)} %pad_add_fusion.limits, bf16[256,512]{1,0:T(8,128)(2,1)} %get-tuple-element.17.leftward, bf16[256,512]{1,0:T(8,128)(2,1)} %copy-done.4, bf16[256,512]{1,0:T(8,128)(2,1)} %get-tuple-element.18.rightward, bf16[256,512]{1,0:T(8,128)(2,1)} %copy-done.3, ...), custom_call_target="tpu_custom_call" | custom-call | tf_op jit(solution)/shard_map/sides/pallas_call | solution.py:300
  44.0 3.5 %all-to-all-start = ((bf16[4,64,1024]{2,1,0:T(8,128)(2,1)}), bf16[4,64,1024]{2,1,0:T(8,128)(2,1)S(1)}, u32[]{:S(2)}, u32[]{:S(2)}) async-start(bf16[4,64,1024]{2,1,0:T(8,128)(2,1)} %bitcast.13), calls=%async_computation | async-start | bytes 1048576 | tf_op jit(solution)/shard_map/all_to_all | solution.py:312
  47.5 13.8 %all-to-all-done.received = bf16[4,64,1024]{2,1,0:T(8,128)(2,1)S(1)} async-done(((bf16[4,64,1024]{2,1,0:T(8,128)(2,1)}), bf16[4,64,1024]{2,1,0:T(8,128)(2,1)S(1)}, u32[]{:S(2)}, u32[]{:S(2)}) %all-to-all-start) | async-done | bytes 524320 | tf_op jit(solution)/shard_map/all_to_all | solution.py:312
  61.3 0.0 copy-start
  61.3 0.8 %copy-done = bf16[4,64,1024]{2,1,0:T(8,128)(2,1)} copy-done((bf16[4,64,1024]{2,1,0:T(8,128)(2,1)}, bf16[4,64,1024]{2,1,0:T(8,128)(2,1)S(1)}, u32[]{:S(2)}) %copy-start) | copy-done | bytes 524312
  62.1 2.3 %finish.1 = f32[64,1024]{1,0:T(8,128)} custom-call(s32[1]{0:T(128)} %bitcast.place, bf16[4,64,1024]{2,1,0:T(8,128)(2,1)} %copy-done, bf16[256,1024]{1,0:T(8,128)(2,1)} %bitcast.15, f32[1,1024]{1,0:T(1,128)} %bitcast.19, bf16[256,1024]{1,0:T(8,128)(2,1)} %bitcast.17), custom_call_target="tpu_custom_call" | custom-call | tf_op jit(solution)/shard_map/finish/pallas_call | solution.py:314
Async XLA Ops:
  3.4 10.5 %collective-permute-start = (bf16[144,512]{1,0:T(8,128)(2,1)}, bf16[144,512]{1,0:T(8,128)(2,1)S(1)}, u32[]{:S(2)}, u32[]{:S(2)}) collective-permute-start(bf16[144,512]{1,0:T(8,128)(2,1)} %get-tuple-element.15), channel_id=1, source_target_pairs={{0,32},{32,64},{64,96},{96,128},{128,160},{160,192},{192,224},{224... | collective-permute-start | bytes 442376 | tf_op jit(solution)/shard_map/ppermute | solution.py:247
  11.4 10.9 %collective-permute-start.1 = (bf16[144,512]{1,0:T(8,128)(2,1)}, bf16[144,512]{1,0:T(8,128)(2,1)S(1)}, u32[]{:S(2)}, u32[]{:S(2)}) collective-permute-start(bf16[144,512]{1,0:T(8,128)(2,1)} %get-tuple-element.16), channel_id=1, source_target_pairs={{32,0},{64,32},{96,64},{128,96},{160,128},{192,160},{224,192},{256... | collective-permute-start | bytes 442376 | tf_op jit(solution)/shard_map/ppermute | solution.py:247
  13.9 8.4 %copy-start.1 = (bf16[144,512]{1,0:T(8,128)(2,1)}, bf16[144,512]{1,0:T(8,128)(2,1)S(1)}, u32[]{:S(2)}) copy-start(bf16[144,512]{1,0:T(8,128)(2,1)S(1)} %collective-permute-done.above) | copy-start | bytes 442372
  22.3 0.6 %copy-start.2 = (bf16[144,512]{1,0:T(8,128)(2,1)}, bf16[144,512]{1,0:T(8,128)(2,1)S(1)}, u32[]{:S(2)}) copy-start(bf16[144,512]{1,0:T(8,128)(2,1)S(1)} %collective-permute-done.1.below) | copy-start | bytes 442372
  25.4 12.0 %collective-permute-start.3 = (bf16[256,512]{1,0:T(8,128)(2,1)}, bf16[256,512]{1,0:T(8,128)(2,1)S(1)}, u32[]{:S(2)}, u32[]{:S(2)}) collective-permute-start(bf16[256,512]{1,0:T(8,128)(2,1)} %get-tuple-element.17.leftward), channel_id=1, source_target_pairs={{4,0},{8,4},{12,8},{16,12},{20,16},{24,20},{28,24},{5,1},{9,5},{13... | collective-permute-start | bytes 786440 | tf_op jit(solution)/shard_map/ppermute | solution.py:247
  27.3 10.1 %collective-permute-start.2 = (bf16[256,512]{1,0:T(8,128)(2,1)}, bf16[256,512]{1,0:T(8,128)(2,1)S(1)}, u32[]{:S(2)}, u32[]{:S(2)}) collective-permute-start(bf16[256,512]{1,0:T(8,128)(2,1)} %get-tuple-element.18.rightward), channel_id=1, source_target_pairs={{0,4},{4,8},{8,12},{12,16},{16,20},{20,24},{24,28},{1,5},{5,9},{9,... | collective-permute-start | bytes 786440 | tf_op jit(solution)/shard_map/ppermute | solution.py:247
  37.4 0.7 %copy-start.3 = (bf16[256,512]{1,0:T(8,128)(2,1)}, bf16[256,512]{1,0:T(8,128)(2,1)S(1)}, u32[]{:S(2)}) copy-start(bf16[256,512]{1,0:T(8,128)(2,1)S(1)} %collective-permute-done.3.from_right) | copy-start | bytes 786436
  37.4 0.8 %copy-start.4 = (bf16[256,512]{1,0:T(8,128)(2,1)}, bf16[256,512]{1,0:T(8,128)(2,1)S(1)}, u32[]{:S(2)}) copy-start(bf16[256,512]{1,0:T(8,128)(2,1)S(1)} %collective-permute-done.2.from_left) | copy-start | bytes 786436
  44.0 17.3 %all-to-all-start = ((bf16[4,64,1024]{2,1,0:T(8,128)(2,1)}), bf16[4,64,1024]{2,1,0:T(8,128)(2,1)S(1)}, u32[]{:S(2)}, u32[]{:S(2)}) async-start(bf16[4,64,1024]{2,1,0:T(8,128)(2,1)} %bitcast.13), calls=%async_computation | async-start | bytes 1048576 | tf_op jit(solution)/shard_map/all_to_all | solution.py:312
  61.3 0.8 %copy-start = (bf16[4,64,1024]{2,1,0:T(8,128)(2,1)}, bf16[4,64,1024]{2,1,0:T(8,128)(2,1)S(1)}, u32[]{:S(2)}) copy-start(bf16[4,64,1024]{2,1,0:T(8,128)(2,1)S(1)} %all-to-all-done.received) | copy-start | bytes 1572868

commit v3 on v2

v3 whole, which is shorter than its diff:
```python
import functools

import jax
import jax.numpy as jnp
import numpy as np
from jax import lax
from jax.experimental import pallas as pl
from jax.experimental.pallas import tpu as pltpu
from jax.sharding import PartitionSpec as P

HEAD_DIM = 64
RADIUS = 3
REACH = 2 * RADIUS
SIDE = 16
WIDE = SIDE + 2 * REACH
TALL = SIDE + 2 * RADIUS
KV_ROWS = REACH * SIDE
QG_ROWS = RADIUS * SIDE
KV_EDGE = 176
QG_EDGE = 80
MIDDLE = SIDE - 2 * RADIUS
MID_QUERIES = 224
OWN_FROM = 32
OWN_EDGE = 112
FAR = 1000.0
bf16 = jnp.bfloat16
f32 = jnp.float32
VMEM = pl.BlockSpec(memory_space=pltpu.VMEM)
HERE = pl.BlockSpec(memory_space=pltpu.VMEM)
SMEM = pl.BlockSpec(memory_space=pltpu.SMEM)
FAR_SPACE = pl.BlockSpec(memory_space=pltpu.HBM)
PARAMS = pltpu.CompilerParams(vmem_limit_bytes=32 * 1024 * 1024)


def in_hbm(block):
    return pltpu.with_memory_space_constraint(block, pltpu.HBM)


def near_call(kernel, name, outs, specs, *operands):
    fixed = [
        pltpu.with_memory_space_constraint(x, pltpu.VMEM) if spec is VMEM else x
        for x, spec in zip(operands, specs)
    ]
    places = [VMEM if spec is HERE else spec for spec in specs]
    return pl.pallas_call(
        kernel,
        out_shape=outs,
        in_specs=places,
        out_specs=jax.tree.map(lambda _: VMEM, outs),
        compiler_params=PARAMS,
        name=name,
    )(*fixed)


def nt(a, b):
    return lax.dot_general(a, b, (((1,), (1,)), ((), ())), preferred_element_type=f32)


def nn(a, b):
    return jnp.dot(a, b, preferred_element_type=f32)


def table(out_rows, in_rows, pairs):
    filled = np.zeros((out_rows, in_rows), np.float32)
    for target, source in pairs:
        filled[target, source] = 1.0
    return jnp.asarray(filled, bf16)


def strip_pairs(lines, count, first):
    return [
        (line * count + step, line * SIDE + first + step)
        for line in range(lines)
        for step in range(count)
    ]


GATHERS = {
    "kv_edges": (0, 2 * KV_EDGE, WIDE * SIDE),
    "qg_edges": (2 * KV_EDGE, 2 * QG_EDGE, TALL * SIDE),
    "middle": (2 * KV_EDGE + 2 * QG_EDGE, MID_QUERIES, TALL * SIDE),
}
SPREADS = {
    "middle": (0, SIDE * SIDE, MID_QUERIES),
    "keys": (SIDE * SIDE, SIDE * SIDE, 2 * OWN_EDGE),
    "queries": (2 * SIDE * SIDE, SIDE * SIDE, 2 * QG_EDGE),
}


def part_of(ref, spot):
    first, rows, cols = spot
    return ref[first : first + rows, :cols]


def gathers():
    pairs = []
    for part, first in enumerate((0, SIDE - REACH)):
        pairs += [(part * KV_EDGE + t, f) for t, f in strip_pairs(WIDE, REACH, first)]
    begin = GATHERS["qg_edges"][0]
    for part, first in enumerate((0, SIDE - RADIUS)):
        pairs += [(begin + part * QG_EDGE + t, f) for t, f in strip_pairs(TALL, RADIUS, first)]
    begin = GATHERS["middle"][0]
    pairs += [(begin + t, f) for t, f in strip_pairs(TALL, MIDDLE, RADIUS)]
    return table(begin + MID_QUERIES, WIDE * SIDE, pairs)


def spreads():
    pairs = []

    def add(name, halo, column, target):
        token = target - halo * SIDE
        if 0 <= token < SIDE * SIDE:
            pairs.append((SPREADS[name][0] + token, column))

    for t, f in strip_pairs(TALL, MIDDLE, RADIUS):
        add("middle", RADIUS, t, f)
    for part, first in enumerate((0, SIDE - REACH)):
        for t, f in strip_pairs(WIDE, REACH, first):
            add("keys", REACH, part * OWN_EDGE + t - OWN_FROM, f)
    for part, first in enumerate((0, SIDE - RADIUS)):
        for t, f in strip_pairs(TALL, RADIUS, first):
            add("queries", RADIUS, part * QG_EDGE + t, f)
    return table(3 * SIDE * SIDE, SIDE * SIDE, pairs)


def coords(lines, reach, first, count, total, pad):
    ys = [float(line - reach) for line in range(lines) for _ in range(count)]
    xs = [float(first + step) for _ in range(lines) for step in range(count)]
    spare = [pad] * (total - len(ys))
    return np.asarray([ys + spare, xs + spare], np.float32)


def places(heads):
    keys = [coords(WIDE, REACH, 0, SIDE, WIDE * SIDE, FAR)]
    queries = [np.tile(coords(TALL, RADIUS, RADIUS, MIDDLE, MID_QUERIES, -FAR), (1, heads))]
    for key_firsts, query_firsts in (
        ((0, -REACH), (0, -RADIUS)),
        ((SIDE - REACH, SIDE), (SIDE - RADIUS, SIDE)),
    ):
        keys += [coords(WIDE, REACH, f, REACH, KV_EDGE, FAR) for f in key_firsts]
        both = [coords(TALL, RADIUS, f, RADIUS, QG_EDGE, -FAR) for f in query_firsts]
        queries.append(np.tile(np.concatenate(both, axis=1), (1, heads)))
    keys, queries = np.concatenate(keys, axis=1), np.concatenate(queries, axis=1)
    joined = np.full((8, queries.shape[1]), FAR, np.float32)
    joined[:2, : keys.shape[1]] = keys
    joined[2:4] = queries
    return jnp.asarray(joined)


def project_kernel(
    row, col, place, latent_any, gain, weight_any, out_weight_any, cotangent_any, kv, qg, far, near,
    latent, weight, out_weight, cotangent, sems
):
    copies = [
        pltpu.make_async_copy(source, target, sems.at[i])
        for i, (source, target) in enumerate(
            (
                (latent_any, latent),
                (weight_any.at[1], weight.at[1]),
                (weight_any.at[2], weight.at[2]),
                (weight_any.at[0], weight.at[0]),
                (cotangent_any, cotangent),
                (out_weight_any, out_weight),
            )
        )
    ]
    for copy in copies:
        copy.start()
    width = out_weight.shape[0]
    copies[0].wait()
    tokens = latent[...].astype(f32)
    inverse = lax.rsqrt(jnp.mean(tokens * tokens, axis=-1, keepdims=True) + 1e-06)
    normed = (tokens * inverse * gain[...]).astype(bf16)
    copies[1].wait()
    copies[2].wait()
    kv[:, :width] = nn(normed, weight[1]).astype(bf16)
    kv[:, width:] = nn(normed, weight[2]).astype(bf16)
    for copy in copies[3:]:
        copy.wait()
    query = nn(normed, weight[0]).astype(bf16)
    qg[:, :width] = query * jnp.asarray(HEAD_DIM ** (-0.5), bf16)
    qg[:, width:] = nt(cotangent[...], out_weight[...]).astype(bf16)
    count = latent.shape[0]
    odd = lax.rem(row[0], 2)
    for strip, at_end in ((far, odd), (near, 1 - odd)):
        first = pl.multiple_of(at_end * (count - KV_ROWS), SIDE)
        strip[:KV_ROWS] = kv[pl.ds(first, KV_ROWS), :]
        first = pl.multiple_of(at_end * (count - QG_ROWS), SIDE)
        strip[KV_ROWS:] = qg[pl.ds(first, QG_ROWS), :]


def tall_blocks(row, kv, qg, far, near):
    odd = lax.rem(row[0], 2) == 1
    above = jnp.where(odd, near[...], far[...])
    below = jnp.where(odd, far[...], near[...])
    kv_all = jnp.concatenate([above[:KV_ROWS], kv[...], below[:KV_ROWS]], axis=0)
    qg_all = jnp.concatenate([above[KV_ROWS:], qg[...], below[KV_ROWS:]], axis=0)
    return kv_all, qg_all


def edges_kernel(row, kv, qg, far, near, gather, left, right, kv_tall, qg_tall):
    kv_all, qg_all = tall_blocks(row, kv, qg, far, near)
    kv_tall[...] = kv_all
    qg_tall[...] = qg_all
    kv_edges = nn(part_of(gather, GATHERS["kv_edges"]), kv_all).astype(bf16)
    qg_edges = nn(part_of(gather, GATHERS["qg_edges"]), qg_all).astype(bf16)
    left[:KV_EDGE] = kv_edges[:KV_EDGE]
    left[KV_EDGE:] = qg_edges[:QG_EDGE]
    right[:KV_EDGE] = kv_edges[KV_EDGE:]
    right[KV_EDGE:] = qg_edges[QG_EDGE:]


def window_bias(spot, extent, keys, queries):
    key_y, key_x = keys[:, 0:1], keys[:, 1:2]
    top, left = (-(at * SIDE).astype(f32) for at in spot)
    bottom, right = ((((n - at) * SIDE) - 1).astype(f32) for at, n in zip(spot, extent))
    inside = (key_y >= top) & (key_y <= bottom) & (key_x >= left) & (key_x <= right)
    key_y = jnp.where(inside, key_y, FAR)
    apart = jnp.maximum(jnp.abs(key_y - queries[0:1, :]), jnp.abs(key_x - queries[1:2, :]))
    return jnp.where(apart <= RADIUS, 0.0, -1e30)


def by_head(block):
    width = block.shape[1]
    lanes = lax.broadcasted_iota(jnp.int32, (1, width), 1) // HEAD_DIM
    return [jnp.where(lanes == head, block, jnp.zeros_like(block)) for head in range(width // HEAD_DIM)]


def attention(bias, kv, qg, own):
    width = kv.shape[1] // 2
    count = qg.shape[0]
    key, value = kv[:, :width], kv[:, width:]
    query = jnp.concatenate(by_head(qg[:, :width]), axis=0)
    upstream = jnp.concatenate(by_head(qg[:, width:]), axis=0)
    scores = nt(key, query) + bias
    dots = nt(value, upstream)
    exponent = jnp.exp(scores - jnp.max(scores, axis=0, keepdims=True))
    scale = 1.0 / jnp.sum(exponent, axis=0, keepdims=True)
    weights = exponent * scale
    centre = jnp.sum(weights * dots, axis=0, keepdims=True)
    score_grads = (weights * (dots - centre)).astype(bf16)
    value_grad = nn(weights[own].astype(bf16), upstream)
    key_grad = nn(score_grads[own], query)
    stacked = nn(key.astype(f32).T.astype(bf16), score_grads).T
    parts = [stacked[first : first + count] for first in range(0, stacked.shape[0], count)]
    lanes = lax.broadcasted_iota(jnp.int32, (1, width), 1) // HEAD_DIM
    query_grad = parts[0]
    for head in range(1, len(parts)):
        query_grad = jnp.where(lanes == head, parts[head], query_grad)
    return query_grad * (HEAD_DIM ** (-0.5)), key_grad, value_grad


def middle_kernel(
    extent, row, col, kv, qg, points, gather, spread, query_out, pair_out, left_bias, right_bias
):
    count, width = query_out.shape
    spot = (row[0], col[0])
    keys, queries = points[...].T, points[2:4]
    qg_mid = nn(part_of(gather, GATHERS["middle"]), qg[...]).astype(bf16)
    first_key, first_query = kv.shape[0], MID_QUERIES * width // HEAD_DIM
    bias = window_bias(spot, extent, keys[:first_key], queries[:, :first_query])
    own = slice(KV_ROWS, KV_ROWS + count)
    query_grad, key_grad, value_grad = attention(bias, kv[...], qg_mid, own)
    scattered = nn(part_of(spread, SPREADS["middle"]), query_grad.astype(bf16))
    query_out[...] = scattered.astype(bf16)
    pair_out[:, :width] = key_grad
    pair_out[:, width:] = value_grad
    for side in (left_bias, right_bias):
        last_key, last_query = first_key + side.shape[0], first_query + side.shape[1]
        side[...] = window_bias(
            spot, extent, keys[first_key:last_key], queries[:, first_query:last_query]
        )
        first_key, first_query = last_key, last_query


def sides_kernel(
    leftward, from_left, rightward, from_right, query_mid, pair_mid, left_bias, right_bias,
    spread, weight, partial
):
    width = query_mid.shape[1]
    own = slice(OWN_FROM, OWN_FROM + OWN_EDGE)
    query_parts, pair_parts = [], []
    for mine, theirs, bias in (
        (leftward, from_left, left_bias),
        (rightward, from_right, right_bias),
    ):
        kv = jnp.concatenate([mine[:KV_EDGE], theirs[:KV_EDGE]], axis=0)
        qg = jnp.concatenate([mine[KV_EDGE:], theirs[KV_EDGE:]], axis=0)
        query_grad, key_grad, value_grad = attention(bias[...], kv, qg, own)
        query_parts.append(query_grad[:QG_EDGE])
        pair_parts.append(jnp.concatenate([key_grad, value_grad], axis=1))
    query_side = jnp.concatenate(query_parts, axis=0).astype(bf16)
    pair_side = jnp.concatenate(pair_parts, axis=0)
    coarse = pair_side.astype(bf16)
    fine = (pair_side - coarse.astype(f32)).astype(bf16)
    key_spread, query_spread = (part_of(spread, SPREADS[name]) for name in ("keys", "queries"))
    pair = pair_mid[...] + (nn(key_spread, coarse) + nn(key_spread, fine))
    query_grad = query_mid[...].astype(f32) + nn(query_spread, query_side)
    pair = pair.astype(bf16)
    total = nt(query_grad.astype(bf16), weight[0])
    total += nt(pair[:, :width], weight[1])
    total += nt(pair[:, width:], weight[2])
    partial[...] = total.astype(bf16)


def finish_kernel(place, received, latent, gain, cotangent, result):
    count = received.shape[1]
    first = pl.multiple_of(place[0] * count, count)
    tokens = latent[pl.ds(first, count), :].astype(f32)
    upstream = cotangent[pl.ds(first, count), :].astype(f32)
    summed = received[0].astype(f32)
    for part in range(1, received.shape[0]):
        summed += received[part].astype(f32)
    inverse = lax.rsqrt(jnp.mean(tokens * tokens, axis=-1, keepdims=True) + 1e-06)
    unit = tokens * inverse
    scaled = summed * gain[...]
    stat = jnp.mean(scaled * unit, axis=-1, keepdims=True)
    result[...] = upstream + inverse * (scaled - unit * stat)


def paired(block, axis, first):
    count = lax.axis_size(axis)
    route = []
    for low in range(first, count - 1, 2):
        route += [(low, low + 1), (low + 1, low)]
    return lax.ppermute(block, axis, route)


def moved(block, axis, distance):
    count = lax.axis_size(axis)
    route = [(i, i + distance) for i in range(count) if 0 <= i + distance < count]
    return lax.ppermute(block, axis, route)


def per_device(latent, norm_gain, qkv_weight, out_weight, cotangent):
    tile_rows, tile_cols, model_width = latent.shape
    head_cols = out_weight.shape[0]
    count = tile_rows * tile_cols
    tp = lax.axis_size("tp")
    flat_latent = latent.reshape(count, model_width)
    flat_cotangent = cotangent.reshape(count, model_width)
    gain = norm_gain.reshape(1, model_width)
    weight = qkv_weight.transpose(1, 0, 2)
    shape = pltpu.VMEM
    heads = head_cols // HEAD_DIM
    row = lax.axis_index("row").astype(jnp.int32).reshape(1)
    col = lax.axis_index("col").astype(jnp.int32).reshape(1)
    place = lax.axis_index("tp").astype(jnp.int32).reshape(1)
    extent = (lax.axis_size("row"), lax.axis_size("col"))
    edge = shape((KV_ROWS + QG_ROWS, 2 * head_cols), bf16)
    kv, qg, far, near = pl.pallas_call(
        project_kernel,
        out_shape=[shape((count, 2 * head_cols), bf16)] * 2 + [edge] * 2,
        in_specs=[SMEM, SMEM, SMEM, FAR_SPACE, HERE, FAR_SPACE, FAR_SPACE, FAR_SPACE],
        out_specs=[HERE] * 4,
        scratch_shapes=[
            pltpu.VMEM(flat_latent.shape, bf16),
            pltpu.VMEM(weight.shape, bf16),
            pltpu.VMEM(out_weight.shape, bf16),
            pltpu.VMEM(flat_cotangent.shape, bf16),
            pltpu.SemaphoreType.DMA((6,)),
        ],
        compiler_params=PARAMS,
        name="project",
    )(
        row,
        col,
        place,
        in_hbm(flat_latent),
        in_hbm(gain),
        in_hbm(weight),
        in_hbm(out_weight),
        in_hbm(flat_cotangent),
    )
    far = paired(far, "row", 1)
    near = paired(near, "row", 0)
    side = shape((KV_EDGE + QG_EDGE, 2 * head_cols), bf16)
    gather, spread = gathers(), spreads()
    tall = [shape((lines * SIDE, 2 * head_cols), bf16) for lines in (WIDE, TALL)]
    leftward, rightward, kv_tall, qg_tall = near_call(
        edges_kernel,
        "edges",
        [side] * 2 + tall,
        [SMEM] + [VMEM] * 5,
        row, kv, qg, far, near, gather,
    )
    from_left = moved(rightward, "col", 1)
    from_right = moved(leftward, "col", -1)
    bias = shape((2 * KV_EDGE, 2 * QG_EDGE * heads), f32)
    query_mid, pair_mid, left_bias, right_bias = near_call(
        functools.partial(middle_kernel, extent),
        "middle",
        [shape((count, head_cols), bf16), shape((count, 2 * head_cols), f32), bias, bias],
        [SMEM] * 2 + [VMEM] * 5,
        row, col, kv_tall, qg_tall, places(heads), gather, spread,
    )
    partial = near_call(
        sides_kernel,
        "sides",
        shape((count, model_width), bf16),
        [VMEM] * 10,
        leftward, from_left, rightward, from_right, query_mid, pair_mid, left_bias, right_bias,
        spread, weight,
    )
    own = count // tp
    received = lax.all_to_all(partial.reshape(tp, own, model_width), "tp", 0, 0)
    result = near_call(
        finish_kernel,
        "finish",
        jax.ShapeDtypeStruct((own, model_width), f32),
        [SMEM] + [VMEM] * 4,
        place, received, flat_latent, gain, flat_cotangent,
    )
    return result.reshape(own // tile_cols, tile_cols, model_width)


def solution(mesh):
    placed = (P("row", "col", None), P(), P(None, None, "tp"), P("tp", None), P("row", "col", None))
    return jax.shard_map(
        per_device,
        mesh=mesh,
        in_specs=placed,
        out_specs=P(("row", "tp"), "col", None),
        check_vma=False,
    )
```

time: 64.8 us -> 56.8 us (0.88)
  the two profiles are of different devices: /device:TPU:195 before, /device:TPU:250 now
where the time goes in v3:
time: 56.8 us; the launch traced here: 56.6 us
  blocking collectives  16.8 us (30%)
  starting transfers between devices  15.2 us (27%)
  waiting for transfers between devices  14.6 us (26%)
  Pallas kernels  9.81 us (17%)
    all_to_all x1, blocking collectives, per_device(): received = lax.all_to_all(partial.reshape(tp, own, model_width), 'tp', 0, 0)  16.8 us
    ppermute x2, starting transfers between devices, paired(): return lax.ppermute(block, axis, route)  7.8 us
    ppermute x2, waiting for transfers between devices, paired(): return lax.ppermute(block, axis, route)  7.47 us
    ppermute x2, starting transfers between devices, moved(): return lax.ppermute(block, axis, route)  7.41 us
    ppermute x2, waiting for transfers between devices, moved(): return lax.ppermute(block, axis, route)  7.1 us
    pallas_call x4, Pallas kernels, near_call(): pl.pallas_call(kernel, out_shape=outs, in_specs=places, out_specs=jax.tre...  6.7 us
    pallas_call x1, Pallas kernels, per_device(): pl.pallas_call(project_kernel, out_shape=[shape((count, 2 * head_cols), b...  3.12 us
  transfers between devices with their start and end apart: 4, of which 3 were waited for; matrix products, arithmetic and copies ran while one was open for 0% of the time, Pallas kernels for 5%

profile of v3, /device:TPU:250, one launch (start us, length us, event | category | flops | bytes accessed | tf_op | source)
XLA Modules:
  0.0 56.6 jit_solution(8590501720044159788)
XLA Ops:
  0.0 0.0 copy-start.1
  0.0 3.1 %project.1 = (bf16[256,512]{1,0:T(8,128)(2,1)S(1)}, bf16[256,512]{1,0:T(8,128)(2,1)S(1)}, bf16[144,512]{1,0:T(8,128)(2,1)S(1)}, bf16[144,512]{1,0:T(8,128)(2,1)S(1)}) custom-call(s32[1]{0:T(128)} %bitcast.1.row, s32[1]{0:T(128)} %bitcast.2.col, s32[1]{0:T(128)} %bitcast.place, bf16[256,1024]{1,0:T(8,128)(2,1)} %bitcast.12, f32[1,1024]{1,0:T(1,128)} %bitcast.16, ...), custom_call_target="tpu_custom_call" | custom-call | tf_op jit(solution)/shard_map/project/pallas_call | solution.py:351
  3.1 0.0 copy-start.4
  3.1 0.0 copy-start.5
  3.2 4.3 %collective-permute-start = (bf16[144,512]{1,0:T(8,128)(2,1)S(1)}, bf16[144,512]{1,0:T(8,128)(2,1)S(1)}, u32[]{:S(2)}, u32[]{:S(2)}) collective-permute-start(bf16[144,512]{1,0:T(8,128)(2,1)S(1)} %get-tuple-element.19), channel_id=1, source_target_pairs={{32,64},{64,32},{96,128},{128,96},{160,192},{192,160},{224,256},{2... | collective-permute-start | bytes 442376 | tf_op jit(solution)/shard_map/ppermute | solution.py:326
  7.5 3.5 %collective-permute-start.1 = (bf16[144,512]{1,0:T(8,128)(2,1)S(1)}, bf16[144,512]{1,0:T(8,128)(2,1)S(1)}, u32[]{:S(2)}, u32[]{:S(2)}) collective-permute-start(bf16[144,512]{1,0:T(8,128)(2,1)S(1)} %get-tuple-element.20), channel_id=1, source_target_pairs={{0,32},{32,0},{64,96},{96,64},{128,160},{160,128},{192,224},{224,1... | collective-permute-start | bytes 442376 | tf_op jit(solution)/shard_map/ppermute | solution.py:326
  11.0 7.5 %collective-permute-done.far = bf16[144,512]{1,0:T(8,128)(2,1)S(1)} collective-permute-done((bf16[144,512]{1,0:T(8,128)(2,1)S(1)}, bf16[144,512]{1,0:T(8,128)(2,1)S(1)}, u32[]{:S(2)}, u32[]{:S(2)}) %collective-permute-start) | collective-permute-done | bytes 147488 | tf_op jit(solution)/shard_map/ppermute | solution.py:326
  18.4 0.0 collective-permute-done.1.near
  18.4 0.0 copy-done.1
  18.4 0.0 copy-start
  18.4 0.5 edges.1
  18.9 5.5 %collective-permute-start.2 = (bf16[256,512]{1,0:T(8,128)(2,1)S(1)}, bf16[256,512]{1,0:T(8,128)(2,1)S(1)}, u32[]{:S(2)}, u32[]{:S(2)}) collective-permute-start(bf16[256,512]{1,0:T(8,128)(2,1)S(1)} %get-tuple-element.22.rightward), channel_id=1, source_target_pairs={{0,4},{4,8},{8,12},{12,16},{16,20},{20,24},{24,28},{1,5},{5,9},{9,... | collective-permute-start | bytes 786440 | tf_op jit(solution)/shard_map/ppermute | solution.py:332
  24.4 1.9 %collective-permute-start.3 = (bf16[256,512]{1,0:T(8,128)(2,1)S(1)}, bf16[256,512]{1,0:T(8,128)(2,1)S(1)}, u32[]{:S(2)}, u32[]{:S(2)}) collective-permute-start(bf16[256,512]{1,0:T(8,128)(2,1)S(1)} %get-tuple-element.21.leftward), channel_id=1, source_target_pairs={{4,0},{8,4},{12,8},{16,12},{20,16},{24,20},{28,24},{5,1},{9,5},{13... | collective-permute-start | bytes 786440 | tf_op jit(solution)/shard_map/ppermute | solution.py:332
  26.3 0.0 copy-done.4
  26.3 0.0 copy-done.5
  26.4 2.7 %middle.1 = (bf16[256,256]{1,0:T(8,128)(2,1)S(1)}, f32[256,512]{1,0:T(8,128)S(1)}, f32[352,640]{1,0:T(8,128)S(1)}, f32[352,640]{1,0:T(8,128)S(1)}) custom-call(s32[1]{0:T(128)} %bitcast.1.row, s32[1]{0:T(128)} %bitcast.2.col, bf16[448,512]{1,0:T(8,128)(2,1)S(1)} %get-tuple-element.23.kv, bf16[352,512]{1,0:T(8,128)(2,1)S(1)} %get-tuple-element.24.qg, ...), custom_call_target="tpu_custom_call" | custom-call | tf_op jit(solution)/shard_map/middle/pallas_call | solution.py:45
  29.1 1.8 %collective-permute-done.2.from_left = bf16[256,512]{1,0:T(8,128)(2,1)S(1)} collective-permute-done((bf16[256,512]{1,0:T(8,128)(2,1)S(1)}, bf16[256,512]{1,0:T(8,128)(2,1)S(1)}, u32[]{:S(2)}, u32[]{:S(2)}) %collective-permute-start.2) | collective-permute-done | bytes 262176 | tf_op jit(solution)/shard_map/ppermute | solution.py:332
  30.8 5.3 %collective-permute-done.3.from_right = bf16[256,512]{1,0:T(8,128)(2,1)S(1)} collective-permute-done((bf16[256,512]{1,0:T(8,128)(2,1)S(1)}, bf16[256,512]{1,0:T(8,128)(2,1)S(1)}, u32[]{:S(2)}, u32[]{:S(2)}) %collective-permute-start.3) | collective-permute-done | bytes 262176 | tf_op jit(solution)/shard_map/ppermute | solution.py:332
  36.2 0.0 copy-done
  36.2 0.0 copy-start.2
  36.2 0.0 copy-start.3
  36.2 0.0 copy-start.6
  36.2 2.6 %sides.1 = bf16[256,1024]{1,0:T(8,128)(2,1)S(1)} custom-call(bf16[256,512]{1,0:T(8,128)(2,1)S(1)} %get-tuple-element.21.leftward, bf16[256,512]{1,0:T(8,128)(2,1)S(1)} %collective-permute-done.2.from_left, bf16[256,512]{1,0:T(8,128)(2,1)S(1)} %get-tuple-element.22.rightward, bf16[256,512]{1,0:T(8,128)(2,1)S(1)} %collective-permute-done.3.from_right, ...), custom_call_target="tpu_custom_call" | custom-call | tf_op jit(solution)/shard_map/sides/pallas_call | solution.py:45
  38.8 16.8 %all_to_all.5.received = bf16[4,64,1024]{2,1,0:T(8,128)(2,1)S(1)} all-to-all(bf16[4,64,1024]{2,1,0:T(8,128)(2,1)S(1)} %bitcast.11), channel_id=1, replica_groups=mesh['row'=16,'col'=8,'tp'=4] {'tp'}, dimensions={0} | all-to-all | bytes 1048576 | tf_op jit(solution)/shard_map/all_to_all | solution.py:406
  55.6 0.0 copy-done.2
  55.6 0.0 copy-done.3
  55.6 0.0 copy-done.6
  55.6 0.9 %finish.1 = f32[64,1024]{1,0:T(8,128)} custom-call(s32[1]{0:T(128)} %bitcast.place, bf16[4,64,1024]{2,1,0:T(8,128)(2,1)S(1)} %all_to_all.5.received, bf16[256,1024]{1,0:T(8,128)(2,1)S(1)} %bitcast.13, f32[1,1024]{1,0:T(1,128)S(1)} %bitcast.17, bf16[256,1024]{1,0:T(8,128)(2,1)S(1)} %bitcast.15), custom_call_target="tpu_custom_call" | custom-call | tf_op jit(solution)/shard_map/finish/pallas_call | solution.py:45
Async XLA Ops:
  0.0 18.4 %copy-start.1 = (bf16[736,448]{1,0:T(8,128)(2,1)S(1)}, bf16[736,448]{1,0:T(8,128)(2,1)}, u32[]{:S(2)}) copy-start(bf16[736,448]{1,0:T(8,128)(2,1)} %constant.21.clone.gather) | copy-start | bytes 1978372
  3.1 23.2 %copy-start.4 = (bf16[768,256]{1,0:T(8,128)(2,1)S(1)}, bf16[768,256]{1,0:T(8,128)(2,1)}, u32[]{:S(2)}) copy-start(bf16[768,256]{1,0:T(8,128)(2,1)} %constant.22.clone.spread) | copy-start | bytes 1179652
  3.1 23.2 %copy-start.5 = (f32[8,2176]{1,0:T(8,128)S(1)}, f32[8,2176]{1,0:T(8,128)}, u32[]{:S(2)}) copy-start(f32[8,2176]{1,0:T(8,128)} %constant.23.clone.points) | copy-start | bytes 208900
  3.2 15.3 %collective-permute-start = (bf16[144,512]{1,0:T(8,128)(2,1)S(1)}, bf16[144,512]{1,0:T(8,128)(2,1)S(1)}, u32[]{:S(2)}, u32[]{:S(2)}) collective-permute-start(bf16[144,512]{1,0:T(8,128)(2,1)S(1)} %get-tuple-element.19), channel_id=1, source_target_pairs={{32,64},{64,32},{96,128},{128,96},{160,192},{192,160},{224,256},{2... | collective-permute-start | bytes 442376 | tf_op jit(solution)/shard_map/ppermute | solution.py:326
  7.5 11.0 %collective-permute-start.1 = (bf16[144,512]{1,0:T(8,128)(2,1)S(1)}, bf16[144,512]{1,0:T(8,128)(2,1)S(1)}, u32[]{:S(2)}, u32[]{:S(2)}) collective-permute-start(bf16[144,512]{1,0:T(8,128)(2,1)S(1)} %get-tuple-element.20), channel_id=1, source_target_pairs={{0,32},{32,0},{64,96},{96,64},{128,160},{160,128},{192,224},{224,1... | collective-permute-start | bytes 442376 | tf_op jit(solution)/shard_map/ppermute | solution.py:326
  18.4 17.7 %copy-start = (bf16[1024,3,256]{2,0,1:T(8,128)(2,1)S(1)}, bf16[1024,3,256]{2,0,1:T(8,128)(2,1)}, u32[]{:S(2)}) copy-start(bf16[1024,3,256]{2,0,1:T(8,128)(2,1)} %param.10) | copy-start | bytes 4718596
  18.9 11.9 %collective-permute-start.2 = (bf16[256,512]{1,0:T(8,128)(2,1)S(1)}, bf16[256,512]{1,0:T(8,128)(2,1)S(1)}, u32[]{:S(2)}, u32[]{:S(2)}) collective-permute-start(bf16[256,512]{1,0:T(8,128)(2,1)S(1)} %get-tuple-element.22.rightward), channel_id=1, source_target_pairs={{0,4},{4,8},{8,12},{12,16},{16,20},{20,24},{24,28},{1,5},{5,9},{9,... | collective-permute-start | bytes 786440 | tf_op jit(solution)/shard_map/ppermute | solution.py:332
  24.4 11.8 %collective-permute-start.3 = (bf16[256,512]{1,0:T(8,128)(2,1)S(1)}, bf16[256,512]{1,0:T(8,128)(2,1)S(1)}, u32[]{:S(2)}, u32[]{:S(2)}) collective-permute-start(bf16[256,512]{1,0:T(8,128)(2,1)S(1)} %get-tuple-element.21.leftward), channel_id=1, source_target_pairs={{4,0},{8,4},{12,8},{16,12},{20,16},{24,20},{28,24},{5,1},{9,5},{13... | collective-permute-start | bytes 786440 | tf_op jit(solution)/shard_map/ppermute | solution.py:332
  36.2 19.5 %copy-start.2 = (bf16[16,16,1024]{2,1,0:T(8,128)(2,1)S(1)}, bf16[16,16,1024]{2,1,0:T(8,128)(2,1)}, u32[]{:S(2)}) copy-start(bf16[16,16,1024]{2,1,0:T(8,128)(2,1)} %param.8) | copy-start | bytes 1572868
  36.2 19.5 %copy-start.3 = (bf16[16,16,1024]{2,1,0:T(8,128)(2,1)S(1)}, bf16[16,16,1024]{2,1,0:T(8,128)(2,1)}, u32[]{:S(2)}) copy-start(bf16[16,16,1024]{2,1,0:T(8,128)(2,1)} %param.12) | copy-start | bytes 1572868
  36.2 19.5 %copy-start.6 = (f32[1024]{0:T(1024)S(1)}, f32[1024]{0:T(1024)}, u32[]{:S(2)}) copy-start(f32[1024]{0:T(1024)} %param.9) | copy-start | bytes 12292

commit v4 on v3

--- a/solution.py
+++ b/solution.py
@@ -36,7 +36,7 @@
     return pltpu.with_memory_space_constraint(block, pltpu.HBM)
 
 
-def near_call(kernel, name, outs, specs, *operands):
+def near_call(kernel, name, outs, specs, *operands, scratch=()):
     fixed = [
         pltpu.with_memory_space_constraint(x, pltpu.VMEM) if spec is VMEM else x
         for x, spec in zip(operands, specs)
@@ -47,6 +47,7 @@
         out_shape=outs,
         in_specs=places,
         out_specs=jax.tree.map(lambda _: VMEM, outs),
+        scratch_shapes=scratch,
         compiler_params=PARAMS,
         name=name,
     )(*fixed)
@@ -80,10 +81,12 @@
     "qg_edges": (2 * KV_EDGE, 2 * QG_EDGE, TALL * SIDE),
     "middle": (2 * KV_EDGE + 2 * QG_EDGE, MID_QUERIES, TALL * SIDE),
 }
+HALF = SIDE // 2
+HALF_TOKENS = SIDE * HALF
 SPREADS = {
-    "middle": (0, SIDE * SIDE, MID_QUERIES),
-    "keys": (SIDE * SIDE, SIDE * SIDE, 2 * OWN_EDGE),
-    "queries": (2 * SIDE * SIDE, SIDE * SIDE, 2 * QG_EDGE),
+    "middle": (0, 2 * HALF_TOKENS, MID_QUERIES),
+    "keys": ((2 * HALF_TOKENS, HALF_TOKENS, OWN_EDGE), (3 * HALF_TOKENS, HALF_TOKENS, OWN_EDGE)),
+    "queries": ((4 * HALF_TOKENS, HALF_TOKENS, QG_EDGE), (5 * HALF_TOKENS, HALF_TOKENS, QG_EDGE)),
 }
 
 
@@ -107,20 +110,21 @@
 def spreads():
     pairs = []
 
-    def add(name, halo, column, target):
+    def add(first, halo, column, target):
         token = target - halo * SIDE
         if 0 <= token < SIDE * SIDE:
-            pairs.append((SPREADS[name][0] + token, column))
+            y, x = divmod(token, SIDE)
+            pairs.append((first + x // HALF * HALF_TOKENS + y * HALF + x % HALF, column))
 
     for t, f in strip_pairs(TALL, MIDDLE, RADIUS):
-        add("middle", RADIUS, t, f)
-    for part, first in enumerate((0, SIDE - REACH)):
+        add(0, RADIUS, t, f)
+    for first in (0, SIDE - REACH):
         for t, f in strip_pairs(WIDE, REACH, first):
-            add("keys", REACH, part * OWN_EDGE + t - OWN_FROM, f)
-    for part, first in enumerate((0, SIDE - RADIUS)):
+            add(SPREADS["keys"][0][0], REACH, t - OWN_FROM, f)
+    for first in (0, SIDE - RADIUS):
         for t, f in strip_pairs(TALL, RADIUS, first):
-            add("queries", RADIUS, part * QG_EDGE + t, f)
-    return table(3 * SIDE * SIDE, SIDE * SIDE, pairs)
+            add(SPREADS["queries"][0][0], RADIUS, t, f)
+    return table(6 * HALF_TOKENS, SIDE * SIDE, pairs)
 
 
 def coords(lines, reach, first, count, total, pad):
@@ -251,9 +255,10 @@
 
 
 def middle_kernel(
-    extent, row, col, kv, qg, points, gather, spread, query_out, pair_out, left_bias, right_bias
+    extent, row, col, kv, qg, points, gather, spread, left_query, right_query, left_pair,
+    right_pair, left_bias, right_bias
 ):
-    count, width = query_out.shape
+    count, width = 2 * left_query.shape[0], left_query.shape[1]
     spot = (row[0], col[0])
     keys, queries = points[...].T, points[2:4]
     qg_mid = nn(part_of(gather, GATHERS["middle"]), qg[...]).astype(bf16)
@@ -262,9 +267,14 @@
     own = slice(KV_ROWS, KV_ROWS + count)
     query_grad, key_grad, value_grad = attention(bias, kv[...], qg_mid, own)
     scattered = nn(part_of(spread, SPREADS["middle"]), query_grad.astype(bf16))
-    query_out[...] = scattered.astype(bf16)
-    pair_out[:, :width] = key_grad
-    pair_out[:, width:] = value_grad
+    key_grad = key_grad.reshape(SIDE, 2, HALF, width)
+    value_grad = value_grad.reshape(SIDE, 2, HALF, width)
+    for half, (query_out, pair_out) in enumerate(
+        ((left_query, left_pair), (right_query, right_pair))
+    ):
+        query_out[...] = scattered[half * HALF_TOKENS : (half + 1) * HALF_TOKENS].astype(bf16)
+        pair_out[:, :width] = key_grad[:, half].reshape(HALF_TOKENS, width)
+        pair_out[:, width:] = value_grad[:, half].reshape(HALF_TOKENS, width)
     for side in (left_bias, right_bias):
         last_key, last_query = first_key + side.shape[0], first_query + side.shape[1]
         side[...] = window_bias(
@@ -273,49 +283,62 @@
         first_key, first_query = last_key, last_query
 
 
-def sides_kernel(
-    leftward, from_left, rightward, from_right, query_mid, pair_mid, left_bias, right_bias,
-    spread, weight, partial
+def side_kernel(
+    half, place, mine, theirs, query_mid, pair_mid, bias, spread, weight, sent, kept, stacked
 ):
     width = query_mid.shape[1]
     own = slice(OWN_FROM, OWN_FROM + OWN_EDGE)
-    query_parts, pair_parts = [], []
-    for mine, theirs, bias in (
-        (leftward, from_left, left_bias),
-        (rightward, from_right, right_bias),
-    ):
-        kv = jnp.concatenate([mine[:KV_EDGE], theirs[:KV_EDGE]], axis=0)
-        qg = jnp.concatenate([mine[KV_EDGE:], theirs[KV_EDGE:]], axis=0)
-        query_grad, key_grad, value_grad = attention(bias[...], kv, qg, own)
-        query_parts.append(query_grad[:QG_EDGE])
-        pair_parts.append(jnp.concatenate([key_grad, value_grad], axis=1))
-    query_side = jnp.concatenate(query_parts, axis=0).astype(bf16)
-    pair_side = jnp.concatenate(pair_parts, axis=0)
+    kv = jnp.concatenate([mine[:KV_EDGE], theirs[:KV_EDGE]], axis=0)
+    qg = jnp.concatenate([mine[KV_EDGE:], theirs[KV_EDGE:]], axis=0)
+    query_grad, key_grad, value_grad = attention(bias[...], kv, qg, own)
+    query_side = query_grad[:QG_EDGE].astype(bf16)
+    pair_side = jnp.concatenate([key_grad, value_grad], axis=1)
     coarse = pair_side.astype(bf16)
     fine = (pair_side - coarse.astype(f32)).astype(bf16)
-    key_spread, query_spread = (part_of(spread, SPREADS[name]) for name in ("keys", "queries"))
+    key_spread = part_of(spread, SPREADS["keys"][half])
+    query_spread = part_of(spread, SPREADS["queries"][half])
     pair = pair_mid[...] + (nn(key_spread, coarse) + nn(key_spread, fine))
     query_grad = query_mid[...].astype(f32) + nn(query_spread, query_side)
-    pair = pair.astype(bf16)
-    total = nt(query_grad.astype(bf16), weight[0])
-    total += nt(pair[:, :width], weight[1])
-    total += nt(pair[:, width:], weight[2])
-    partial[...] = total.astype(bf16)
-
-
-def finish_kernel(place, received, latent, gain, cotangent, result):
-    count = received.shape[1]
+    stacked[:, :width] = query_grad.astype(bf16)
+    stacked[:, width:] = pair.astype(bf16)
+    block = sent.shape[0] // 2
+    ordered = []
+    for other in (1, 3, 0, 2):
+        first = pl.multiple_of(jnp.bitwise_xor(place[0], other) * block, block)
+        ordered.append(stacked[pl.ds(first, block), :])
+    ordered = jnp.concatenate(ordered, axis=0)
+    total = nt(ordered[:, :width], weight[0])
+    total += nt(ordered[:, width : 2 * width], weight[1])
+    total += nt(ordered[:, 2 * width :], weight[2])
+    sent[...] = total[: 2 * block].astype(bf16)
+    kept[...] = total[2 * block :]
+
+
+def fold_kernel(kept, received, sent, still):
+    block = sent.shape[0]
+    still[...] = kept[:block] + received[:block].astype(f32)
+    sent[...] = (kept[block:] + received[block:].astype(f32)).astype(bf16)
+
+
+def finish_kernel(
+    place, left_kept, left_received, right_kept, right_received, latent, gain, cotangent, result
+):
+    lines, cols, width = result.shape
+    count = lines * cols
     first = pl.multiple_of(place[0] * count, count)
     tokens = latent[pl.ds(first, count), :].astype(f32)
     upstream = cotangent[pl.ds(first, count), :].astype(f32)
-    summed = received[0].astype(f32)
-    for part in range(1, received.shape[0]):
-        summed += received[part].astype(f32)
+    halves = [
+        (kept[...] + received[...].astype(f32)).reshape(lines, cols // 2, width)
+        for kept, received in ((left_kept, left_received), (right_kept, right_received))
+    ]
+    summed = jnp.concatenate(halves, axis=1).reshape(count, width)
     inverse = lax.rsqrt(jnp.mean(tokens * tokens, axis=-1, keepdims=True) + 1e-06)
     unit = tokens * inverse
     scaled = summed * gain[...]
     stat = jnp.mean(scaled * unit, axis=-1, keepdims=True)
-    result[...] = upstream + inverse * (scaled - unit * stat)
+    outcome = upstream + inverse * (scaled - unit * stat)
+    result[...] = outcome.reshape(lines, cols, width)
 
 
 def paired(block, axis, first):
@@ -387,31 +410,46 @@
     from_left = moved(rightward, "col", 1)
     from_right = moved(leftward, "col", -1)
     bias = shape((2 * KV_EDGE, 2 * QG_EDGE * heads), f32)
-    query_mid, pair_mid, left_bias, right_bias = near_call(
+    queries, pairs = shape((count // 2, head_cols), bf16), shape((count // 2, 2 * head_cols), f32)
+    left_query, right_query, left_pair, right_pair, left_bias, right_bias = near_call(
         functools.partial(middle_kernel, extent),
         "middle",
-        [shape((count, head_cols), bf16), shape((count, 2 * head_cols), f32), bias, bias],
+        [queries, queries, pairs, pairs, bias, bias],
         [SMEM] * 2 + [VMEM] * 5,
         row, col, kv_tall, qg_tall, places(heads), gather, spread,
     )
-    partial = near_call(
-        sides_kernel,
-        "sides",
-        shape((count, model_width), bf16),
-        [VMEM] * 10,
-        leftward, from_left, rightward, from_right, query_mid, pair_mid, left_bias, right_bias,
-        spread, weight,
-    )
     own = count // tp
-    received = lax.all_to_all(partial.reshape(tp, own, model_width), "tp", 0, 0)
-    result = near_call(
+    reduced = []
+    for half, operands in enumerate(
+        (
+            (leftward, from_left, left_query, left_pair, left_bias),
+            (rightward, from_right, right_query, right_pair, right_bias),
+        )
+    ):
+        sent, kept = near_call(
+            functools.partial(side_kernel, half),
+            ("left_side", "right_side")[half],
+            [shape((own, model_width), bf16), shape((own, model_width), f32)],
+            [SMEM] + [VMEM] * 7,
+            place, *operands, spread, weight,
+            scratch=[pltpu.VMEM((count // 2, 3 * head_cols), bf16)],
+        )
+        received = lax.ppermute(sent, "tp", [(i, i ^ 1) for i in range(tp)])
+        sent, kept = near_call(
+            fold_kernel,
+            ("left_fold", "right_fold")[half],
+            [shape((own // 2, model_width), bf16), shape((own // 2, model_width), f32)],
+            [VMEM] * 2,
+            kept, received,
+        )
+        reduced += [kept, lax.ppermute(sent, "tp", [(i, i ^ 2) for i in range(tp)])]
+    return near_call(
         finish_kernel,
         "finish",
-        jax.ShapeDtypeStruct((own, model_width), f32),
-        [SMEM] + [VMEM] * 4,
-        place, received, flat_latent, gain, flat_cotangent,
+        jax.ShapeDtypeStruct((own // tile_cols, tile_cols, model_width), f32),
+        [SMEM] + [VMEM] * 7,
+        place, *reduced, flat_latent, gain, flat_cotangent,
     )
-    return result.reshape(own // tile_cols, tile_cols, model_width)
 
 
 def solution(mesh):

time: 56.8 us -> 54.8 us (0.965)
  blocking collectives: 16.8 us -> 0 us
  starting transfers between devices: 15.2 us -> 27.5 us
  Pallas kernels: 9.81 us -> 11.1 us
  waiting for transfers between devices: 14.6 us -> 15.6 us
    all_to_all x1 -> x0, blocking collectives: 16.8 us -> none  [per_device(): received = lax.all_to_all(partial.reshape(tp, own, model_width), 'tp', 0, 0)]
    ppermute x0 -> x4, starting transfers between devices: none -> 12.3 us  [the longest x2 6.43 us: per_device(): reduced += [kept, lax.ppermute(sent, 'tp', [(i, i ^ 2) for i in range(tp)])]]
    ppermute x0 -> x4, waiting for transfers between devices: none -> 5.75 us  [the longest x2 5.04 us: per_device(): reduced += [kept, lax.ppermute(sent, 'tp', [(i, i ^ 2) for i in range(tp)])]]
    ppermute x2, waiting for transfers between devices: 7.1 us -> 2.42 us  [moved(): return lax.ppermute(block, axis, route)]
    pallas_call x4 -> x7, Pallas kernels: 6.7 us -> 8 us  [near_call(): pl.pallas_call(kernel, out_shape=outs, in_specs=places, out_specs=jax.tre...]
  transfers between devices with their start and end apart: 4 -> 8, of which waited for: 3 -> 4; matrix products, arithmetic and copies ran while one was open for 0% -> 0% of each run, Pallas kernels for 5% -> 12%
where the time goes in v4:
time: 54.8 us; the launch traced here: 54.5 us
  starting transfers between devices  27.5 us (50%)
  waiting for transfers between devices  15.6 us (28%)
  Pallas kernels  11.1 us (20%)
    pallas_call x7, Pallas kernels, near_call(): pl.pallas_call(kernel, out_shape=outs, in_specs=places, out_specs=jax.tre...  8 us
    ppermute x2, starting transfers between devices, paired(): return lax.ppermute(block, axis, route)  7.8 us
    ppermute x2, waiting for transfers between devices, paired(): return lax.ppermute(block, axis, route)  7.47 us
    ppermute x2, starting transfers between devices, moved(): return lax.ppermute(block, axis, route)  7.41 us
    ppermute x2, starting transfers between devices, per_device(): reduced += [kept, lax.ppermute(sent, 'tp', [(i, i ^ 2) for i in range(tp)])]  6.43 us
    ppermute x2, starting transfers between devices, per_device(): received = lax.ppermute(sent, 'tp', [(i, i ^ 1) for i in range(tp)])  5.84 us
    ppermute x2, waiting for transfers between devices, per_device(): reduced += [kept, lax.ppermute(sent, 'tp', [(i, i ^ 2) for i in range(tp)])]  5.04 us
    pallas_call x1, Pallas kernels, per_device(): pl.pallas_call(project_kernel, out_shape=[shape((count, 2 * head_cols), b...  3.12 us
  transfers between devices with their start and end apart: 8, of which 4 were waited for; matrix products, arithmetic and copies ran while one was open for 0% of the time, Pallas kernels for 12%

profile of v4, /device:TPU:250, one launch (start us, length us, event | category | flops | bytes accessed | tf_op | source)
XLA Modules:
  0.0 54.5 jit_solution(7048820591965376537)
XLA Ops:
  0.0 0.0 copy-start.2
  0.0 3.1 %project.1 = (bf16[256,512]{1,0:T(8,128)(2,1)S(1)}, bf16[256,512]{1,0:T(8,128)(2,1)S(1)}, bf16[144,512]{1,0:T(8,128)(2,1)S(1)}, bf16[144,512]{1,0:T(8,128)(2,1)S(1)}) custom-call(s32[1]{0:T(128)} %bitcast.1.row, s32[1]{0:T(128)} %bitcast.2.col, s32[1]{0:T(128)} %bitcast.place, bf16[256,1024]{1,0:T(8,128)(2,1)} %bitcast.10, f32[1,1024]{1,0:T(1,128)} %bitcast.14, ...), custom_call_target="tpu_custom_call" | custom-call | tf_op jit(solution)/shard_map/project/pallas_call | solution.py:374
  3.1 0.0 copy-start.1
  3.1 0.0 copy-start.5
  3.2 4.3 %collective-permute-start = (bf16[144,512]{1,0:T(8,128)(2,1)S(1)}, bf16[144,512]{1,0:T(8,128)(2,1)S(1)}, u32[]{:S(2)}, u32[]{:S(2)}) collective-permute-start(bf16[144,512]{1,0:T(8,128)(2,1)S(1)} %get-tuple-element.29), channel_id=1, source_target_pairs={{32,64},{64,32},{96,128},{128,96},{160,192},{192,160},{224,256},{2... | collective-permute-start | bytes 442376 | tf_op jit(solution)/shard_map/ppermute | solution.py:349
  7.5 3.5 %collective-permute-start.1 = (bf16[144,512]{1,0:T(8,128)(2,1)S(1)}, bf16[144,512]{1,0:T(8,128)(2,1)S(1)}, u32[]{:S(2)}, u32[]{:S(2)}) collective-permute-start(bf16[144,512]{1,0:T(8,128)(2,1)S(1)} %get-tuple-element.30), channel_id=1, source_target_pairs={{0,32},{32,0},{64,96},{96,64},{128,160},{160,128},{192,224},{224,1... | collective-permute-start | bytes 442376 | tf_op jit(solution)/shard_map/ppermute | solution.py:349
  11.0 7.5 %collective-permute-done.far = bf16[144,512]{1,0:T(8,128)(2,1)S(1)} collective-permute-done((bf16[144,512]{1,0:T(8,128)(2,1)S(1)}, bf16[144,512]{1,0:T(8,128)(2,1)S(1)}, u32[]{:S(2)}, u32[]{:S(2)}) %collective-permute-start) | collective-permute-done | bytes 147488 | tf_op jit(solution)/shard_map/ppermute | solution.py:349
  18.4 0.0 collective-permute-done.1.near
  18.4 0.0 copy-done.2
  18.4 0.0 copy-start
  18.4 0.5 edges.1
  18.9 1.9 %collective-permute-start.5 = (bf16[256,512]{1,0:T(8,128)(2,1)S(1)}, bf16[256,512]{1,0:T(8,128)(2,1)S(1)}, u32[]{:S(2)}, u32[]{:S(2)}) collective-permute-start(bf16[256,512]{1,0:T(8,128)(2,1)S(1)} %get-tuple-element.31.mine), channel_id=1, source_target_pairs={{4,0},{8,4},{12,8},{16,12},{20,16},{24,20},{28,24},{5,1},{9,5},{13... | collective-permute-start | bytes 786440 | tf_op jit(solution)/shard_map/ppermute | solution.py:355
  20.8 5.5 %collective-permute-start.2 = (bf16[256,512]{1,0:T(8,128)(2,1)S(1)}, bf16[256,512]{1,0:T(8,128)(2,1)S(1)}, u32[]{:S(2)}, u32[]{:S(2)}) collective-permute-start(bf16[256,512]{1,0:T(8,128)(2,1)S(1)} %get-tuple-element.32.mine), channel_id=1, source_target_pairs={{0,4},{4,8},{8,12},{12,16},{16,20},{20,24},{24,28},{1,5},{5,9},{9,... | collective-permute-start | bytes 786440 | tf_op jit(solution)/shard_map/ppermute | solution.py:355
  26.3 0.0 copy-done.1
  26.3 0.0 copy-done.5
  26.4 2.7 %middle.1 = (bf16[128,256]{1,0:T(8,128)(2,1)S(1)}, bf16[128,256]{1,0:T(8,128)(2,1)S(1)}, f32[128,512]{1,0:T(8,128)S(1)}, f32[128,512]{1,0:T(8,128)S(1)}, f32[352,640]{1,0:T(8,128)S(1)}, /*index=5*/f32[352,640]{1,0:T(8,128)S(1)}) custom-call(s32[1]{0:T(128)} %bitcast.1.row, s32[1]{0:T(128)} %bitcast.2.col, bf16[448,512]{1,0:T(8,128)(2,1)S(1)} %get-tuple-element.33.kv, ...), custom_call_target="tpu_custom_call" | custom-call | tf_op jit(solution)/shard_map/middle/pallas_call | solution.py:45
  29.1 2.4 %collective-permute-done.5.theirs = bf16[256,512]{1,0:T(8,128)(2,1)S(1)} collective-permute-done((bf16[256,512]{1,0:T(8,128)(2,1)S(1)}, bf16[256,512]{1,0:T(8,128)(2,1)S(1)}, u32[]{:S(2)}, u32[]{:S(2)}) %collective-permute-start.5) | collective-permute-done | bytes 262176 | tf_op jit(solution)/shard_map/ppermute | solution.py:355
  31.5 0.0 copy-done
  31.5 1.9 %right_side.1 = (bf16[64,1024]{1,0:T(8,128)(2,1)S(1)}, f32[64,1024]{1,0:T(8,128)S(1)}) custom-call(s32[1]{0:T(128)} %bitcast.place, bf16[256,512]{1,0:T(8,128)(2,1)S(1)} %get-tuple-element.32.mine, bf16[256,512]{1,0:T(8,128)(2,1)S(1)} %collective-permute-done.5.theirs, bf16[128,256]{1,0:T(8,128)(2,1)S(1)} %get-tuple-element.42.query_mid, ...), custom_call_target="tpu_custom_call" | custom-call | tf_op jit(solution)/shard_map/right_side/pallas_call | solution.py:45
  33.4 3.2 %collective-permute-start.6 = (bf16[64,1024]{1,0:T(8,128)(2,1)S(1)}, bf16[64,1024]{1,0:T(8,128)(2,1)S(1)}, u32[]{:S(2)}, u32[]{:S(2)}) collective-permute-start(bf16[64,1024]{1,0:T(8,128)(2,1)S(1)} %get-tuple-element.46), channel_id=1, source_target_pairs={{0,1},{1,0},{2,3},{3,2},{4,5},{5,4},{6,7},{7,6},{8,9},{9,8},{10,11... | collective-permute-start | bytes 393224 | tf_op jit(solution)/shard_map/ppermute | solution.py:437
  36.6 0.0 collective-permute-done.2.theirs
  36.7 0.0 copy-start.3
  36.7 0.0 copy-start.4
  36.7 0.0 copy-start.6
  36.7 1.9 %left_side.1 = (bf16[64,1024]{1,0:T(8,128)(2,1)S(1)}, f32[64,1024]{1,0:T(8,128)S(1)}) custom-call(s32[1]{0:T(128)} %bitcast.place, bf16[256,512]{1,0:T(8,128)(2,1)S(1)} %get-tuple-element.31.mine, bf16[256,512]{1,0:T(8,128)(2,1)S(1)} %collective-permute-done.2.theirs, bf16[128,256]{1,0:T(8,128)(2,1)S(1)} %get-tuple-element.35.query_mid, ...), custom_call_target="tpu_custom_call" | custom-call | tf_op jit(solution)/shard_map/left_side/pallas_call | solution.py:45
  38.6 2.6 %collective-permute-start.3 = (bf16[64,1024]{1,0:T(8,128)(2,1)S(1)}, bf16[64,1024]{1,0:T(8,128)(2,1)S(1)}, u32[]{:S(2)}, u32[]{:S(2)}) collective-permute-start(bf16[64,1024]{1,0:T(8,128)(2,1)S(1)} %get-tuple-element.39), channel_id=1, source_target_pairs={{0,1},{1,0},{2,3},{3,2},{4,5},{5,4},{6,7},{7,6},{8,9},{9,8},{10,11... | collective-permute-start | bytes 393224 | tf_op jit(solution)/shard_map/ppermute | solution.py:437
  41.2 0.0 collective-permute-done.6.received
  41.3 3.7 %collective-permute-start.7 = (bf16[32,1024]{1,0:T(8,128)(2,1)S(1)}, bf16[32,1024]{1,0:T(8,128)(2,1)S(1)}, u32[]{:S(2)}, u32[]{:S(2)}) collective-permute-start(bf16[32,1024]{1,0:T(8,128)(2,1)S(1)} %get-tuple-element.48), channel_id=1, source_target_pairs={{0,2},{1,3},{2,0},{3,1},{4,6},{5,7},{6,4},{7,5},{8,10},{9,11},{10,... | collective-permute-start | bytes 196616 | tf_op jit(solution)/shard_map/ppermute | solution.py:445
  45.0 0.7 %collective-permute-done.3.received = bf16[64,1024]{1,0:T(8,128)(2,1)S(1)} collective-permute-done((bf16[64,1024]{1,0:T(8,128)(2,1)S(1)}, bf16[64,1024]{1,0:T(8,128)(2,1)S(1)}, u32[]{:S(2)}, u32[]{:S(2)}) %collective-permute-start.3) | collective-permute-done | bytes 131104 | tf_op jit(solution)/shard_map/ppermute | solution.py:437
  45.8 2.7 %collective-permute-start.4 = (bf16[32,1024]{1,0:T(8,128)(2,1)S(1)}, bf16[32,1024]{1,0:T(8,128)(2,1)S(1)}, u32[]{:S(2)}, u32[]{:S(2)}) collective-permute-start(bf16[32,1024]{1,0:T(8,128)(2,1)S(1)} %get-tuple-element.41), channel_id=1, source_target_pairs={{0,2},{1,3},{2,0},{3,1},{4,6},{5,7},{6,4},{7,5},{8,10},{9,11},{10,... | collective-permute-start | bytes 196616 | tf_op jit(solution)/shard_map/ppermute | solution.py:445
  48.5 0.0 collective-permute-done.7.right_received
  48.5 5.0 %collective-permute-done.4.left_received = bf16[32,1024]{1,0:T(8,128)(2,1)S(1)} collective-permute-done((bf16[32,1024]{1,0:T(8,128)(2,1)S(1)}, bf16[32,1024]{1,0:T(8,128)(2,1)S(1)}, u32[]{:S(2)}, u32[]{:S(2)}) %collective-permute-start.4) | collective-permute-done | bytes 65568 | tf_op jit(solution)/shard_map/ppermute | solution.py:445
  53.5 0.0 copy-done.3
  53.5 0.0 copy-done.4
  53.5 0.0 copy-done.6
  53.5 0.9 %finish.1 = f32[4,16,1024]{2,1,0:T(8,128)} custom-call(s32[1]{0:T(128)} %bitcast.place, f32[32,1024]{1,0:T(8,128)S(1)} %get-tuple-element.40.left_kept, bf16[32,1024]{1,0:T(8,128)(2,1)S(1)} %collective-permute-done.4.left_received, f32[32,1024]{1,0:T(8,128)S(1)} %get-tuple-element.47.right_kept, bf16[32,1024]{1,0:T(8,128)(2,1)S(1)} %collective-permute-done.7.right_received, ...), custom_call_target="tpu_custom_call" | custom-call | tf_op jit(solution)/shard_map/finish/pallas_call | solution.py:45
  (2 shorter events, 0.1 us)
Async XLA Ops:
  0.0 18.4 %copy-start.2 = (bf16[736,448]{1,0:T(8,128)(2,1)S(1)}, bf16[736,448]{1,0:T(8,128)(2,1)}, u32[]{:S(2)}) copy-start(bf16[736,448]{1,0:T(8,128)(2,1)} %constant.21.clone.gather) | copy-start | bytes 1978372
  3.1 23.2 %copy-start.1 = (bf16[768,256]{1,0:T(8,128)(2,1)S(1)}, bf16[768,256]{1,0:T(8,128)(2,1)}, u32[]{:S(2)}) copy-start(bf16[768,256]{1,0:T(8,128)(2,1)} %constant.22.clone.spread) | copy-start | bytes 1179652
  3.1 23.2 %copy-start.5 = (f32[8,2176]{1,0:T(8,128)S(1)}, f32[8,2176]{1,0:T(8,128)}, u32[]{:S(2)}) copy-start(f32[8,2176]{1,0:T(8,128)} %constant.23.clone.points) | copy-start | bytes 208900
  3.2 15.3 %collective-permute-start = (bf16[144,512]{1,0:T(8,128)(2,1)S(1)}, bf16[144,512]{1,0:T(8,128)(2,1)S(1)}, u32[]{:S(2)}, u32[]{:S(2)}) collective-permute-start(bf16[144,512]{1,0:T(8,128)(2,1)S(1)} %get-tuple-element.29), channel_id=1, source_target_pairs={{32,64},{64,32},{96,128},{128,96},{160,192},{192,160},{224,256},{2... | collective-permute-start | bytes 442376 | tf_op jit(solution)/shard_map/ppermute | solution.py:349
  7.5 11.0 %collective-permute-start.1 = (bf16[144,512]{1,0:T(8,128)(2,1)S(1)}, bf16[144,512]{1,0:T(8,128)(2,1)S(1)}, u32[]{:S(2)}, u32[]{:S(2)}) collective-permute-start(bf16[144,512]{1,0:T(8,128)(2,1)S(1)} %get-tuple-element.30), channel_id=1, source_target_pairs={{0,32},{32,0},{64,96},{96,64},{128,160},{160,128},{192,224},{224,1... | collective-permute-start | bytes 442376 | tf_op jit(solution)/shard_map/ppermute | solution.py:349
  18.4 13.1 %copy-start = (bf16[1024,3,256]{2,0,1:T(8,128)(2,1)S(1)}, bf16[1024,3,256]{2,0,1:T(8,128)(2,1)}, u32[]{:S(2)}) copy-start(bf16[1024,3,256]{2,0,1:T(8,128)(2,1)} %param.10) | copy-start | bytes 4718596
  18.9 12.6 %collective-permute-start.5 = (bf16[256,512]{1,0:T(8,128)(2,1)S(1)}, bf16[256,512]{1,0:T(8,128)(2,1)S(1)}, u32[]{:S(2)}, u32[]{:S(2)}) collective-permute-start(bf16[256,512]{1,0:T(8,128)(2,1)S(1)} %get-tuple-element.31.mine), channel_id=1, source_target_pairs={{4,0},{8,4},{12,8},{16,12},{20,16},{24,20},{28,24},{5,1},{9,5},{13... | collective-permute-start | bytes 786440 | tf_op jit(solution)/shard_map/ppermute | solution.py:355
  20.8 15.8 %collective-permute-start.2 = (bf16[256,512]{1,0:T(8,128)(2,1)S(1)}, bf16[256,512]{1,0:T(8,128)(2,1)S(1)}, u32[]{:S(2)}, u32[]{:S(2)}) collective-permute-start(bf16[256,512]{1,0:T(8,128)(2,1)S(1)} %get-tuple-element.32.mine), channel_id=1, source_target_pairs={{0,4},{4,8},{8,12},{12,16},{16,20},{20,24},{24,28},{1,5},{5,9},{9,... | collective-permute-start | bytes 786440 | tf_op jit(solution)/shard_map/ppermute | solution.py:355
  33.4 7.8 %collective-permute-start.6 = (bf16[64,1024]{1,0:T(8,128)(2,1)S(1)}, bf16[64,1024]{1,0:T(8,128)(2,1)S(1)}, u32[]{:S(2)}, u32[]{:S(2)}) collective-permute-start(bf16[64,1024]{1,0:T(8,128)(2,1)S(1)} %get-tuple-element.46), channel_id=1, source_target_pairs={{0,1},{1,0},{2,3},{3,2},{4,5},{5,4},{6,7},{7,6},{8,9},{9,8},{10,11... | collective-permute-start | bytes 393224 | tf_op jit(solution)/shard_map/ppermute | solution.py:437
  36.7 16.9 %copy-start.3 = (bf16[16,16,1024]{2,1,0:T(8,128)(2,1)S(1)}, bf16[16,16,1024]{2,1,0:T(8,128)(2,1)}, u32[]{:S(2)}) copy-start(bf16[16,16,1024]{2,1,0:T(8,128)(2,1)} %param.8) | copy-start | bytes 1572868
  36.7 16.9 %copy-start.4 = (bf16[16,16,1024]{2,1,0:T(8,128)(2,1)S(1)}, bf16[16,16,1024]{2,1,0:T(8,128)(2,1)}, u32[]{:S(2)}) copy-start(bf16[16,16,1024]{2,1,0:T(8,128)(2,1)} %param.12) | copy-start | bytes 1572868
  36.7 16.9 %copy-start.6 = (f32[1024]{0:T(1024)S(1)}, f32[1024]{0:T(1024)}, u32[]{:S(2)}) copy-start(f32[1024]{0:T(1024)} %param.9) | copy-start | bytes 12292
  38.6 7.1 %collective-permute-start.3 = (bf16[64,1024]{1,0:T(8,128)(2,1)S(1)}, bf16[64,1024]{1,0:T(8,128)(2,1)S(1)}, u32[]{:S(2)}, u32[]{:S(2)}) collective-permute-start(bf16[64,1024]{1,0:T(8,128)(2,1)S(1)} %get-tuple-element.39), channel_id=1, source_target_pairs={{0,1},{1,0},{2,3},{3,2},{4,5},{5,4},{6,7},{7,6},{8,9},{9,8},{10,11... | collective-permute-start | bytes 393224 | tf_op jit(solution)/shard_map/ppermute | solution.py:437
  41.3 7.2 %collective-permute-start.7 = (bf16[32,1024]{1,0:T(8,128)(2,1)S(1)}, bf16[32,1024]{1,0:T(8,128)(2,1)S(1)}, u32[]{:S(2)}, u32[]{:S(2)}) collective-permute-start(bf16[32,1024]{1,0:T(8,128)(2,1)S(1)} %get-tuple-element.48), channel_id=1, source_target_pairs={{0,2},{1,3},{2,0},{3,1},{4,6},{5,7},{6,4},{7,5},{8,10},{9,11},{10,... | collective-permute-start | bytes 196616 | tf_op jit(solution)/shard_map/ppermute | solution.py:445
  45.8 7.8 %collective-permute-start.4 = (bf16[32,1024]{1,0:T(8,128)(2,1)S(1)}, bf16[32,1024]{1,0:T(8,128)(2,1)S(1)}, u32[]{:S(2)}, u32[]{:S(2)}) collective-permute-start(bf16[32,1024]{1,0:T(8,128)(2,1)S(1)} %get-tuple-element.41), channel_id=1, source_target_pairs={{0,2},{1,3},{2,0},{3,1},{4,6},{5,7},{6,4},{7,5},{8,10},{9,11},{10,... | collective-permute-start | bytes 196616 | tf_op jit(solution)/shard_map/ppermute | solution.py:445

commit v5 on v4

--- a/solution.py
+++ b/solution.py
@@ -23,6 +23,7 @@
 OWN_FROM = 32
 OWN_EDGE = 112
 FAR = 1000.0
+FOLD_COST = 40_000_000_000
 bf16 = jnp.bfloat16
 f32 = jnp.float32
 VMEM = pl.BlockSpec(memory_space=pltpu.VMEM)
@@ -36,7 +37,7 @@
     return pltpu.with_memory_space_constraint(block, pltpu.HBM)
 
 
-def near_call(kernel, name, outs, specs, *operands, scratch=()):
+def near_call(kernel, name, outs, specs, *operands, scratch=(), cost=None):
     fixed = [
         pltpu.with_memory_space_constraint(x, pltpu.VMEM) if spec is VMEM else x
         for x, spec in zip(operands, specs)
@@ -48,6 +49,7 @@
         in_specs=places,
         out_specs=jax.tree.map(lambda _: VMEM, outs),
         scratch_shapes=scratch,
+        cost_estimate=cost,
         compiler_params=PARAMS,
         name=name,
     )(*fixed)
@@ -283,10 +285,7 @@
         first_key, first_query = last_key, last_query
 
 
-def side_kernel(
-    half, place, mine, theirs, query_mid, pair_mid, bias, spread, weight, sent, kept, stacked
-):
-    width = query_mid.shape[1]
+def side_grads(half, mine, theirs, query_mid, pair_mid, bias, spread):
     own = slice(OWN_FROM, OWN_FROM + OWN_EDGE)
     kv = jnp.concatenate([mine[:KV_EDGE], theirs[:KV_EDGE]], axis=0)
     qg = jnp.concatenate([mine[KV_EDGE:], theirs[KV_EDGE:]], axis=0)
@@ -299,17 +298,35 @@
     query_spread = part_of(spread, SPREADS["queries"][half])
     pair = pair_mid[...] + (nn(key_spread, coarse) + nn(key_spread, fine))
     query_grad = query_mid[...].astype(f32) + nn(query_spread, query_side)
-    stacked[:, :width] = query_grad.astype(bf16)
-    stacked[:, width:] = pair.astype(bf16)
+    return query_grad.astype(bf16), pair.astype(bf16)
+
+
+def back_projected(stacked, weight):
+    width = weight.shape[2]
+    total = nt(stacked[:, :width], weight[0])
+    total += nt(stacked[:, width : 2 * width], weight[1])
+    total += nt(stacked[:, 2 * width :], weight[2])
+    return total
+
+
+def left_kernel(after, mine, theirs, query_mid, pair_mid, bias, spread, weight, partial):
+    grads = side_grads(0, mine, theirs, query_mid, pair_mid, bias, spread)
+    partial[...] = back_projected(jnp.concatenate(grads, axis=1), weight).astype(bf16)
+
+
+def right_kernel(
+    place, mine, theirs, query_mid, pair_mid, bias, spread, weight, sent, kept, stacked
+):
+    width = query_mid.shape[1]
+    query_grad, pair = side_grads(1, mine, theirs, query_mid, pair_mid, bias, spread)
+    stacked[:, :width] = query_grad
+    stacked[:, width:] = pair
     block = sent.shape[0] // 2
     ordered = []
     for other in (1, 3, 0, 2):
         first = pl.multiple_of(jnp.bitwise_xor(place[0], other) * block, block)
         ordered.append(stacked[pl.ds(first, block), :])
-    ordered = jnp.concatenate(ordered, axis=0)
-    total = nt(ordered[:, :width], weight[0])
-    total += nt(ordered[:, width : 2 * width], weight[1])
-    total += nt(ordered[:, 2 * width :], weight[2])
+    total = back_projected(jnp.concatenate(ordered, axis=0), weight)
     sent[...] = total[: 2 * block].astype(bf16)
     kept[...] = total[2 * block :]
 
@@ -321,17 +338,18 @@
 
 
 def finish_kernel(
-    place, left_kept, left_received, right_kept, right_received, latent, gain, cotangent, result
+    place, left_received, right_kept, right_received, latent, gain, cotangent, result
 ):
     lines, cols, width = result.shape
     count = lines * cols
     first = pl.multiple_of(place[0] * count, count)
     tokens = latent[pl.ds(first, count), :].astype(f32)
     upstream = cotangent[pl.ds(first, count), :].astype(f32)
-    halves = [
-        (kept[...] + received[...].astype(f32)).reshape(lines, cols // 2, width)
-        for kept, received in ((left_kept, left_received), (right_kept, right_received))
-    ]
+    left = left_received[0].astype(f32)
+    for part in range(1, left_received.shape[0]):
+        left += left_received[part].astype(f32)
+    right = right_kept[...] + right_received[...].astype(f32)
+    halves = [half.reshape(lines, cols // 2, width) for half in (left, right)]
     summed = jnp.concatenate(halves, axis=1).reshape(count, width)
     inverse = lax.rsqrt(jnp.mean(tokens * tokens, axis=-1, keepdims=True) + 1e-06)
     unit = tokens * inverse
@@ -419,36 +437,38 @@
         row, col, kv_tall, qg_tall, places(heads), gather, spread,
     )
     own = count // tp
-    reduced = []
-    for half, operands in enumerate(
-        (
-            (leftward, from_left, left_query, left_pair, left_bias),
-            (rightward, from_right, right_query, right_pair, right_bias),
-        )
-    ):
-        sent, kept = near_call(
-            functools.partial(side_kernel, half),
-            ("left_side", "right_side")[half],
-            [shape((own, model_width), bf16), shape((own, model_width), f32)],
-            [SMEM] + [VMEM] * 7,
-            place, *operands, spread, weight,
-            scratch=[pltpu.VMEM((count // 2, 3 * head_cols), bf16)],
-        )
-        received = lax.ppermute(sent, "tp", [(i, i ^ 1) for i in range(tp)])
-        sent, kept = near_call(
-            fold_kernel,
-            ("left_fold", "right_fold")[half],
-            [shape((own // 2, model_width), bf16), shape((own // 2, model_width), f32)],
-            [VMEM] * 2,
-            kept, received,
-        )
-        reduced += [kept, lax.ppermute(sent, "tp", [(i, i ^ 2) for i in range(tp)])]
+    sent, kept = near_call(
+        right_kernel,
+        "right_side",
+        [shape((own, model_width), bf16), shape((own, model_width), f32)],
+        [SMEM] + [VMEM] * 7,
+        place, rightward, from_right, right_query, right_pair, right_bias, spread, weight,
+        scratch=[pltpu.VMEM((count // 2, 3 * head_cols), bf16)],
+    )
+    received = lax.ppermute(sent, "tp", [(i, i ^ 1) for i in range(tp)])
+    partial = near_call(
+        left_kernel,
+        "left_side",
+        shape((count // 2, model_width), bf16),
+        [VMEM] * 8,
+        kept, leftward, from_left, left_query, left_pair, left_bias, spread, weight,
+    )
+    sent, right_kept = near_call(
+        fold_kernel,
+        "right_fold",
+        [shape((own // 2, model_width), bf16), shape((own // 2, model_width), f32)],
+        [VMEM] * 2,
+        kept, received,
+        cost=pl.CostEstimate(flops=FOLD_COST, transcendentals=0, bytes_accessed=1 << 18),
+    )
+    right_received = lax.ppermute(sent, "tp", [(i, i ^ 2) for i in range(tp)])
+    left_received = lax.all_to_all(partial.reshape(tp, own // 2, model_width), "tp", 0, 0)
     return near_call(
         finish_kernel,
         "finish",
         jax.ShapeDtypeStruct((own // tile_cols, tile_cols, model_width), f32),
-        [SMEM] + [VMEM] * 7,
-        place, *reduced, flat_latent, gain, flat_cotangent,
+        [SMEM] + [VMEM] * 6,
+        place, left_received, right_kept, right_received, flat_latent, gain, flat_cotangent,
     )
 
 

time: 54.8 us -> 55.4 us (1.011)
  the two profiles are of different devices: /device:TPU:250 before, /device:TPU:252 now
where the time goes in v5:
time: 55.4 us; the launch traced here: 55 us
  starting transfers between devices  27.8 us (50%)
  waiting for transfers between devices  15.4 us (28%)
  Pallas kernels  11.6 us (21%)
    pallas_call x6, Pallas kernels, near_call(): pl.pallas_call(kernel, out_shape=outs, in_specs=places, out_specs=jax.tre...  8.47 us
    ppermute x2, waiting for transfers between devices, paired(): return lax.ppermute(block, axis, route)  7.76 us
    ppermute x2, starting transfers between devices, paired(): return lax.ppermute(block, axis, route)  7.51 us
    ppermute x2, starting transfers between devices, moved(): return lax.ppermute(block, axis, route)  7.41 us
    ppermute x1, waiting for transfers between devices, per_device(): right_received = lax.ppermute(sent, 'tp', [(i, i ^ 2) for i in range(tp)])  6.94 us
    all_to_all x1, starting transfers between devices, per_device(): lax.all_to_all(partial.reshape(tp, own // 2, model_width), 'tp', 0, 0)  5.58 us
    ppermute x1, starting transfers between devices, per_device(): received = lax.ppermute(sent, 'tp', [(i, i ^ 1) for i in range(tp)])  4.73 us
    pallas_call x1, Pallas kernels, per_device(): pl.pallas_call(project_kernel, out_shape=[shape((count, 2 * head_cols), b...  3.12 us
  transfers between devices with their start and end apart: 7, of which 3 were waited for; matrix products, arithmetic and copies ran while one was open for 0% of the time, Pallas kernels for 13%

profile of v5, /device:TPU:252, one launch (start us, length us, event | category | flops | bytes accessed | tf_op | source)
XLA Modules:
  0.0 55.0 jit_solution(16397117812462438835)
XLA Ops:
  0.0 0.0 copy-start.2
  0.0 3.1 %project.1 = (bf16[256,512]{1,0:T(8,128)(2,1)S(1)}, bf16[256,512]{1,0:T(8,128)(2,1)S(1)}, bf16[144,512]{1,0:T(8,128)(2,1)S(1)}, bf16[144,512]{1,0:T(8,128)(2,1)S(1)}) custom-call(s32[1]{0:T(128)} %bitcast.1.row, s32[1]{0:T(128)} %bitcast.2.col, s32[1]{0:T(128)} %bitcast.place, bf16[256,1024]{1,0:T(8,128)(2,1)} %bitcast.11, f32[1,1024]{1,0:T(1,128)} %bitcast.15, ...), custom_call_target="tpu_custom_call" | custom-call | tf_op jit(solution)/shard_map/project/pallas_call | solution.py:392
  3.1 0.0 copy-start.1
  3.1 0.0 copy-start.5
  3.2 4.3 %collective-permute-start = (bf16[144,512]{1,0:T(8,128)(2,1)S(1)}, bf16[144,512]{1,0:T(8,128)(2,1)S(1)}, u32[]{:S(2)}, u32[]{:S(2)}) collective-permute-start(bf16[144,512]{1,0:T(8,128)(2,1)S(1)} %get-tuple-element.25), channel_id=1, source_target_pairs={{32,64},{64,32},{96,128},{128,96},{160,192},{192,160},{224,256},{2... | collective-permute-start | bytes 442376 | tf_op jit(solution)/shard_map/ppermute | solution.py:367
  7.4 3.2 %collective-permute-start.1 = (bf16[144,512]{1,0:T(8,128)(2,1)S(1)}, bf16[144,512]{1,0:T(8,128)(2,1)S(1)}, u32[]{:S(2)}, u32[]{:S(2)}) collective-permute-start(bf16[144,512]{1,0:T(8,128)(2,1)S(1)} %get-tuple-element.26), channel_id=1, source_target_pairs={{0,32},{32,0},{64,96},{96,64},{128,160},{160,128},{192,224},{224,1... | collective-permute-start | bytes 442376 | tf_op jit(solution)/shard_map/ppermute | solution.py:367
  10.7 7.8 %collective-permute-done.far = bf16[144,512]{1,0:T(8,128)(2,1)S(1)} collective-permute-done((bf16[144,512]{1,0:T(8,128)(2,1)S(1)}, bf16[144,512]{1,0:T(8,128)(2,1)S(1)}, u32[]{:S(2)}, u32[]{:S(2)}) %collective-permute-start) | collective-permute-done | bytes 147488 | tf_op jit(solution)/shard_map/ppermute | solution.py:367
  18.4 0.0 collective-permute-done.1.near
  18.4 0.0 copy-done.2
  18.4 0.0 copy-start
  18.4 0.5 edges.1
  18.9 1.9 %collective-permute-start.2 = (bf16[256,512]{1,0:T(8,128)(2,1)S(1)}, bf16[256,512]{1,0:T(8,128)(2,1)S(1)}, u32[]{:S(2)}, u32[]{:S(2)}) collective-permute-start(bf16[256,512]{1,0:T(8,128)(2,1)S(1)} %get-tuple-element.28.mine), channel_id=1, source_target_pairs={{4,0},{8,4},{12,8},{16,12},{20,16},{24,20},{28,24},{5,1},{9,5},{13... | collective-permute-start | bytes 786440 | tf_op jit(solution)/shard_map/ppermute | solution.py:373
  20.8 5.5 %collective-permute-start.3 = (bf16[256,512]{1,0:T(8,128)(2,1)S(1)}, bf16[256,512]{1,0:T(8,128)(2,1)S(1)}, u32[]{:S(2)}, u32[]{:S(2)}) collective-permute-start(bf16[256,512]{1,0:T(8,128)(2,1)S(1)} %get-tuple-element.27.mine), channel_id=1, source_target_pairs={{0,4},{4,8},{8,12},{12,16},{16,20},{20,24},{24,28},{1,5},{5,9},{9,... | collective-permute-start | bytes 786440 | tf_op jit(solution)/shard_map/ppermute | solution.py:373
  26.3 0.0 copy-done.1
  26.3 0.0 copy-done.5
  26.3 2.7 %middle.1 = (bf16[128,256]{1,0:T(8,128)(2,1)S(1)}, bf16[128,256]{1,0:T(8,128)(2,1)S(1)}, f32[128,512]{1,0:T(8,128)S(1)}, f32[128,512]{1,0:T(8,128)S(1)}, f32[352,640]{1,0:T(8,128)S(1)}, /*index=5*/f32[352,640]{1,0:T(8,128)S(1)}) custom-call(s32[1]{0:T(128)} %bitcast.1.row, s32[1]{0:T(128)} %bitcast.2.col, bf16[448,512]{1,0:T(8,128)(2,1)S(1)} %get-tuple-element.29.kv, ...), custom_call_target="tpu_custom_call" | custom-call | tf_op jit(solution)/shard_map/middle/pallas_call | solution.py:46
  29.1 0.7 %collective-permute-done.2.theirs = bf16[256,512]{1,0:T(8,128)(2,1)S(1)} collective-permute-done((bf16[256,512]{1,0:T(8,128)(2,1)S(1)}, bf16[256,512]{1,0:T(8,128)(2,1)S(1)}, u32[]{:S(2)}, u32[]{:S(2)}) %collective-permute-start.2) | collective-permute-done | bytes 262176 | tf_op jit(solution)/shard_map/ppermute | solution.py:373
  29.8 0.0 copy-done
  29.8 1.9 %right_side.1 = (bf16[64,1024]{1,0:T(8,128)(2,1)S(1)}, f32[64,1024]{1,0:T(8,128)S(1)}) custom-call(s32[1]{0:T(128)} %bitcast.place, bf16[256,512]{1,0:T(8,128)(2,1)S(1)} %get-tuple-element.27.mine, bf16[256,512]{1,0:T(8,128)(2,1)S(1)} %collective-permute-done.2.theirs, bf16[128,256]{1,0:T(8,128)(2,1)S(1)} %get-tuple-element.31.query_mid, ...), custom_call_target="tpu_custom_call" | custom-call | tf_op jit(solution)/shard_map/right_side/pallas_call | solution.py:46
  31.7 4.7 %collective-permute-start.4 = (bf16[64,1024]{1,0:T(8,128)(2,1)S(1)}, bf16[64,1024]{1,0:T(8,128)(2,1)S(1)}, u32[]{:S(2)}, u32[]{:S(2)}) collective-permute-start(bf16[64,1024]{1,0:T(8,128)(2,1)S(1)} %get-tuple-element.38), channel_id=1, source_target_pairs={{0,1},{1,0},{2,3},{3,2},{4,5},{5,4},{6,7},{7,6},{8,9},{9,8},{10,11... | collective-permute-start | bytes 393224 | tf_op jit(solution)/shard_map/ppermute | solution.py:448
  36.4 0.0 collective-permute-done.3.theirs
  36.5 2.4 %left_side.1 = bf16[128,1024]{1,0:T(8,128)(2,1)} custom-call(f32[64,1024]{1,0:T(8,128)S(1)} %get-tuple-element.34.after.kept, bf16[256,512]{1,0:T(8,128)(2,1)S(1)} %get-tuple-element.28.mine, bf16[256,512]{1,0:T(8,128)(2,1)S(1)} %collective-permute-done.3.theirs, bf16[128,256]{1,0:T(8,128)(2,1)S(1)} %get-tuple-element.35.query_mid, ...), custom_call_target="tpu_custom_call" | custom-call | tf_op jit(solution)/shard_map/left_side/pallas_call | solution.py:46
  38.9 5.6 %all-to-all-start = ((bf16[4,32,1024]{2,1,0:T(8,128)(2,1)}), bf16[4,32,1024]{2,1,0:T(8,128)(2,1)S(1)}, u32[]{:S(2)}, u32[]{:S(2)}) async-start(bf16[4,32,1024]{2,1,0:T(8,128)(2,1)} %bitcast.7), calls=%async_computation | async-start | bytes 524288 | tf_op jit(solution)/shard_map/all_to_all | solution.py:465
  44.5 0.0 copy-start.3
  44.5 0.0 copy-start.4
  44.5 0.0 copy-start.6
  44.5 0.0 collective-permute-done.4.received
  44.5 2.6 %collective-permute-start.5 = (bf16[32,1024]{1,0:T(8,128)(2,1)S(1)}, bf16[32,1024]{1,0:T(8,128)(2,1)S(1)}, u32[]{:S(2)}, u32[]{:S(2)}) collective-permute-start(bf16[32,1024]{1,0:T(8,128)(2,1)S(1)} %get-tuple-element.40), channel_id=1, source_target_pairs={{0,2},{1,3},{2,0},{3,1},{4,6},{5,7},{6,4},{7,5},{8,10},{9,11},{10,... | collective-permute-start | bytes 196616 | tf_op jit(solution)/shard_map/ppermute | solution.py:464
  47.1 6.9 %collective-permute-done.5.right_received = bf16[32,1024]{1,0:T(8,128)(2,1)S(1)} collective-permute-done((bf16[32,1024]{1,0:T(8,128)(2,1)S(1)}, bf16[32,1024]{1,0:T(8,128)(2,1)S(1)}, u32[]{:S(2)}, u32[]{:S(2)}) %collective-permute-start.5) | collective-permute-done | bytes 65568 | tf_op jit(solution)/shard_map/ppermute | solution.py:464
  54.1 0.0 all-to-all-done.left_received
  54.1 0.0 copy-done.3
  54.1 0.0 copy-done.4
  54.1 0.0 copy-done.6
  54.1 0.9 %finish.1 = f32[4,16,1024]{2,1,0:T(8,128)} custom-call(s32[1]{0:T(128)} %bitcast.place, bf16[4,32,1024]{2,1,0:T(8,128)(2,1)S(1)} %all-to-all-done.left_received, f32[32,1024]{1,0:T(8,128)S(1)} %get-tuple-element.39.right_kept, bf16[32,1024]{1,0:T(8,128)(2,1)S(1)} %collective-permute-done.5.right_received, bf16[256,1024]{1,0:T(8,128)(2,1)S(1)} %bitcast.12, ...), custom_call_target="tpu_custom_call" | custom-call | tf_op jit(solution)/shard_map/finish/pallas_call | solution.py:46
  (1 shorter events, 0.0 us)
Async XLA Ops:
  0.0 18.4 %copy-start.2 = (bf16[736,448]{1,0:T(8,128)(2,1)S(1)}, bf16[736,448]{1,0:T(8,128)(2,1)}, u32[]{:S(2)}) copy-start(bf16[736,448]{1,0:T(8,128)(2,1)} %constant.21.clone.gather) | copy-start | bytes 1978372
  3.1 23.2 %copy-start.1 = (bf16[768,256]{1,0:T(8,128)(2,1)S(1)}, bf16[768,256]{1,0:T(8,128)(2,1)}, u32[]{:S(2)}) copy-start(bf16[768,256]{1,0:T(8,128)(2,1)} %constant.22.clone.spread) | copy-start | bytes 1179652
  3.1 23.2 %copy-start.5 = (f32[8,2176]{1,0:T(8,128)S(1)}, f32[8,2176]{1,0:T(8,128)}, u32[]{:S(2)}) copy-start(f32[8,2176]{1,0:T(8,128)} %constant.23.clone.points) | copy-start | bytes 208900
  3.2 15.3 %collective-permute-start = (bf16[144,512]{1,0:T(8,128)(2,1)S(1)}, bf16[144,512]{1,0:T(8,128)(2,1)S(1)}, u32[]{:S(2)}, u32[]{:S(2)}) collective-permute-start(bf16[144,512]{1,0:T(8,128)(2,1)S(1)} %get-tuple-element.25), channel_id=1, source_target_pairs={{32,64},{64,32},{96,128},{128,96},{160,192},{192,160},{224,256},{2... | collective-permute-start | bytes 442376 | tf_op jit(solution)/shard_map/ppermute | solution.py:367
  7.4 11.0 %collective-permute-start.1 = (bf16[144,512]{1,0:T(8,128)(2,1)S(1)}, bf16[144,512]{1,0:T(8,128)(2,1)S(1)}, u32[]{:S(2)}, u32[]{:S(2)}) collective-permute-start(bf16[144,512]{1,0:T(8,128)(2,1)S(1)} %get-tuple-element.26), channel_id=1, source_target_pairs={{0,32},{32,0},{64,96},{96,64},{128,160},{160,128},{192,224},{224,1... | collective-permute-start | bytes 442376 | tf_op jit(solution)/shard_map/ppermute | solution.py:367
  18.4 11.4 %copy-start = (bf16[1024,3,256]{2,0,1:T(8,128)(2,1)S(1)}, bf16[1024,3,256]{2,0,1:T(8,128)(2,1)}, u32[]{:S(2)}) copy-start(bf16[1024,3,256]{2,0,1:T(8,128)(2,1)} %param.10) | copy-start | bytes 4718596
  18.9 10.9 %collective-permute-start.2 = (bf16[256,512]{1,0:T(8,128)(2,1)S(1)}, bf16[256,512]{1,0:T(8,128)(2,1)S(1)}, u32[]{:S(2)}, u32[]{:S(2)}) collective-permute-start(bf16[256,512]{1,0:T(8,128)(2,1)S(1)} %get-tuple-element.28.mine), channel_id=1, source_target_pairs={{4,0},{8,4},{12,8},{16,12},{20,16},{24,20},{28,24},{5,1},{9,5},{13... | collective-permute-start | bytes 786440 | tf_op jit(solution)/shard_map/ppermute | solution.py:373
  20.8 15.6 %collective-permute-start.3 = (bf16[256,512]{1,0:T(8,128)(2,1)S(1)}, bf16[256,512]{1,0:T(8,128)(2,1)S(1)}, u32[]{:S(2)}, u32[]{:S(2)}) collective-permute-start(bf16[256,512]{1,0:T(8,128)(2,1)S(1)} %get-tuple-element.27.mine), channel_id=1, source_target_pairs={{0,4},{4,8},{8,12},{12,16},{16,20},{20,24},{24,28},{1,5},{5,9},{9,... | collective-permute-start | bytes 786440 | tf_op jit(solution)/shard_map/ppermute | solution.py:373
  31.7 12.8 %collective-permute-start.4 = (bf16[64,1024]{1,0:T(8,128)(2,1)S(1)}, bf16[64,1024]{1,0:T(8,128)(2,1)S(1)}, u32[]{:S(2)}, u32[]{:S(2)}) collective-permute-start(bf16[64,1024]{1,0:T(8,128)(2,1)S(1)} %get-tuple-element.38), channel_id=1, source_target_pairs={{0,1},{1,0},{2,3},{3,2},{4,5},{5,4},{6,7},{7,6},{8,9},{9,8},{10,11... | collective-permute-start | bytes 393224 | tf_op jit(solution)/shard_map/ppermute | solution.py:448
  38.9 15.2 %all-to-all-start = ((bf16[4,32,1024]{2,1,0:T(8,128)(2,1)}), bf16[4,32,1024]{2,1,0:T(8,128)(2,1)S(1)}, u32[]{:S(2)}, u32[]{:S(2)}) async-start(bf16[4,32,1024]{2,1,0:T(8,128)(2,1)} %bitcast.7), calls=%async_computation | async-start | bytes 524288 | tf_op jit(solution)/shard_map/all_to_all | solution.py:465
  44.5 9.6 %copy-start.3 = (bf16[16,16,1024]{2,1,0:T(8,128)(2,1)S(1)}, bf16[16,16,1024]{2,1,0:T(8,128)(2,1)}, u32[]{:S(2)}) copy-start(bf16[16,16,1024]{2,1,0:T(8,128)(2,1)} %param.8) | copy-start | bytes 1572868
  44.5 9.6 %copy-start.4 = (bf16[16,16,1024]{2,1,0:T(8,128)(2,1)S(1)}, bf16[16,16,1024]{2,1,0:T(8,128)(2,1)}, u32[]{:S(2)}) copy-start(bf16[16,16,1024]{2,1,0:T(8,128)(2,1)} %param.12) | copy-start | bytes 1572868
  44.5 9.6 %copy-start.6 = (f32[1024]{0:T(1024)S(1)}, f32[1024]{0:T(1024)}, u32[]{:S(2)}) copy-start(f32[1024]{0:T(1024)} %param.9) | copy-start | bytes 12292
  44.5 9.6 %collective-permute-start.5 = (bf16[32,1024]{1,0:T(8,128)(2,1)S(1)}, bf16[32,1024]{1,0:T(8,128)(2,1)S(1)}, u32[]{:S(2)}, u32[]{:S(2)}) collective-permute-start(bf16[32,1024]{1,0:T(8,128)(2,1)S(1)} %get-tuple-element.40), channel_id=1, source_target_pairs={{0,2},{1,3},{2,0},{3,1},{4,6},{5,7},{6,4},{7,5},{8,10},{9,11},{10,... | collective-permute-start | bytes 196616 | tf_op jit(solution)/shard_map/ppermute | solution.py:464

commit v6 on v4

--- a/solution.py
+++ b/solution.py
@@ -18,8 +18,15 @@
 QG_ROWS = RADIUS * SIDE
 KV_EDGE = 176
 QG_EDGE = 80
-MIDDLE = SIDE - 2 * RADIUS
-MID_QUERIES = 224
+INNER = range(RADIUS, SIDE - RADIUS)
+ALONG = range(SIDE)
+TOP = range(-RADIUS, RADIUS)
+BOTTOM = range(SIDE - RADIUS, SIDE + RADIUS)
+TOP_KEYS = range(-REACH, REACH)
+BOTTOM_KEYS = range(SIDE - REACH, SIDE + REACH)
+CORE_QUERIES = 128
+RIM_QUERIES = 64
+RIM_KEYS = 2 * REACH * SIDE
 OWN_FROM = 32
 OWN_EDGE = 112
 FAR = 1000.0
@@ -76,23 +83,29 @@
     ]
 
 
+def cells(rows, cols):
+    return [(y, x) for y in rows for x in cols]
+
+
 GATHERS = {
     "kv_edges": (0, 2 * KV_EDGE, WIDE * SIDE),
     "qg_edges": (2 * KV_EDGE, 2 * QG_EDGE, TALL * SIDE),
-    "middle": (2 * KV_EDGE + 2 * QG_EDGE, MID_QUERIES, TALL * SIDE),
+    "core": (2 * KV_EDGE + 2 * QG_EDGE, CORE_QUERIES, SIDE * SIDE),
+    "rim": (2 * KV_EDGE + 2 * QG_EDGE + CORE_QUERIES, 2 * RIM_QUERIES, TALL * SIDE),
 }
 HALF = SIDE // 2
 HALF_TOKENS = SIDE * HALF
 SPREADS = {
-    "middle": (0, 2 * HALF_TOKENS, MID_QUERIES),
+    "core": (0, 2 * HALF_TOKENS, CORE_QUERIES),
+    "rim": (0, 2 * HALF_TOKENS, 2 * RIM_QUERIES, CORE_QUERIES),
     "keys": ((2 * HALF_TOKENS, HALF_TOKENS, OWN_EDGE), (3 * HALF_TOKENS, HALF_TOKENS, OWN_EDGE)),
     "queries": ((4 * HALF_TOKENS, HALF_TOKENS, QG_EDGE), (5 * HALF_TOKENS, HALF_TOKENS, QG_EDGE)),
 }
 
 
 def part_of(ref, spot):
-    first, rows, cols = spot
-    return ref[first : first + rows, :cols]
+    first, rows, cols, begin = (*spot, 0)[:4]
+    return ref[first : first + rows, begin : begin + cols]
 
 
 def gathers():
@@ -102,9 +115,13 @@
     begin = GATHERS["qg_edges"][0]
     for part, first in enumerate((0, SIDE - RADIUS)):
         pairs += [(begin + part * QG_EDGE + t, f) for t, f in strip_pairs(TALL, RADIUS, first)]
-    begin = GATHERS["middle"][0]
-    pairs += [(begin + t, f) for t, f in strip_pairs(TALL, MIDDLE, RADIUS)]
-    return table(begin + MID_QUERIES, WIDE * SIDE, pairs)
+    begin = GATHERS["core"][0]
+    pairs += [(begin + t, y * SIDE + x) for t, (y, x) in enumerate(cells(INNER, INNER))]
+    begin = GATHERS["rim"][0]
+    for part, rows in enumerate((TOP, BOTTOM)):
+        for t, (y, x) in enumerate(cells(rows, INNER)):
+            pairs.append((begin + part * RIM_QUERIES + t, (y + RADIUS) * SIDE + x))
+    return table(begin + 2 * RIM_QUERIES, WIDE * SIDE, pairs)
 
 
 def spreads():
@@ -116,8 +133,11 @@
             y, x = divmod(token, SIDE)
             pairs.append((first + x // HALF * HALF_TOKENS + y * HALF + x % HALF, column))
 
-    for t, f in strip_pairs(TALL, MIDDLE, RADIUS):
-        add(0, RADIUS, t, f)
+    for t, (y, x) in enumerate(cells(INNER, INNER)):
+        add(0, 0, t, y * SIDE + x)
+    for part, rows in enumerate((TOP, BOTTOM)):
+        for t, (y, x) in enumerate(cells(rows, INNER)):
+            add(0, 0, CORE_QUERIES + part * RIM_QUERIES + t, y * SIDE + x)
     for first in (0, SIDE - REACH):
         for t, f in strip_pairs(WIDE, REACH, first):
             add(SPREADS["keys"][0][0], REACH, t - OWN_FROM, f)
@@ -127,22 +147,25 @@
     return table(6 * HALF_TOKENS, SIDE * SIDE, pairs)
 
 
-def coords(lines, reach, first, count, total, pad):
-    ys = [float(line - reach) for line in range(lines) for _ in range(count)]
-    xs = [float(first + step) for _ in range(lines) for step in range(count)]
-    spare = [pad] * (total - len(ys))
-    return np.asarray([ys + spare, xs + spare], np.float32)
+def coords(rows, cols, total, pad):
+    spots = cells(rows, cols)
+    spots += [(pad, pad)] * (total - len(spots))
+    return np.asarray(spots, np.float32).T
 
 
 def places(heads):
-    keys = [coords(WIDE, REACH, 0, SIDE, WIDE * SIDE, FAR)]
-    queries = [np.tile(coords(TALL, RADIUS, RADIUS, MIDDLE, MID_QUERIES, -FAR), (1, heads))]
+    keys = [coords(ALONG, ALONG, SIDE * SIDE, FAR)]
+    queries = [np.tile(coords(INNER, INNER, CORE_QUERIES, -FAR), (1, heads))]
+    for rows, key_rows in ((TOP, TOP_KEYS), (BOTTOM, BOTTOM_KEYS)):
+        keys.append(coords(key_rows, ALONG, RIM_KEYS, FAR))
+        queries.append(np.tile(coords(rows, INNER, RIM_QUERIES, -FAR), (1, heads)))
+    wide, tall = range(-REACH, SIDE + REACH), range(-RADIUS, SIDE + RADIUS)
     for key_firsts, query_firsts in (
         ((0, -REACH), (0, -RADIUS)),
         ((SIDE - REACH, SIDE), (SIDE - RADIUS, SIDE)),
     ):
-        keys += [coords(WIDE, REACH, f, REACH, KV_EDGE, FAR) for f in key_firsts]
-        both = [coords(TALL, RADIUS, f, RADIUS, QG_EDGE, -FAR) for f in query_firsts]
+        keys += [coords(wide, range(f, f + REACH), KV_EDGE, FAR) for f in key_firsts]
+        both = [coords(tall, range(f, f + RADIUS), QG_EDGE, -FAR) for f in query_firsts]
         queries.append(np.tile(np.concatenate(both, axis=1), (1, heads)))
     keys, queries = np.concatenate(keys, axis=1), np.concatenate(queries, axis=1)
     joined = np.full((8, queries.shape[1]), FAR, np.float32)
@@ -202,7 +225,7 @@
     return kv_all, qg_all
 
 
-def edges_kernel(row, kv, qg, far, near, gather, left, right, kv_tall, qg_tall):
+def edges_kernel(row, kv, qg, far, near, gather, after, left, right, kv_tall, qg_tall):
     kv_all, qg_all = tall_blocks(row, kv, qg, far, near)
     kv_tall[...] = kv_all
     qg_tall[...] = qg_all
@@ -254,33 +277,56 @@
     return query_grad * (HEAD_DIM ** (-0.5)), key_grad, value_grad
 
 
-def middle_kernel(
-    extent, row, col, kv, qg, points, gather, spread, left_query, right_query, left_pair,
-    right_pair, left_bias, right_bias
+def core_kernel(
+    extent, row, col, kv, qg, points, gather, spread, query_out, pair_out, *biases
 ):
-    count, width = 2 * left_query.shape[0], left_query.shape[1]
+    count = kv.shape[0]
+    width = kv.shape[1] // 2
     spot = (row[0], col[0])
     keys, queries = points[...].T, points[2:4]
-    qg_mid = nn(part_of(gather, GATHERS["middle"]), qg[...]).astype(bf16)
-    first_key, first_query = kv.shape[0], MID_QUERIES * width // HEAD_DIM
-    bias = window_bias(spot, extent, keys[:first_key], queries[:, :first_query])
-    own = slice(KV_ROWS, KV_ROWS + count)
-    query_grad, key_grad, value_grad = attention(bias, kv[...], qg_mid, own)
-    scattered = nn(part_of(spread, SPREADS["middle"]), query_grad.astype(bf16))
-    key_grad = key_grad.reshape(SIDE, 2, HALF, width)
-    value_grad = value_grad.reshape(SIDE, 2, HALF, width)
-    for half, (query_out, pair_out) in enumerate(
-        ((left_query, left_pair), (right_query, right_pair))
-    ):
-        query_out[...] = scattered[half * HALF_TOKENS : (half + 1) * HALF_TOKENS].astype(bf16)
-        pair_out[:, :width] = key_grad[:, half].reshape(HALF_TOKENS, width)
-        pair_out[:, width:] = value_grad[:, half].reshape(HALF_TOKENS, width)
-    for side in (left_bias, right_bias):
-        last_key, last_query = first_key + side.shape[0], first_query + side.shape[1]
-        side[...] = window_bias(
-            spot, extent, keys[first_key:last_key], queries[:, first_query:last_query]
-        )
-        first_key, first_query = last_key, last_query
+
+    def mask(first_key, key_count, first_query, query_count):
+        at_keys = keys[first_key : first_key + key_count]
+        at_queries = queries[:, first_query : first_query + query_count]
+        return window_bias(spot, extent, at_keys, at_queries)
+
+    lanes = CORE_QUERIES * width // HEAD_DIM
+    bias = mask(0, count, 0, lanes)
+    inner = nn(part_of(gather, GATHERS["core"]), qg[...]).astype(bf16)
+    query_grad, key_grad, value_grad = attention(bias, kv[...], inner, slice(0, count))
+    query_out[...] = nn(part_of(spread, SPREADS["core"]), query_grad.astype(bf16)).astype(bf16)
+    pair_out[:, :width] = key_grad
+    pair_out[:, width:] = value_grad
+    first_key, first_query = count, lanes
+    for side in biases:
+        side[...] = mask(first_key, side.shape[0], first_query, side.shape[1])
+        first_key, first_query = first_key + side.shape[0], first_query + side.shape[1]
+
+
+def middle_kernel(
+    kv, qg, top_bias, bottom_bias, gather, spread, core_query, core_pair, left_query,
+    right_query, left_pair, right_pair
+):
+    width = left_query.shape[1]
+    rim = nn(part_of(gather, GATHERS["rim"]), qg[...]).astype(bf16)
+    near_rows = REACH * SIDE
+    last = kv.shape[0] - RIM_KEYS
+    top = attention(
+        top_bias[...], kv[:RIM_KEYS], rim[:RIM_QUERIES], slice(near_rows, 2 * near_rows)
+    )
+    bottom = attention(bottom_bias[...], kv[last:], rim[RIM_QUERIES:], slice(0, near_rows))
+    query_grad = jnp.concatenate([top[0], bottom[0]], axis=0).astype(bf16)
+    scattered = nn(part_of(spread, SPREADS["rim"]), query_grad)
+    scattered = (scattered + core_query[...].astype(f32)).astype(bf16)
+    between = jnp.zeros((SIDE * SIDE - 2 * near_rows, width), f32)
+    for which, first in ((1, 0), (2, width)):
+        grad = jnp.concatenate([top[which], between, bottom[which]], axis=0)
+        grad += core_pair[:, first : first + width]
+        grad = grad.reshape(SIDE, 2, HALF, width)
+        for half, pair_out in enumerate((left_pair, right_pair)):
+            pair_out[:, first : first + width] = grad[:, half].reshape(HALF_TOKENS, width)
+    left_query[...] = scattered[:HALF_TOKENS]
+    right_query[...] = scattered[HALF_TOKENS:]
 
 
 def side_kernel(
@@ -397,26 +443,34 @@
     )
     far = paired(far, "row", 1)
     near = paired(near, "row", 0)
+    bias = shape((2 * KV_EDGE, 2 * QG_EDGE * heads), f32)
+    rim = shape((RIM_KEYS, RIM_QUERIES * heads), f32)
+    gather, spread = gathers(), spreads()
+    core_query, core_pair, top_bias, bottom_bias, left_bias, right_bias = near_call(
+        functools.partial(core_kernel, extent),
+        "core",
+        [shape((count, head_cols), bf16), shape((count, 2 * head_cols), f32), rim, rim, bias, bias],
+        [SMEM] * 2 + [VMEM] * 5,
+        row, col, kv, qg, places(heads), gather, spread,
+    )
     side = shape((KV_EDGE + QG_EDGE, 2 * head_cols), bf16)
-    gather, spread = gathers(), spreads()
     tall = [shape((lines * SIDE, 2 * head_cols), bf16) for lines in (WIDE, TALL)]
     leftward, rightward, kv_tall, qg_tall = near_call(
         edges_kernel,
         "edges",
         [side] * 2 + tall,
-        [SMEM] + [VMEM] * 5,
-        row, kv, qg, far, near, gather,
+        [SMEM] + [VMEM] * 6,
+        row, kv, qg, far, near, gather, core_query,
     )
     from_left = moved(rightward, "col", 1)
     from_right = moved(leftward, "col", -1)
-    bias = shape((2 * KV_EDGE, 2 * QG_EDGE * heads), f32)
     queries, pairs = shape((count // 2, head_cols), bf16), shape((count // 2, 2 * head_cols), f32)
-    left_query, right_query, left_pair, right_pair, left_bias, right_bias = near_call(
-        functools.partial(middle_kernel, extent),
+    left_query, right_query, left_pair, right_pair = near_call(
+        middle_kernel,
         "middle",
-        [queries, queries, pairs, pairs, bias, bias],
-        [SMEM] * 2 + [VMEM] * 5,
-        row, col, kv_tall, qg_tall, places(heads), gather, spread,
+        [queries, queries, pairs, pairs],
+        [VMEM] * 8,
+        kv_tall, qg_tall, top_bias, bottom_bias, gather, spread, core_query, core_pair,
     )
     own = count // tp
     reduced = []

time: 54.8 us -> 54.8 us (level)
  Pallas kernels: 11.1 us -> 11.9 us
  waiting for transfers between devices: 15.6 us -> 14.8 us
    ppermute x2, waiting for transfers between devices: 7.47 us -> 5.28 us  [paired(): return lax.ppermute(block, axis, route)]
    ppermute x2, waiting for transfers between devices: 2.42 us -> 3.83 us  [moved(): return lax.ppermute(block, axis, route)]
    pallas_call x7 -> x8, Pallas kernels: 8 us -> 8.73 us  [near_call(): pl.pallas_call(kernel, out_shape=outs, in_specs=places, out_specs=jax.tre...]
  transfers between devices with their start and end apart: 8 -> 8, of which waited for: 4 -> 4; matrix products, arithmetic and copies ran while one was open for 0% -> 0% of each run, Pallas kernels for 12% -> 13%
where the time goes in v6:
time: 54.8 us; the launch traced here: 54.5 us
  starting transfers between devices  27.5 us (50%)
  waiting for transfers between devices  14.8 us (27%)
  Pallas kernels  11.9 us (22%)
    pallas_call x8, Pallas kernels, near_call(): pl.pallas_call(kernel, out_shape=outs, in_specs=places, out_specs=jax.tre...  8.73 us
    ppermute x2, starting transfers between devices, paired(): return lax.ppermute(block, axis, route)  7.66 us
    ppermute x2, starting transfers between devices, moved(): return lax.ppermute(block, axis, route)  7.55 us
    ppermute x2, starting transfers between devices, per_device(): reduced += [kept, lax.ppermute(sent, 'tp', [(i, i ^ 2) for i in range(tp)])]  6.47 us
    ppermute x2, starting transfers between devices, per_device(): received = lax.ppermute(sent, 'tp', [(i, i ^ 1) for i in range(tp)])  5.84 us
    ppermute x2, waiting for transfers between devices, paired(): return lax.ppermute(block, axis, route)  5.28 us
    ppermute x2, waiting for transfers between devices, per_device(): reduced += [kept, lax.ppermute(sent, 'tp', [(i, i ^ 2) for i in range(tp)])]  5.01 us
    ppermute x2, waiting for transfers between devices, moved(): return lax.ppermute(block, axis, route)  3.83 us
  transfers between devices with their start and end apart: 8, of which 4 were waited for; matrix products, arithmetic and copies ran while one was open for 0% of the time, Pallas kernels for 13%

profile of v6, /device:TPU:250, one launch (start us, length us, event | category | flops | bytes accessed | tf_op | source)
XLA Modules:
  0.0 54.5 jit_solution(4243933237042518293)
XLA Ops:
  0.0 0.0 copy-start.1
  0.0 0.0 copy-start.2
  0.0 0.0 copy-start.5
  0.0 3.2 %project.1 = (bf16[256,512]{1,0:T(8,128)(2,1)S(1)}, bf16[256,512]{1,0:T(8,128)(2,1)S(1)}, bf16[144,512]{1,0:T(8,128)(2,1)S(1)}, bf16[144,512]{1,0:T(8,128)(2,1)S(1)}) custom-call(s32[1]{0:T(128)} %bitcast.1.row, s32[1]{0:T(128)} %bitcast.2.col, s32[1]{0:T(128)} %bitcast.place, bf16[256,1024]{1,0:T(8,128)(2,1)} %bitcast.10, f32[1,1024]{1,0:T(1,128)} %bitcast.14, ...), custom_call_target="tpu_custom_call" | custom-call | tf_op jit(solution)/shard_map/project/pallas_call | solution.py:420
  3.2 4.2 %collective-permute-start = (bf16[144,512]{1,0:T(8,128)(2,1)S(1)}, bf16[144,512]{1,0:T(8,128)(2,1)S(1)}, u32[]{:S(2)}, u32[]{:S(2)}) collective-permute-start(bf16[144,512]{1,0:T(8,128)(2,1)S(1)} %get-tuple-element.33), channel_id=1, source_target_pairs={{32,64},{64,32},{96,128},{128,96},{160,192},{192,160},{224,256},{2... | collective-permute-start | bytes 442376 | tf_op jit(solution)/shard_map/ppermute | solution.py:395
  7.3 3.5 %collective-permute-start.1 = (bf16[144,512]{1,0:T(8,128)(2,1)S(1)}, bf16[144,512]{1,0:T(8,128)(2,1)S(1)}, u32[]{:S(2)}, u32[]{:S(2)}) collective-permute-start(bf16[144,512]{1,0:T(8,128)(2,1)S(1)} %get-tuple-element.34), channel_id=1, source_target_pairs={{0,32},{32,0},{64,96},{96,64},{128,160},{160,128},{192,224},{224,1... | collective-permute-start | bytes 442376 | tf_op jit(solution)/shard_map/ppermute | solution.py:395
  10.8 0.0 copy-done.1
  10.9 0.0 copy-done.2
  10.9 0.0 copy-done.5
  10.9 2.1 %core.1 = (bf16[256,256]{1,0:T(8,128)(2,1)S(1)}, f32[256,512]{1,0:T(8,128)S(1)}, f32[192,256]{1,0:T(8,128)S(1)}, f32[192,256]{1,0:T(8,128)S(1)}, f32[352,640]{1,0:T(8,128)S(1)}, /*index=5*/f32[352,640]{1,0:T(8,128)S(1)}) custom-call(s32[1]{0:T(128)} %bitcast.1.row, s32[1]{0:T(128)} %bitcast.2.col, bf16[256,512]{1,0:T(8,128)(2,1)S(1)} %get-tuple-element.31.kv, ...), custom_call_target="tpu_custom_call" | custom-call | tf_op jit(solution)/shard_map/core/pallas_call | solution.py:52
  13.0 5.3 %collective-permute-done.far = bf16[144,512]{1,0:T(8,128)(2,1)S(1)} collective-permute-done((bf16[144,512]{1,0:T(8,128)(2,1)S(1)}, bf16[144,512]{1,0:T(8,128)(2,1)S(1)}, u32[]{:S(2)}, u32[]{:S(2)}) %collective-permute-start) | collective-permute-done | bytes 147488 | tf_op jit(solution)/shard_map/ppermute | solution.py:395
  18.3 0.0 collective-permute-done.1.near
  18.3 0.5 edges.1
  18.8 0.0 copy-start
  18.8 2.1 %collective-permute-start.5 = (bf16[256,512]{1,0:T(8,128)(2,1)S(1)}, bf16[256,512]{1,0:T(8,128)(2,1)S(1)}, u32[]{:S(2)}, u32[]{:S(2)}) collective-permute-start(bf16[256,512]{1,0:T(8,128)(2,1)S(1)} %get-tuple-element.36.mine), channel_id=1, source_target_pairs={{4,0},{8,4},{12,8},{16,12},{20,16},{24,20},{28,24},{5,1},{9,5},{13... | collective-permute-start | bytes 786440 | tf_op jit(solution)/shard_map/ppermute | solution.py:401
  20.9 5.5 %collective-permute-start.2 = (bf16[256,512]{1,0:T(8,128)(2,1)S(1)}, bf16[256,512]{1,0:T(8,128)(2,1)S(1)}, u32[]{:S(2)}, u32[]{:S(2)}) collective-permute-start(bf16[256,512]{1,0:T(8,128)(2,1)S(1)} %get-tuple-element.37.mine), channel_id=1, source_target_pairs={{0,4},{4,8},{8,12},{12,16},{16,20},{20,24},{24,28},{1,5},{5,9},{9,... | collective-permute-start | bytes 786440 | tf_op jit(solution)/shard_map/ppermute | solution.py:401
  26.4 1.3 %middle.1 = (bf16[128,256]{1,0:T(8,128)(2,1)S(1)}, bf16[128,256]{1,0:T(8,128)(2,1)S(1)}, f32[128,512]{1,0:T(8,128)S(1)}, f32[128,512]{1,0:T(8,128)S(1)}) custom-call(bf16[448,512]{1,0:T(8,128)(2,1)S(1)} %get-tuple-element.38.kv, bf16[352,512]{1,0:T(8,128)(2,1)S(1)} %get-tuple-element.39.qg, f32[192,256]{1,0:T(8,128)S(1)} %get-tuple-element.40.top_bias, ...), custom_call_target="tpu_custom_call" | custom-call | tf_op jit(solution)/shard_map/middle/pallas_call | solution.py:52
  27.7 3.8 %collective-permute-done.5.theirs = bf16[256,512]{1,0:T(8,128)(2,1)S(1)} collective-permute-done((bf16[256,512]{1,0:T(8,128)(2,1)S(1)}, bf16[256,512]{1,0:T(8,128)(2,1)S(1)}, u32[]{:S(2)}, u32[]{:S(2)}) %collective-permute-start.5) | collective-permute-done | bytes 262176 | tf_op jit(solution)/shard_map/ppermute | solution.py:401
  31.5 0.0 copy-done
  31.5 1.9 %right_side.1 = (bf16[64,1024]{1,0:T(8,128)(2,1)S(1)}, f32[64,1024]{1,0:T(8,128)S(1)}) custom-call(s32[1]{0:T(128)} %bitcast.place, bf16[256,512]{1,0:T(8,128)(2,1)S(1)} %get-tuple-element.37.mine, bf16[256,512]{1,0:T(8,128)(2,1)S(1)} %collective-permute-done.5.theirs, bf16[128,256]{1,0:T(8,128)(2,1)S(1)} %get-tuple-element.50.query_mid, ...), custom_call_target="tpu_custom_call" | custom-call | tf_op jit(solution)/shard_map/right_side/pallas_call | solution.py:52
  33.4 3.2 %collective-permute-start.6 = (bf16[64,1024]{1,0:T(8,128)(2,1)S(1)}, bf16[64,1024]{1,0:T(8,128)(2,1)S(1)}, u32[]{:S(2)}, u32[]{:S(2)}) collective-permute-start(bf16[64,1024]{1,0:T(8,128)(2,1)S(1)} %get-tuple-element.54), channel_id=1, source_target_pairs={{0,1},{1,0},{2,3},{3,2},{4,5},{5,4},{6,7},{7,6},{8,9},{9,8},{10,11... | collective-permute-start | bytes 393224 | tf_op jit(solution)/shard_map/ppermute | solution.py:491
  36.6 0.0 collective-permute-done.2.theirs
  36.7 0.0 copy-start.3
  36.7 0.0 copy-start.4
  36.7 0.0 copy-start.6
  36.7 1.9 %left_side.1 = (bf16[64,1024]{1,0:T(8,128)(2,1)S(1)}, f32[64,1024]{1,0:T(8,128)S(1)}) custom-call(s32[1]{0:T(128)} %bitcast.place, bf16[256,512]{1,0:T(8,128)(2,1)S(1)} %get-tuple-element.36.mine, bf16[256,512]{1,0:T(8,128)(2,1)S(1)} %collective-permute-done.2.theirs, bf16[128,256]{1,0:T(8,128)(2,1)S(1)} %get-tuple-element.43.query_mid, ...), custom_call_target="tpu_custom_call" | custom-call | tf_op jit(solution)/shard_map/left_side/pallas_call | solution.py:52
  38.6 2.6 %collective-permute-start.3 = (bf16[64,1024]{1,0:T(8,128)(2,1)S(1)}, bf16[64,1024]{1,0:T(8,128)(2,1)S(1)}, u32[]{:S(2)}, u32[]{:S(2)}) collective-permute-start(bf16[64,1024]{1,0:T(8,128)(2,1)S(1)} %get-tuple-element.47), channel_id=1, source_target_pairs={{0,1},{1,0},{2,3},{3,2},{4,5},{5,4},{6,7},{7,6},{8,9},{9,8},{10,11... | collective-permute-start | bytes 393224 | tf_op jit(solution)/shard_map/ppermute | solution.py:491
  41.2 0.0 collective-permute-done.6.received
  41.3 3.7 %collective-permute-start.7 = (bf16[32,1024]{1,0:T(8,128)(2,1)S(1)}, bf16[32,1024]{1,0:T(8,128)(2,1)S(1)}, u32[]{:S(2)}, u32[]{:S(2)}) collective-permute-start(bf16[32,1024]{1,0:T(8,128)(2,1)S(1)} %get-tuple-element.56), channel_id=1, source_target_pairs={{0,2},{1,3},{2,0},{3,1},{4,6},{5,7},{6,4},{7,5},{8,10},{9,11},{10,... | collective-permute-start | bytes 196616 | tf_op jit(solution)/shard_map/ppermute | solution.py:499
  45.0 0.7 %collective-permute-done.3.received = bf16[64,1024]{1,0:T(8,128)(2,1)S(1)} collective-permute-done((bf16[64,1024]{1,0:T(8,128)(2,1)S(1)}, bf16[64,1024]{1,0:T(8,128)(2,1)S(1)}, u32[]{:S(2)}, u32[]{:S(2)}) %collective-permute-start.3) | collective-permute-done | bytes 131104 | tf_op jit(solution)/shard_map/ppermute | solution.py:491
  45.8 2.7 %collective-permute-start.4 = (bf16[32,1024]{1,0:T(8,128)(2,1)S(1)}, bf16[32,1024]{1,0:T(8,128)(2,1)S(1)}, u32[]{:S(2)}, u32[]{:S(2)}) collective-permute-start(bf16[32,1024]{1,0:T(8,128)(2,1)S(1)} %get-tuple-element.49), channel_id=1, source_target_pairs={{0,2},{1,3},{2,0},{3,1},{4,6},{5,7},{6,4},{7,5},{8,10},{9,11},{10,... | collective-permute-start | bytes 196616 | tf_op jit(solution)/shard_map/ppermute | solution.py:499
  48.5 0.0 collective-permute-done.7.right_received
  48.5 5.0 %collective-permute-done.4.left_received = bf16[32,1024]{1,0:T(8,128)(2,1)S(1)} collective-permute-done((bf16[32,1024]{1,0:T(8,128)(2,1)S(1)}, bf16[32,1024]{1,0:T(8,128)(2,1)S(1)}, u32[]{:S(2)}, u32[]{:S(2)}) %collective-permute-start.4) | collective-permute-done | bytes 65568 | tf_op jit(solution)/shard_map/ppermute | solution.py:499
  53.5 0.0 copy-done.3
  53.5 0.0 copy-done.4
  53.5 0.0 copy-done.6
  53.5 0.9 %finish.1 = f32[4,16,1024]{2,1,0:T(8,128)} custom-call(s32[1]{0:T(128)} %bitcast.place, f32[32,1024]{1,0:T(8,128)S(1)} %get-tuple-element.48.left_kept, bf16[32,1024]{1,0:T(8,128)(2,1)S(1)} %collective-permute-done.4.left_received, f32[32,1024]{1,0:T(8,128)S(1)} %get-tuple-element.55.right_kept, bf16[32,1024]{1,0:T(8,128)(2,1)S(1)} %collective-permute-done.7.right_received, ...), custom_call_target="tpu_custom_call" | custom-call | tf_op jit(solution)/shard_map/finish/pallas_call | solution.py:52
  (2 shorter events, 0.1 us)
Async XLA Ops:
  0.0 10.9 %copy-start.1 = (bf16[768,448]{1,0:T(8,128)(2,1)S(1)}, bf16[768,448]{1,0:T(8,128)(2,1)}, u32[]{:S(2)}) copy-start(bf16[768,448]{1,0:T(8,128)(2,1)} %constant.21.clone.gather) | copy-start | bytes 2064388
  0.0 10.9 %copy-start.2 = (bf16[768,256]{1,0:T(8,128)(2,1)S(1)}, bf16[768,256]{1,0:T(8,128)(2,1)}, u32[]{:S(2)}) copy-start(bf16[768,256]{1,0:T(8,128)(2,1)} %constant.22.clone.spread) | copy-start | bytes 1179652
  0.0 10.9 %copy-start.5 = (f32[8,2304]{1,0:T(8,128)S(1)}, f32[8,2304]{1,0:T(8,128)}, u32[]{:S(2)}) copy-start(f32[8,2304]{1,0:T(8,128)} %constant.23.clone.points) | copy-start | bytes 221188
  3.2 15.1 %collective-permute-start = (bf16[144,512]{1,0:T(8,128)(2,1)S(1)}, bf16[144,512]{1,0:T(8,128)(2,1)S(1)}, u32[]{:S(2)}, u32[]{:S(2)}) collective-permute-start(bf16[144,512]{1,0:T(8,128)(2,1)S(1)} %get-tuple-element.33), channel_id=1, source_target_pairs={{32,64},{64,32},{96,128},{128,96},{160,192},{192,160},{224,256},{2... | collective-permute-start | bytes 442376 | tf_op jit(solution)/shard_map/ppermute | solution.py:395
  7.3 11.0 %collective-permute-start.1 = (bf16[144,512]{1,0:T(8,128)(2,1)S(1)}, bf16[144,512]{1,0:T(8,128)(2,1)S(1)}, u32[]{:S(2)}, u32[]{:S(2)}) collective-permute-start(bf16[144,512]{1,0:T(8,128)(2,1)S(1)} %get-tuple-element.34), channel_id=1, source_target_pairs={{0,32},{32,0},{64,96},{96,64},{128,160},{160,128},{192,224},{224,1... | collective-permute-start | bytes 442376 | tf_op jit(solution)/shard_map/ppermute | solution.py:395
  18.8 12.7 %copy-start = (bf16[1024,3,256]{2,0,1:T(8,128)(2,1)S(1)}, bf16[1024,3,256]{2,0,1:T(8,128)(2,1)}, u32[]{:S(2)}) copy-start(bf16[1024,3,256]{2,0,1:T(8,128)(2,1)} %param.10) | copy-start | bytes 4718596
  18.8 12.7 %collective-permute-start.5 = (bf16[256,512]{1,0:T(8,128)(2,1)S(1)}, bf16[256,512]{1,0:T(8,128)(2,1)S(1)}, u32[]{:S(2)}, u32[]{:S(2)}) collective-permute-start(bf16[256,512]{1,0:T(8,128)(2,1)S(1)} %get-tuple-element.36.mine), channel_id=1, source_target_pairs={{4,0},{8,4},{12,8},{16,12},{20,16},{24,20},{28,24},{5,1},{9,5},{13... | collective-permute-start | bytes 786440 | tf_op jit(solution)/shard_map/ppermute | solution.py:401
  20.9 15.8 %collective-permute-start.2 = (bf16[256,512]{1,0:T(8,128)(2,1)S(1)}, bf16[256,512]{1,0:T(8,128)(2,1)S(1)}, u32[]{:S(2)}, u32[]{:S(2)}) collective-permute-start(bf16[256,512]{1,0:T(8,128)(2,1)S(1)} %get-tuple-element.37.mine), channel_id=1, source_target_pairs={{0,4},{4,8},{8,12},{12,16},{16,20},{20,24},{24,28},{1,5},{5,9},{9,... | collective-permute-start | bytes 786440 | tf_op jit(solution)/shard_map/ppermute | solution.py:401
  33.4 7.8 %collective-permute-start.6 = (bf16[64,1024]{1,0:T(8,128)(2,1)S(1)}, bf16[64,1024]{1,0:T(8,128)(2,1)S(1)}, u32[]{:S(2)}, u32[]{:S(2)}) collective-permute-start(bf16[64,1024]{1,0:T(8,128)(2,1)S(1)} %get-tuple-element.54), channel_id=1, source_target_pairs={{0,1},{1,0},{2,3},{3,2},{4,5},{5,4},{6,7},{7,6},{8,9},{9,8},{10,11... | collective-permute-start | bytes 393224 | tf_op jit(solution)/shard_map/ppermute | solution.py:491
  36.7 16.9 %copy-start.3 = (bf16[16,16,1024]{2,1,0:T(8,128)(2,1)S(1)}, bf16[16,16,1024]{2,1,0:T(8,128)(2,1)}, u32[]{:S(2)}) copy-start(bf16[16,16,1024]{2,1,0:T(8,128)(2,1)} %param.8) | copy-start | bytes 1572868
  36.7 16.9 %copy-start.4 = (bf16[16,16,1024]{2,1,0:T(8,128)(2,1)S(1)}, bf16[16,16,1024]{2,1,0:T(8,128)(2,1)}, u32[]{:S(2)}) copy-start(bf16[16,16,1024]{2,1,0:T(8,128)(2,1)} %param.12) | copy-start | bytes 1572868
  36.7 16.9 %copy-start.6 = (f32[1024]{0:T(1024)S(1)}, f32[1024]{0:T(1024)}, u32[]{:S(2)}) copy-start(f32[1024]{0:T(1024)} %param.9) | copy-start | bytes 12292
  38.6 7.1 %collective-permute-start.3 = (bf16[64,1024]{1,0:T(8,128)(2,1)S(1)}, bf16[64,1024]{1,0:T(8,128)(2,1)S(1)}, u32[]{:S(2)}, u32[]{:S(2)}) collective-permute-start(bf16[64,1024]{1,0:T(8,128)(2,1)S(1)} %get-tuple-element.47), channel_id=1, source_target_pairs={{0,1},{1,0},{2,3},{3,2},{4,5},{5,4},{6,7},{7,6},{8,9},{9,8},{10,11... | collective-permute-start | bytes 393224 | tf_op jit(solution)/shard_map/ppermute | solution.py:491
  41.3 7.2 %collective-permute-start.7 = (bf16[32,1024]{1,0:T(8,128)(2,1)S(1)}, bf16[32,1024]{1,0:T(8,128)(2,1)S(1)}, u32[]{:S(2)}, u32[]{:S(2)}) collective-permute-start(bf16[32,1024]{1,0:T(8,128)(2,1)S(1)} %get-tuple-element.56), channel_id=1, source_target_pairs={{0,2},{1,3},{2,0},{3,1},{4,6},{5,7},{6,4},{7,5},{8,10},{9,11},{10,... | collective-permute-start | bytes 196616 | tf_op jit(solution)/shard_map/ppermute | solution.py:499
  45.8 7.8 %collective-permute-start.4 = (bf16[32,1024]{1,0:T(8,128)(2,1)S(1)}, bf16[32,1024]{1,0:T(8,128)(2,1)S(1)}, u32[]{:S(2)}, u32[]{:S(2)}) collective-permute-start(bf16[32,1024]{1,0:T(8,128)(2,1)S(1)} %get-tuple-element.49), channel_id=1, source_target_pairs={{0,2},{1,3},{2,0},{3,1},{4,6},{5,7},{6,4},{7,5},{8,10},{9,11},{10,... | collective-permute-start | bytes 196616 | tf_op jit(solution)/shard_map/ppermute | solution.py:499

commit v7 on v6

--- a/solution.py
+++ b/solution.py
@@ -30,6 +30,7 @@
 OWN_FROM = 32
 OWN_EDGE = 112
 FAR = 1000.0
+LANES = 128
 bf16 = jnp.bfloat16
 f32 = jnp.float32
 VMEM = pl.BlockSpec(memory_space=pltpu.VMEM)
@@ -93,13 +94,11 @@
     "core": (2 * KV_EDGE + 2 * QG_EDGE, CORE_QUERIES, SIDE * SIDE),
     "rim": (2 * KV_EDGE + 2 * QG_EDGE + CORE_QUERIES, 2 * RIM_QUERIES, TALL * SIDE),
 }
-HALF = SIDE // 2
-HALF_TOKENS = SIDE * HALF
 SPREADS = {
-    "core": (0, 2 * HALF_TOKENS, CORE_QUERIES),
-    "rim": (0, 2 * HALF_TOKENS, 2 * RIM_QUERIES, CORE_QUERIES),
-    "keys": ((2 * HALF_TOKENS, HALF_TOKENS, OWN_EDGE), (3 * HALF_TOKENS, HALF_TOKENS, OWN_EDGE)),
-    "queries": ((4 * HALF_TOKENS, HALF_TOKENS, QG_EDGE), (5 * HALF_TOKENS, HALF_TOKENS, QG_EDGE)),
+    "core": (0, SIDE * SIDE, CORE_QUERIES),
+    "rim": (0, SIDE * SIDE, 2 * RIM_QUERIES, CORE_QUERIES),
+    "keys": (SIDE * SIDE, SIDE * SIDE, 2 * OWN_EDGE),
+    "queries": (2 * SIDE * SIDE, SIDE * SIDE, 2 * QG_EDGE),
 }
 
 
@@ -127,24 +126,22 @@
 def spreads():
     pairs = []
 
-    def add(first, halo, column, target):
-        token = target - halo * SIDE
+    def add(name, column, token):
         if 0 <= token < SIDE * SIDE:
-            y, x = divmod(token, SIDE)
-            pairs.append((first + x // HALF * HALF_TOKENS + y * HALF + x % HALF, column))
+            pairs.append((SPREADS[name][0] + token, column))
 
     for t, (y, x) in enumerate(cells(INNER, INNER)):
-        add(0, 0, t, y * SIDE + x)
+        add("core", t, y * SIDE + x)
     for part, rows in enumerate((TOP, BOTTOM)):
         for t, (y, x) in enumerate(cells(rows, INNER)):
-            add(0, 0, CORE_QUERIES + part * RIM_QUERIES + t, y * SIDE + x)
-    for first in (0, SIDE - REACH):
+            add("rim", CORE_QUERIES + part * RIM_QUERIES + t, y * SIDE + x)
+    for part, first in enumerate((0, SIDE - REACH)):
         for t, f in strip_pairs(WIDE, REACH, first):
-            add(SPREADS["keys"][0][0], REACH, t - OWN_FROM, f)
-    for first in (0, SIDE - RADIUS):
+            add("keys", part * OWN_EDGE + t - OWN_FROM, f - KV_ROWS)
+    for part, first in enumerate((0, SIDE - RADIUS)):
         for t, f in strip_pairs(TALL, RADIUS, first):
-            add(SPREADS["queries"][0][0], RADIUS, t, f)
-    return table(6 * HALF_TOKENS, SIDE * SIDE, pairs)
+            add("queries", part * QG_EDGE + t, f - QG_ROWS)
+    return table(3 * SIDE * SIDE, SIDE * SIDE, pairs)
 
 
 def coords(rows, cols, total, pad):
@@ -166,7 +163,7 @@
     ):
         keys += [coords(wide, range(f, f + REACH), KV_EDGE, FAR) for f in key_firsts]
         both = [coords(tall, range(f, f + RADIUS), QG_EDGE, -FAR) for f in query_firsts]
-        queries.append(np.tile(np.concatenate(both, axis=1), (1, heads)))
+        queries += [np.tile(part, (1, heads)) for part in both]
     keys, queries = np.concatenate(keys, axis=1), np.concatenate(queries, axis=1)
     joined = np.full((8, queries.shape[1]), FAR, np.float32)
     joined[:2, : keys.shape[1]] = keys
@@ -253,12 +250,11 @@
     return [jnp.where(lanes == head, block, jnp.zeros_like(block)) for head in range(width // HEAD_DIM)]
 
 
-def attention(bias, kv, qg, own):
+def attention(bias, kv, groups, own):
     width = kv.shape[1] // 2
-    count = qg.shape[0]
     key, value = kv[:, :width], kv[:, width:]
-    query = jnp.concatenate(by_head(qg[:, :width]), axis=0)
-    upstream = jnp.concatenate(by_head(qg[:, width:]), axis=0)
+    query = jnp.concatenate([part for qg in groups for part in by_head(qg[:, :width])], axis=0)
+    upstream = jnp.concatenate([part for qg in groups for part in by_head(qg[:, width:])], axis=0)
     scores = nt(key, query) + bias
     dots = nt(value, upstream)
     exponent = jnp.exp(scores - jnp.max(scores, axis=0, keepdims=True))
@@ -268,12 +264,15 @@
     score_grads = (weights * (dots - centre)).astype(bf16)
     value_grad = nn(weights[own].astype(bf16), upstream)
     key_grad = nn(score_grads[own], query)
-    stacked = nn(key.astype(f32).T.astype(bf16), score_grads).T
-    parts = [stacked[first : first + count] for first in range(0, stacked.shape[0], count)]
+    count = groups[0].shape[0]
+    heads = width // HEAD_DIM
+    used = -(-count * heads // LANES) * LANES
+    stacked = nn(key.astype(f32).T.astype(bf16), score_grads[:, :used]).T
     lanes = lax.broadcasted_iota(jnp.int32, (1, width), 1) // HEAD_DIM
-    query_grad = parts[0]
-    for head in range(1, len(parts)):
-        query_grad = jnp.where(lanes == head, parts[head], query_grad)
+    query_grad = stacked[:count]
+    for head in range(1, heads):
+        part = stacked[head * count : (head + 1) * count]
+        query_grad = jnp.where(lanes == head, part, query_grad)
     return query_grad * (HEAD_DIM ** (-0.5)), key_grad, value_grad
 
 
@@ -293,7 +292,7 @@
     lanes = CORE_QUERIES * width // HEAD_DIM
     bias = mask(0, count, 0, lanes)
     inner = nn(part_of(gather, GATHERS["core"]), qg[...]).astype(bf16)
-    query_grad, key_grad, value_grad = attention(bias, kv[...], inner, slice(0, count))
+    query_grad, key_grad, value_grad = attention(bias, kv[...], [inner], slice(0, count))
     query_out[...] = nn(part_of(spread, SPREADS["core"]), query_grad.astype(bf16)).astype(bf16)
     pair_out[:, :width] = key_grad
     pair_out[:, width:] = value_grad
@@ -304,60 +303,68 @@
 
 
 def middle_kernel(
-    kv, qg, top_bias, bottom_bias, gather, spread, core_query, core_pair, left_query,
-    right_query, left_pair, right_pair
+    kv, qg, top_bias, bottom_bias, gather, spread, core_query, core_pair, query_out, pair_out
 ):
-    width = left_query.shape[1]
+    width = query_out.shape[1]
     rim = nn(part_of(gather, GATHERS["rim"]), qg[...]).astype(bf16)
     near_rows = REACH * SIDE
     last = kv.shape[0] - RIM_KEYS
     top = attention(
-        top_bias[...], kv[:RIM_KEYS], rim[:RIM_QUERIES], slice(near_rows, 2 * near_rows)
-    )
-    bottom = attention(bottom_bias[...], kv[last:], rim[RIM_QUERIES:], slice(0, near_rows))
+        top_bias[...], kv[:RIM_KEYS], [rim[:RIM_QUERIES]], slice(near_rows, 2 * near_rows)
+    )
+    bottom = attention(bottom_bias[...], kv[last:], [rim[RIM_QUERIES:]], slice(0, near_rows))
     query_grad = jnp.concatenate([top[0], bottom[0]], axis=0).astype(bf16)
     scattered = nn(part_of(spread, SPREADS["rim"]), query_grad)
-    scattered = (scattered + core_query[...].astype(f32)).astype(bf16)
+    query_out[...] = (scattered + core_query[...].astype(f32)).astype(bf16)
     between = jnp.zeros((SIDE * SIDE - 2 * near_rows, width), f32)
     for which, first in ((1, 0), (2, width)):
         grad = jnp.concatenate([top[which], between, bottom[which]], axis=0)
-        grad += core_pair[:, first : first + width]
-        grad = grad.reshape(SIDE, 2, HALF, width)
-        for half, pair_out in enumerate((left_pair, right_pair)):
-            pair_out[:, first : first + width] = grad[:, half].reshape(HALF_TOKENS, width)
-    left_query[...] = scattered[:HALF_TOKENS]
-    right_query[...] = scattered[HALF_TOKENS:]
-
-
-def side_kernel(
-    half, place, mine, theirs, query_mid, pair_mid, bias, spread, weight, sent, kept, stacked
+        pair_out[:, first : first + width] = grad + core_pair[:, first : first + width]
+
+
+def back_projected(place, others, stacked, weight):
+    width = weight.shape[2]
+    block = stacked.shape[0] // 4
+    parts = []
+    for other in others:
+        first = pl.multiple_of(jnp.bitwise_xor(place[0], other) * block, block)
+        parts.append(stacked[pl.ds(first, block), :])
+    rows = jnp.concatenate(parts, axis=0)
+    total = nt(rows[:, :width], weight[0])
+    total += nt(rows[:, width : 2 * width], weight[1])
+    return total + nt(rows[:, 2 * width :], weight[2])
+
+
+def sides_kernel(
+    place, leftward, from_left, rightward, from_right, query_mid, pair_mid, left_bias, right_bias,
+    spread, weight, sent, stacked
 ):
     width = query_mid.shape[1]
     own = slice(OWN_FROM, OWN_FROM + OWN_EDGE)
-    kv = jnp.concatenate([mine[:KV_EDGE], theirs[:KV_EDGE]], axis=0)
-    qg = jnp.concatenate([mine[KV_EDGE:], theirs[KV_EDGE:]], axis=0)
-    query_grad, key_grad, value_grad = attention(bias[...], kv, qg, own)
-    query_side = query_grad[:QG_EDGE].astype(bf16)
-    pair_side = jnp.concatenate([key_grad, value_grad], axis=1)
+    query_parts, pair_parts = [], []
+    for mine, theirs, bias in (
+        (leftward, from_left, left_bias),
+        (rightward, from_right, right_bias),
+    ):
+        kv = jnp.concatenate([mine[:KV_EDGE], theirs[:KV_EDGE]], axis=0)
+        groups = [mine[KV_EDGE:], theirs[KV_EDGE:]]
+        query_grad, key_grad, value_grad = attention(bias[...], kv, groups, own)
+        query_parts.append(query_grad)
+        pair_parts.append(jnp.concatenate([key_grad, value_grad], axis=1))
+    query_side = jnp.concatenate(query_parts, axis=0).astype(bf16)
+    pair_side = jnp.concatenate(pair_parts, axis=0)
     coarse = pair_side.astype(bf16)
     fine = (pair_side - coarse.astype(f32)).astype(bf16)
-    key_spread = part_of(spread, SPREADS["keys"][half])
-    query_spread = part_of(spread, SPREADS["queries"][half])
+    key_spread, query_spread = (part_of(spread, SPREADS[name]) for name in ("keys", "queries"))
     pair = pair_mid[...] + (nn(key_spread, coarse) + nn(key_spread, fine))
     query_grad = query_mid[...].astype(f32) + nn(query_spread, query_side)
     stacked[:, :width] = query_grad.astype(bf16)
     stacked[:, width:] = pair.astype(bf16)
-    block = sent.shape[0] // 2
-    ordered = []
-    for other in (1, 3, 0, 2):
-        first = pl.multiple_of(jnp.bitwise_xor(place[0], other) * block, block)
-        ordered.append(stacked[pl.ds(first, block), :])
-    ordered = jnp.concatenate(ordered, axis=0)
-    total = nt(ordered[:, :width], weight[0])
-    total += nt(ordered[:, width : 2 * width], weight[1])
-    total += nt(ordered[:, 2 * width :], weight[2])
-    sent[...] = total[: 2 * block].astype(bf16)
-    kept[...] = total[2 * block :]
+    sent[...] = back_projected(place, (1, 3), stacked, weight).astype(bf16)
+
+
+def keep_kernel(place, stacked, weight, kept):
+    kept[...] = back_projected(place, (0, 2), stacked, weight)
 
 
 def fold_kernel(kept, received, sent, still):
@@ -366,25 +373,17 @@
     sent[...] = (kept[block:] + received[block:].astype(f32)).astype(bf16)
 
 
-def finish_kernel(
-    place, left_kept, left_received, right_kept, right_received, latent, gain, cotangent, result
-):
-    lines, cols, width = result.shape
-    count = lines * cols
+def finish_kernel(place, kept, received, latent, gain, cotangent, result):
+    count = kept.shape[0]
     first = pl.multiple_of(place[0] * count, count)
     tokens = latent[pl.ds(first, count), :].astype(f32)
     upstream = cotangent[pl.ds(first, count), :].astype(f32)
-    halves = [
-        (kept[...] + received[...].astype(f32)).reshape(lines, cols // 2, width)
-        for kept, received in ((left_kept, left_received), (right_kept, right_received))
-    ]
-    summed = jnp.concatenate(halves, axis=1).reshape(count, width)
+    summed = kept[...] + received[...].astype(f32)
     inverse = lax.rsqrt(jnp.mean(tokens * tokens, axis=-1, keepdims=True) + 1e-06)
     unit = tokens * inverse
     scaled = summed * gain[...]
     stat = jnp.mean(scaled * unit, axis=-1, keepdims=True)
-    outcome = upstream + inverse * (scaled - unit * stat)
-    result[...] = outcome.reshape(lines, cols, width)
+    result[...] = upstream + inverse * (scaled - unit * stat)
 
 
 def paired(block, axis, first):
@@ -464,46 +463,46 @@
     )
     from_left = moved(rightward, "col", 1)
     from_right = moved(leftward, "col", -1)
-    queries, pairs = shape((count // 2, head_cols), bf16), shape((count // 2, 2 * head_cols), f32)
-    left_query, right_query, left_pair, right_pair = near_call(
+    query_mid, pair_mid = near_call(
         middle_kernel,
         "middle",
-        [queries, queries, pairs, pairs],
+        [shape((count, head_cols), bf16), shape((count, 2 * head_cols), f32)],
         [VMEM] * 8,
         kv_tall, qg_tall, top_bias, bottom_bias, gather, spread, core_query, core_pair,
     )
     own = count // tp
-    reduced = []
-    for half, operands in enumerate(
-        (
-            (leftward, from_left, left_query, left_pair, left_bias),
-            (rightward, from_right, right_query, right_pair, right_bias),
-        )
-    ):
-        sent, kept = near_call(
-            functools.partial(side_kernel, half),
-            ("left_side", "right_side")[half],
-            [shape((own, model_width), bf16), shape((own, model_width), f32)],
-            [SMEM] + [VMEM] * 7,
-            place, *operands, spread, weight,
-            scratch=[pltpu.VMEM((count // 2, 3 * head_cols), bf16)],
-        )
-        received = lax.ppermute(sent, "tp", [(i, i ^ 1) for i in range(tp)])
-        sent, kept = near_call(
-            fold_kernel,
-            ("left_fold", "right_fold")[half],
-            [shape((own // 2, model_width), bf16), shape((own // 2, model_width), f32)],
-            [VMEM] * 2,
-            kept, received,
-        )
-        reduced += [kept, lax.ppermute(sent, "tp", [(i, i ^ 2) for i in range(tp)])]
-    return near_call(
+    sent, stacked = near_call(
+        sides_kernel,
+        "sides",
+        [shape((2 * own, model_width), bf16), shape((count, 3 * head_cols), bf16)],
+        [SMEM] + [VMEM] * 10,
+        place, leftward, from_left, rightward, from_right, query_mid, pair_mid, left_bias,
+        right_bias, spread, weight,
+    )
+    received = lax.ppermute(sent, "tp", [(i, i ^ 1) for i in range(tp)])
+    kept = near_call(
+        keep_kernel,
+        "keep",
+        shape((2 * own, model_width), f32),
+        [SMEM] + [VMEM] * 2,
+        place, stacked, weight,
+    )
+    sent, kept = near_call(
+        fold_kernel,
+        "fold",
+        [shape((own, model_width), bf16), shape((own, model_width), f32)],
+        [VMEM] * 2,
+        kept, received,
+    )
+    received = lax.ppermute(sent, "tp", [(i, i ^ 2) for i in range(tp)])
+    result = near_call(
         finish_kernel,
         "finish",
-        jax.ShapeDtypeStruct((own // tile_cols, tile_cols, model_width), f32),
-        [SMEM] + [VMEM] * 7,
-        place, *reduced, flat_latent, gain, flat_cotangent,
-    )
+        jax.ShapeDtypeStruct((own, model_width), f32),
+        [SMEM] + [VMEM] * 5,
+        place, kept, received, flat_latent, gain, flat_cotangent,
+    )
+    return result.reshape(own // tile_cols, tile_cols, model_width)
 
 
 def solution(mesh):

time: 54.8 us -> 56.9 us (1.038)
  the two profiles are of different devices: /device:TPU:250 before, /device:TPU:314 now
where the time goes in v7:
time: 56.9 us; the launch traced here: 56.6 us
  waiting for transfers between devices  24.5 us (43%)
  starting transfers between devices  20.5 us (36%)
  Pallas kernels  11.4 us (20%)
    pallas_call x7, Pallas kernels, near_call(): pl.pallas_call(kernel, out_shape=outs, in_specs=places, out_specs=jax.tre...  8.27 us
    ppermute x2, starting transfers between devices, paired(): return lax.ppermute(block, axis, route)  7.66 us
    ppermute x2, waiting for transfers between devices, moved(): return lax.ppermute(block, axis, route)  6.78 us
    ppermute x1, waiting for transfers between devices, per_device(): received = lax.ppermute(sent, 'tp', [(i, i ^ 2) for i in range(tp)])  6.31 us
    ppermute x1, waiting for transfers between devices, per_device(): received = lax.ppermute(sent, 'tp', [(i, i ^ 1) for i in range(tp)])  6.08 us
    ppermute x2, starting transfers between devices, moved(): return lax.ppermute(block, axis, route)  5.97 us
    ppermute x2, waiting for transfers between devices, paired(): return lax.ppermute(block, axis, route)  5.29 us
    ppermute x1, starting transfers between devices, per_device(): received = lax.ppermute(sent, 'tp', [(i, i ^ 2) for i in range(tp)])  3.7 us
  transfers between devices with their start and end apart: 6, of which 5 were waited for; matrix products, arithmetic and copies ran while one was open for 0% of the time, Pallas kernels for 7%

profile of v7, /device:TPU:314, one launch (start us, length us, event | category | flops | bytes accessed | tf_op | source)
XLA Modules:
  0.0 56.6 jit_solution(482917723497828621)
XLA Ops:
  0.0 0.0 copy-start.1
  0.0 0.0 copy-start.2
  0.0 0.0 copy-start.5
  0.0 3.2 %project.1 = (bf16[256,512]{1,0:T(8,128)(2,1)S(1)}, bf16[256,512]{1,0:T(8,128)(2,1)S(1)}, bf16[144,512]{1,0:T(8,128)(2,1)S(1)}, bf16[144,512]{1,0:T(8,128)(2,1)S(1)}) custom-call(s32[1]{0:T(128)} %bitcast.1.row, s32[1]{0:T(128)} %bitcast.2.col, s32[1]{0:T(128)} %bitcast.place, bf16[256,1024]{1,0:T(8,128)(2,1)} %bitcast.11, f32[1,1024]{1,0:T(1,128)} %bitcast.15, ...), custom_call_target="tpu_custom_call" | custom-call | tf_op jit(solution)/shard_map/project/pallas_call | solution.py:419
  3.2 4.2 %collective-permute-start = (bf16[144,512]{1,0:T(8,128)(2,1)S(1)}, bf16[144,512]{1,0:T(8,128)(2,1)S(1)}, u32[]{:S(2)}, u32[]{:S(2)}) collective-permute-start(bf16[144,512]{1,0:T(8,128)(2,1)S(1)} %get-tuple-element.27), channel_id=1, source_target_pairs={{32,64},{64,32},{96,128},{128,96},{160,192},{192,160},{224,256},{2... | collective-permute-start | bytes 442376 | tf_op jit(solution)/shard_map/ppermute | solution.py:394
  7.3 3.5 %collective-permute-start.1 = (bf16[144,512]{1,0:T(8,128)(2,1)S(1)}, bf16[144,512]{1,0:T(8,128)(2,1)S(1)}, u32[]{:S(2)}, u32[]{:S(2)}) collective-permute-start(bf16[144,512]{1,0:T(8,128)(2,1)S(1)} %get-tuple-element.28), channel_id=1, source_target_pairs={{0,32},{32,0},{64,96},{96,64},{128,160},{160,128},{192,224},{224,1... | collective-permute-start | bytes 442376 | tf_op jit(solution)/shard_map/ppermute | solution.py:394
  10.8 0.0 copy-done.1
  10.9 0.0 copy-done.2
  10.9 0.0 copy-done.5
  10.9 2.1 %core.1 = (bf16[256,256]{1,0:T(8,128)(2,1)S(1)}, f32[256,512]{1,0:T(8,128)S(1)}, f32[192,256]{1,0:T(8,128)S(1)}, f32[192,256]{1,0:T(8,128)S(1)}, f32[352,640]{1,0:T(8,128)S(1)}, /*index=5*/f32[352,640]{1,0:T(8,128)S(1)}) custom-call(s32[1]{0:T(128)} %bitcast.1.row, s32[1]{0:T(128)} %bitcast.2.col, bf16[256,512]{1,0:T(8,128)(2,1)S(1)} %get-tuple-element.25.kv, ...), custom_call_target="tpu_custom_call" | custom-call | tf_op jit(solution)/shard_map/core/pallas_call | solution.py:53
  13.0 5.3 %collective-permute-done.far = bf16[144,512]{1,0:T(8,128)(2,1)S(1)} collective-permute-done((bf16[144,512]{1,0:T(8,128)(2,1)S(1)}, bf16[144,512]{1,0:T(8,128)(2,1)S(1)}, u32[]{:S(2)}, u32[]{:S(2)}) %collective-permute-start) | collective-permute-done | bytes 147488 | tf_op jit(solution)/shard_map/ppermute | solution.py:394
  18.3 0.0 collective-permute-done.1.near
  18.3 0.5 edges.1
  18.8 0.0 copy-start
  18.8 2.1 %collective-permute-start.3 = (bf16[256,512]{1,0:T(8,128)(2,1)S(1)}, bf16[256,512]{1,0:T(8,128)(2,1)S(1)}, u32[]{:S(2)}, u32[]{:S(2)}) collective-permute-start(bf16[256,512]{1,0:T(8,128)(2,1)S(1)} %get-tuple-element.30.leftward), channel_id=1, source_target_pairs={{4,0},{8,4},{12,8},{16,12},{20,16},{24,20},{28,24},{5,1},{9,5},{13... | collective-permute-start | bytes 786440 | tf_op jit(solution)/shard_map/ppermute | solution.py:400
  20.9 3.9 %collective-permute-start.2 = (bf16[256,512]{1,0:T(8,128)(2,1)S(1)}, bf16[256,512]{1,0:T(8,128)(2,1)S(1)}, u32[]{:S(2)}, u32[]{:S(2)}) collective-permute-start(bf16[256,512]{1,0:T(8,128)(2,1)S(1)} %get-tuple-element.31.rightward), channel_id=1, source_target_pairs={{0,4},{4,8},{8,12},{12,16},{16,20},{20,24},{24,28},{1,5},{5,9},{9,... | collective-permute-start | bytes 786440 | tf_op jit(solution)/shard_map/ppermute | solution.py:400
  24.8 1.3 %middle.1 = (bf16[256,256]{1,0:T(8,128)(2,1)S(1)}, f32[256,512]{1,0:T(8,128)S(1)}) custom-call(bf16[448,512]{1,0:T(8,128)(2,1)S(1)} %get-tuple-element.32.kv, bf16[352,512]{1,0:T(8,128)(2,1)S(1)} %get-tuple-element.33.qg, f32[192,256]{1,0:T(8,128)S(1)} %get-tuple-element.34.top_bias, f32[192,256]{1,0:T(8,128)S(1)} %get-tuple-element.35.bottom_bias, ...), custom_call_target="tpu_custom_call" | custom-call | tf_op jit(solution)/shard_map/middle/pallas_call | solution.py:53
  26.1 3.6 %collective-permute-done.3.from_right = bf16[256,512]{1,0:T(8,128)(2,1)S(1)} collective-permute-done((bf16[256,512]{1,0:T(8,128)(2,1)S(1)}, bf16[256,512]{1,0:T(8,128)(2,1)S(1)}, u32[]{:S(2)}, u32[]{:S(2)}) %collective-permute-start.3) | collective-permute-done | bytes 262176 | tf_op jit(solution)/shard_map/ppermute | solution.py:400
  29.8 3.1 %collective-permute-done.2.from_left = bf16[256,512]{1,0:T(8,128)(2,1)S(1)} collective-permute-done((bf16[256,512]{1,0:T(8,128)(2,1)S(1)}, bf16[256,512]{1,0:T(8,128)(2,1)S(1)}, u32[]{:S(2)}, u32[]{:S(2)}) %collective-permute-start.2) | collective-permute-done | bytes 262176 | tf_op jit(solution)/shard_map/ppermute | solution.py:400
  32.9 0.0 copy-done
  32.9 2.7 %sides.1 = (bf16[128,1024]{1,0:T(8,128)(2,1)S(1)}, bf16[256,768]{1,0:T(8,128)(2,1)S(1)}) custom-call(s32[1]{0:T(128)} %bitcast.place, bf16[256,512]{1,0:T(8,128)(2,1)S(1)} %get-tuple-element.30.leftward, bf16[256,512]{1,0:T(8,128)(2,1)S(1)} %collective-permute-done.2.from_left, bf16[256,512]{1,0:T(8,128)(2,1)S(1)} %get-tuple-element.31.rightward, ...), custom_call_target="tpu_custom_call" | custom-call | tf_op jit(solution)/shard_map/sides/pallas_call | solution.py:53
  35.6 3.2 %collective-permute-start.4 = (bf16[128,1024]{1,0:T(8,128)(2,1)S(1)}, bf16[128,1024]{1,0:T(8,128)(2,1)S(1)}, u32[]{:S(2)}, u32[]{:S(2)}) collective-permute-start(bf16[128,1024]{1,0:T(8,128)(2,1)S(1)} %get-tuple-element.42), channel_id=1, source_target_pairs={{0,1},{1,0},{2,3},{3,2},{4,5},{5,4},{6,7},{7,6},{8,9},{9,8},{10,11... | collective-permute-start | bytes 786440 | tf_op jit(solution)/shard_map/ppermute | solution.py:482
  38.8 0.0 copy-start.3
  38.8 0.0 copy-start.4
  38.9 0.0 copy-start.6
  38.9 0.6 %keep.1.kept = f32[128,1024]{1,0:T(8,128)S(1)} custom-call(s32[1]{0:T(128)} %bitcast.place, bf16[256,768]{1,0:T(8,128)(2,1)S(1)} %get-tuple-element.41.stacked, bf16[3,1024,256]{2,1,0:T(8,128)(2,1)S(1)} %bitcast.10), custom_call_target="tpu_custom_call" | custom-call | tf_op jit(solution)/shard_map/keep/pallas_call | solution.py:53
  39.5 6.1 %collective-permute-done.4.received = bf16[128,1024]{1,0:T(8,128)(2,1)S(1)} collective-permute-done((bf16[128,1024]{1,0:T(8,128)(2,1)S(1)}, bf16[128,1024]{1,0:T(8,128)(2,1)S(1)}, u32[]{:S(2)}, u32[]{:S(2)}) %collective-permute-start.4) | collective-permute-done | bytes 262176 | tf_op jit(solution)/shard_map/ppermute | solution.py:482
  45.7 3.7 %collective-permute-start.5 = (bf16[64,1024]{1,0:T(8,128)(2,1)S(1)}, bf16[64,1024]{1,0:T(8,128)(2,1)S(1)}, u32[]{:S(2)}, u32[]{:S(2)}) collective-permute-start(bf16[64,1024]{1,0:T(8,128)(2,1)S(1)} %get-tuple-element.44), channel_id=1, source_target_pairs={{0,2},{1,3},{2,0},{3,1},{4,6},{5,7},{6,4},{7,5},{8,10},{9,11},{10,... | collective-permute-start | bytes 393224 | tf_op jit(solution)/shard_map/ppermute | solution.py:497
  49.4 6.3 %collective-permute-done.5.received = bf16[64,1024]{1,0:T(8,128)(2,1)S(1)} collective-permute-done((bf16[64,1024]{1,0:T(8,128)(2,1)S(1)}, bf16[64,1024]{1,0:T(8,128)(2,1)S(1)}, u32[]{:S(2)}, u32[]{:S(2)}) %collective-permute-start.5) | collective-permute-done | bytes 131104 | tf_op jit(solution)/shard_map/ppermute | solution.py:497
  55.7 0.0 copy-done.3
  55.7 0.0 copy-done.4
  55.7 0.0 copy-done.6
  55.7 0.9 %finish.1 = f32[64,1024]{1,0:T(8,128)} custom-call(s32[1]{0:T(128)} %bitcast.place, f32[64,1024]{1,0:T(8,128)S(1)} %get-tuple-element.43.kept, bf16[64,1024]{1,0:T(8,128)(2,1)S(1)} %collective-permute-done.5.received, bf16[256,1024]{1,0:T(8,128)(2,1)S(1)} %bitcast.12, f32[1,1024]{1,0:T(1,128)S(1)} %bitcast.16, bf16[256,1024]{1,0:T(8,128)(2,1)S(1)} %bitcast.14), custom_call_target="tpu_custom_call" | custom-call | tf_op jit(solution)/shard_map/finish/pallas_call | solution.py:53
  (1 shorter events, 0.0 us)
Async XLA Ops:
  0.0 10.8 %copy-start.1 = (bf16[768,448]{1,0:T(8,128)(2,1)S(1)}, bf16[768,448]{1,0:T(8,128)(2,1)}, u32[]{:S(2)}) copy-start(bf16[768,448]{1,0:T(8,128)(2,1)} %constant.21.clone.gather) | copy-start | bytes 2064388
  0.0 10.9 %copy-start.2 = (bf16[768,256]{1,0:T(8,128)(2,1)S(1)}, bf16[768,256]{1,0:T(8,128)(2,1)}, u32[]{:S(2)}) copy-start(bf16[768,256]{1,0:T(8,128)(2,1)} %constant.22.clone.spread) | copy-start | bytes 1179652
  0.0 10.9 %copy-start.5 = (f32[8,2304]{1,0:T(8,128)S(1)}, f32[8,2304]{1,0:T(8,128)}, u32[]{:S(2)}) copy-start(f32[8,2304]{1,0:T(8,128)} %constant.23.clone.points) | copy-start | bytes 221188
  3.2 15.1 %collective-permute-start = (bf16[144,512]{1,0:T(8,128)(2,1)S(1)}, bf16[144,512]{1,0:T(8,128)(2,1)S(1)}, u32[]{:S(2)}, u32[]{:S(2)}) collective-permute-start(bf16[144,512]{1,0:T(8,128)(2,1)S(1)} %get-tuple-element.27), channel_id=1, source_target_pairs={{32,64},{64,32},{96,128},{128,96},{160,192},{192,160},{224,256},{2... | collective-permute-start | bytes 442376 | tf_op jit(solution)/shard_map/ppermute | solution.py:394
  7.3 11.0 %collective-permute-start.1 = (bf16[144,512]{1,0:T(8,128)(2,1)S(1)}, bf16[144,512]{1,0:T(8,128)(2,1)S(1)}, u32[]{:S(2)}, u32[]{:S(2)}) collective-permute-start(bf16[144,512]{1,0:T(8,128)(2,1)S(1)} %get-tuple-element.28), channel_id=1, source_target_pairs={{0,32},{32,0},{64,96},{96,64},{128,160},{160,128},{192,224},{224,1... | collective-permute-start | bytes 442376 | tf_op jit(solution)/shard_map/ppermute | solution.py:394
  18.8 14.1 %copy-start = (bf16[1024,3,256]{2,0,1:T(8,128)(2,1)S(1)}, bf16[1024,3,256]{2,0,1:T(8,128)(2,1)}, u32[]{:S(2)}) copy-start(bf16[1024,3,256]{2,0,1:T(8,128)(2,1)} %param.10) | copy-start | bytes 4718596
  18.8 11.0 %collective-permute-start.3 = (bf16[256,512]{1,0:T(8,128)(2,1)S(1)}, bf16[256,512]{1,0:T(8,128)(2,1)S(1)}, u32[]{:S(2)}, u32[]{:S(2)}) collective-permute-start(bf16[256,512]{1,0:T(8,128)(2,1)S(1)} %get-tuple-element.30.leftward), channel_id=1, source_target_pairs={{4,0},{8,4},{12,8},{16,12},{20,16},{24,20},{28,24},{5,1},{9,5},{13... | collective-permute-start | bytes 786440 | tf_op jit(solution)/shard_map/ppermute | solution.py:400
  20.9 12.1 %collective-permute-start.2 = (bf16[256,512]{1,0:T(8,128)(2,1)S(1)}, bf16[256,512]{1,0:T(8,128)(2,1)S(1)}, u32[]{:S(2)}, u32[]{:S(2)}) collective-permute-start(bf16[256,512]{1,0:T(8,128)(2,1)S(1)} %get-tuple-element.31.rightward), channel_id=1, source_target_pairs={{0,4},{4,8},{8,12},{12,16},{16,20},{20,24},{24,28},{1,5},{5,9},{9,... | collective-permute-start | bytes 786440 | tf_op jit(solution)/shard_map/ppermute | solution.py:400
  35.6 10.0 %collective-permute-start.4 = (bf16[128,1024]{1,0:T(8,128)(2,1)S(1)}, bf16[128,1024]{1,0:T(8,128)(2,1)S(1)}, u32[]{:S(2)}, u32[]{:S(2)}) collective-permute-start(bf16[128,1024]{1,0:T(8,128)(2,1)S(1)} %get-tuple-element.42), channel_id=1, source_target_pairs={{0,1},{1,0},{2,3},{3,2},{4,5},{5,4},{6,7},{7,6},{8,9},{9,8},{10,11... | collective-permute-start | bytes 786440 | tf_op jit(solution)/shard_map/ppermute | solution.py:482
  38.8 16.8 %copy-start.3 = (bf16[16,16,1024]{2,1,0:T(8,128)(2,1)S(1)}, bf16[16,16,1024]{2,1,0:T(8,128)(2,1)}, u32[]{:S(2)}) copy-start(bf16[16,16,1024]{2,1,0:T(8,128)(2,1)} %param.8) | copy-start | bytes 1572868
  38.8 16.8 %copy-start.4 = (bf16[16,16,1024]{2,1,0:T(8,128)(2,1)S(1)}, bf16[16,16,1024]{2,1,0:T(8,128)(2,1)}, u32[]{:S(2)}) copy-start(bf16[16,16,1024]{2,1,0:T(8,128)(2,1)} %param.12) | copy-start | bytes 1572868
  38.9 16.8 %copy-start.6 = (f32[1024]{0:T(1024)S(1)}, f32[1024]{0:T(1024)}, u32[]{:S(2)}) copy-start(f32[1024]{0:T(1024)} %param.9) | copy-start | bytes 12292
  45.7 10.0 %collective-permute-start.5 = (bf16[64,1024]{1,0:T(8,128)(2,1)S(1)}, bf16[64,1024]{1,0:T(8,128)(2,1)S(1)}, u32[]{:S(2)}, u32[]{:S(2)}) collective-permute-start(bf16[64,1024]{1,0:T(8,128)(2,1)S(1)} %get-tuple-element.44), channel_id=1, source_target_pairs={{0,2},{1,3},{2,0},{3,1},{4,6},{5,7},{6,4},{7,5},{8,10},{9,11},{10,... | collective-permute-start | bytes 393224 | tf_op jit(solution)/shard_map/ppermute | solution.py:497

commit v8 on v7

--- a/solution.py
+++ b/solution.py
@@ -322,22 +322,9 @@
         pair_out[:, first : first + width] = grad + core_pair[:, first : first + width]
 
 
-def back_projected(place, others, stacked, weight):
-    width = weight.shape[2]
-    block = stacked.shape[0] // 4
-    parts = []
-    for other in others:
-        first = pl.multiple_of(jnp.bitwise_xor(place[0], other) * block, block)
-        parts.append(stacked[pl.ds(first, block), :])
-    rows = jnp.concatenate(parts, axis=0)
-    total = nt(rows[:, :width], weight[0])
-    total += nt(rows[:, width : 2 * width], weight[1])
-    return total + nt(rows[:, 2 * width :], weight[2])
-
-
 def sides_kernel(
-    place, leftward, from_left, rightward, from_right, query_mid, pair_mid, left_bias, right_bias,
-    spread, weight, sent, stacked
+    leftward, from_left, rightward, from_right, query_mid, pair_mid, left_bias, right_bias,
+    spread, weight, partial
 ):
     width = query_mid.shape[1]
     own = slice(OWN_FROM, OWN_FROM + OWN_EDGE)
@@ -358,27 +345,21 @@
     key_spread, query_spread = (part_of(spread, SPREADS[name]) for name in ("keys", "queries"))
     pair = pair_mid[...] + (nn(key_spread, coarse) + nn(key_spread, fine))
     query_grad = query_mid[...].astype(f32) + nn(query_spread, query_side)
-    stacked[:, :width] = query_grad.astype(bf16)
-    stacked[:, width:] = pair.astype(bf16)
-    sent[...] = back_projected(place, (1, 3), stacked, weight).astype(bf16)
-
-
-def keep_kernel(place, stacked, weight, kept):
-    kept[...] = back_projected(place, (0, 2), stacked, weight)
-
-
-def fold_kernel(kept, received, sent, still):
-    block = sent.shape[0]
-    still[...] = kept[:block] + received[:block].astype(f32)
-    sent[...] = (kept[block:] + received[block:].astype(f32)).astype(bf16)
-
-
-def finish_kernel(place, kept, received, latent, gain, cotangent, result):
-    count = kept.shape[0]
+    pair = pair.astype(bf16)
+    total = nt(query_grad.astype(bf16), weight[0])
+    total += nt(pair[:, :width], weight[1])
+    total += nt(pair[:, width:], weight[2])
+    partial[...] = total.astype(bf16)
+
+
+def finish_kernel(place, received, latent, gain, cotangent, result):
+    count = received.shape[1]
     first = pl.multiple_of(place[0] * count, count)
     tokens = latent[pl.ds(first, count), :].astype(f32)
     upstream = cotangent[pl.ds(first, count), :].astype(f32)
-    summed = kept[...] + received[...].astype(f32)
+    summed = received[0].astype(f32)
+    for part in range(1, received.shape[0]):
+        summed += received[part].astype(f32)
     inverse = lax.rsqrt(jnp.mean(tokens * tokens, axis=-1, keepdims=True) + 1e-06)
     unit = tokens * inverse
     scaled = summed * gain[...]
@@ -471,36 +452,21 @@
         kv_tall, qg_tall, top_bias, bottom_bias, gather, spread, core_query, core_pair,
     )
     own = count // tp
-    sent, stacked = near_call(
+    partial = near_call(
         sides_kernel,
         "sides",
-        [shape((2 * own, model_width), bf16), shape((count, 3 * head_cols), bf16)],
-        [SMEM] + [VMEM] * 10,
-        place, leftward, from_left, rightward, from_right, query_mid, pair_mid, left_bias,
-        right_bias, spread, weight,
-    )
-    received = lax.ppermute(sent, "tp", [(i, i ^ 1) for i in range(tp)])
-    kept = near_call(
-        keep_kernel,
-        "keep",
-        shape((2 * own, model_width), f32),
-        [SMEM] + [VMEM] * 2,
-        place, stacked, weight,
-    )
-    sent, kept = near_call(
-        fold_kernel,
-        "fold",
-        [shape((own, model_width), bf16), shape((own, model_width), f32)],
-        [VMEM] * 2,
-        kept, received,
-    )
-    received = lax.ppermute(sent, "tp", [(i, i ^ 2) for i in range(tp)])
+        shape((count, model_width), bf16),
+        [VMEM] * 10,
+        leftward, from_left, rightward, from_right, query_mid, pair_mid, left_bias, right_bias,
+        spread, weight,
+    )
+    received = lax.all_to_all(partial.reshape(tp, own, model_width), "tp", 0, 0)
     result = near_call(
         finish_kernel,
         "finish",
         jax.ShapeDtypeStruct((own, model_width), f32),
-        [SMEM] + [VMEM] * 5,
-        place, kept, received, flat_latent, gain, flat_cotangent,
+        [SMEM] + [VMEM] * 4,
+        place, received, flat_latent, gain, flat_cotangent,
     )
     return result.reshape(own // tile_cols, tile_cols, model_width)
 

time: 56.9 us -> 53.6 us (0.942)
  blocking collectives: 0 us -> 17.1 us
  waiting for transfers between devices: 24.5 us -> 12.1 us
  starting transfers between devices: 20.5 us -> 13.6 us
  Pallas kernels: 11.4 us -> 10.5 us
    all_to_all x0 -> x1, blocking collectives: none -> 17.1 us  [per_device(): received = lax.all_to_all(partial.reshape(tp, own, model_width), 'tp', 0, 0)]
    ppermute x2 -> x0, waiting for transfers between devices: 12.4 us -> none  [the longest x1 6.31 us: per_device(): received = lax.ppermute(sent, 'tp', [(i, i ^ 2) for i in range(tp)])]
    ppermute x2 -> x0, starting transfers between devices: 6.91 us -> none  [the longest x1 3.7 us: per_device(): received = lax.ppermute(sent, 'tp', [(i, i ^ 2) for i in range(tp)])]
    pallas_call x7 -> x5, Pallas kernels: 8.27 us -> 7.32 us  [near_call(): pl.pallas_call(kernel, out_shape=outs, in_specs=places, out_specs=jax.tre...]
  transfers between devices with their start and end apart: 6 -> 4, of which waited for: 5 -> 3; matrix products, arithmetic and copies ran while one was open for 0% -> 0% of each run, Pallas kernels for 7% -> 7%
where the time goes in v8:
time: 53.6 us; the launch traced here: 53.4 us
  blocking collectives  17.1 us (32%)
  starting transfers between devices  13.6 us (25%)
  waiting for transfers between devices  12.1 us (23%)
  Pallas kernels  10.5 us (20%)
    all_to_all x1, blocking collectives, per_device(): received = lax.all_to_all(partial.reshape(tp, own, model_width), 'tp', 0, 0)  17.1 us
    ppermute x2, starting transfers between devices, paired(): return lax.ppermute(block, axis, route)  7.66 us
    pallas_call x5, Pallas kernels, near_call(): pl.pallas_call(kernel, out_shape=outs, in_specs=places, out_specs=jax.tre...  7.32 us
    ppermute x2, waiting for transfers between devices, moved(): return lax.ppermute(block, axis, route)  6.78 us
    ppermute x2, starting transfers between devices, moved(): return lax.ppermute(block, axis, route)  5.97 us
    ppermute x2, waiting for transfers between devices, paired(): return lax.ppermute(block, axis, route)  5.29 us
    pallas_call x1, Pallas kernels, per_device(): pl.pallas_call(project_kernel, out_shape=[shape((count, 2 * head_cols), b...  3.15 us
  transfers between devices with their start and end apart: 4, of which 3 were waited for; matrix products, arithmetic and copies ran while one was open for 0% of the time, Pallas kernels for 7%

profile of v8, /device:TPU:314, one launch (start us, length us, event | category | flops | bytes accessed | tf_op | source)
XLA Modules:
  0.0 53.4 jit_solution(3772472390960993057)
XLA Ops:
  0.0 0.0 copy-start
  0.0 0.0 copy-start.2
  0.0 0.0 copy-start.5
  0.0 3.2 %project.1 = (bf16[256,512]{1,0:T(8,128)(2,1)S(1)}, bf16[256,512]{1,0:T(8,128)(2,1)S(1)}, bf16[144,512]{1,0:T(8,128)(2,1)S(1)}, bf16[144,512]{1,0:T(8,128)(2,1)S(1)}) custom-call(s32[1]{0:T(128)} %bitcast.1.row, s32[1]{0:T(128)} %bitcast.2.col, s32[1]{0:T(128)} %bitcast.place, bf16[256,1024]{1,0:T(8,128)(2,1)} %bitcast.12, f32[1,1024]{1,0:T(1,128)} %bitcast.16, ...), custom_call_target="tpu_custom_call" | custom-call | tf_op jit(solution)/shard_map/project/pallas_call | solution.py:400
  3.2 4.2 %collective-permute-start = (bf16[144,512]{1,0:T(8,128)(2,1)S(1)}, bf16[144,512]{1,0:T(8,128)(2,1)S(1)}, u32[]{:S(2)}, u32[]{:S(2)}) collective-permute-start(bf16[144,512]{1,0:T(8,128)(2,1)S(1)} %get-tuple-element.23), channel_id=1, source_target_pairs={{32,64},{64,32},{96,128},{128,96},{160,192},{192,160},{224,256},{2... | collective-permute-start | bytes 442376 | tf_op jit(solution)/shard_map/ppermute | solution.py:375
  7.3 3.5 %collective-permute-start.1 = (bf16[144,512]{1,0:T(8,128)(2,1)S(1)}, bf16[144,512]{1,0:T(8,128)(2,1)S(1)}, u32[]{:S(2)}, u32[]{:S(2)}) collective-permute-start(bf16[144,512]{1,0:T(8,128)(2,1)S(1)} %get-tuple-element.24), channel_id=1, source_target_pairs={{0,32},{32,0},{64,96},{96,64},{128,160},{160,128},{192,224},{224,1... | collective-permute-start | bytes 442376 | tf_op jit(solution)/shard_map/ppermute | solution.py:375
  10.8 0.0 copy-done
  10.9 0.0 copy-done.2
  10.9 0.0 copy-done.5
  10.9 2.1 %core.1 = (bf16[256,256]{1,0:T(8,128)(2,1)S(1)}, f32[256,512]{1,0:T(8,128)S(1)}, f32[192,256]{1,0:T(8,128)S(1)}, f32[192,256]{1,0:T(8,128)S(1)}, f32[352,640]{1,0:T(8,128)S(1)}, /*index=5*/f32[352,640]{1,0:T(8,128)S(1)}) custom-call(s32[1]{0:T(128)} %bitcast.1.row, s32[1]{0:T(128)} %bitcast.2.col, bf16[256,512]{1,0:T(8,128)(2,1)S(1)} %get-tuple-element.21.kv, ...), custom_call_target="tpu_custom_call" | custom-call | tf_op jit(solution)/shard_map/core/pallas_call | solution.py:53
  13.0 5.3 %collective-permute-done.far = bf16[144,512]{1,0:T(8,128)(2,1)S(1)} collective-permute-done((bf16[144,512]{1,0:T(8,128)(2,1)S(1)}, bf16[144,512]{1,0:T(8,128)(2,1)S(1)}, u32[]{:S(2)}, u32[]{:S(2)}) %collective-permute-start) | collective-permute-done | bytes 147488 | tf_op jit(solution)/shard_map/ppermute | solution.py:375
  18.3 0.0 collective-permute-done.1.near
  18.3 0.5 edges.1
  18.8 0.0 copy-start.1
  18.8 2.1 %collective-permute-start.3 = (bf16[256,512]{1,0:T(8,128)(2,1)S(1)}, bf16[256,512]{1,0:T(8,128)(2,1)S(1)}, u32[]{:S(2)}, u32[]{:S(2)}) collective-permute-start(bf16[256,512]{1,0:T(8,128)(2,1)S(1)} %get-tuple-element.26.leftward), channel_id=1, source_target_pairs={{4,0},{8,4},{12,8},{16,12},{20,16},{24,20},{28,24},{5,1},{9,5},{13... | collective-permute-start | bytes 786440 | tf_op jit(solution)/shard_map/ppermute | solution.py:381
  20.8 3.9 %collective-permute-start.2 = (bf16[256,512]{1,0:T(8,128)(2,1)S(1)}, bf16[256,512]{1,0:T(8,128)(2,1)S(1)}, u32[]{:S(2)}, u32[]{:S(2)}) collective-permute-start(bf16[256,512]{1,0:T(8,128)(2,1)S(1)} %get-tuple-element.27.rightward), channel_id=1, source_target_pairs={{0,4},{4,8},{8,12},{12,16},{16,20},{20,24},{24,28},{1,5},{5,9},{9,... | collective-permute-start | bytes 786440 | tf_op jit(solution)/shard_map/ppermute | solution.py:381
  24.8 1.3 %middle.1 = (bf16[256,256]{1,0:T(8,128)(2,1)S(1)}, f32[256,512]{1,0:T(8,128)S(1)}) custom-call(bf16[448,512]{1,0:T(8,128)(2,1)S(1)} %get-tuple-element.28.kv, bf16[352,512]{1,0:T(8,128)(2,1)S(1)} %get-tuple-element.29.qg, f32[192,256]{1,0:T(8,128)S(1)} %get-tuple-element.30.top_bias, f32[192,256]{1,0:T(8,128)S(1)} %get-tuple-element.31.bottom_bias, ...), custom_call_target="tpu_custom_call" | custom-call | tf_op jit(solution)/shard_map/middle/pallas_call | solution.py:53
  26.1 3.6 %collective-permute-done.3.from_right = bf16[256,512]{1,0:T(8,128)(2,1)S(1)} collective-permute-done((bf16[256,512]{1,0:T(8,128)(2,1)S(1)}, bf16[256,512]{1,0:T(8,128)(2,1)S(1)}, u32[]{:S(2)}, u32[]{:S(2)}) %collective-permute-start.3) | collective-permute-done | bytes 262176 | tf_op jit(solution)/shard_map/ppermute | solution.py:381
  29.8 3.1 %collective-permute-done.2.from_left = bf16[256,512]{1,0:T(8,128)(2,1)S(1)} collective-permute-done((bf16[256,512]{1,0:T(8,128)(2,1)S(1)}, bf16[256,512]{1,0:T(8,128)(2,1)S(1)}, u32[]{:S(2)}, u32[]{:S(2)}) %collective-permute-start.2) | collective-permute-done | bytes 262176 | tf_op jit(solution)/shard_map/ppermute | solution.py:381
  32.9 0.0 copy-done.1
  32.9 0.0 copy-start.3
  32.9 0.0 copy-start.4
  32.9 0.0 copy-start.6
  32.9 2.5 %sides.1 = bf16[256,1024]{1,0:T(8,128)(2,1)S(1)} custom-call(bf16[256,512]{1,0:T(8,128)(2,1)S(1)} %get-tuple-element.26.leftward, bf16[256,512]{1,0:T(8,128)(2,1)S(1)} %collective-permute-done.2.from_left, bf16[256,512]{1,0:T(8,128)(2,1)S(1)} %get-tuple-element.27.rightward, bf16[256,512]{1,0:T(8,128)(2,1)S(1)} %collective-permute-done.3.from_right, ...), custom_call_target="tpu_custom_call" | custom-call | tf_op jit(solution)/shard_map/sides/pallas_call | solution.py:53
  35.4 17.1 %all_to_all.5.received = bf16[4,64,1024]{2,1,0:T(8,128)(2,1)S(1)} all-to-all(bf16[4,64,1024]{2,1,0:T(8,128)(2,1)S(1)} %bitcast.11), channel_id=1, replica_groups=mesh['row'=16,'col'=8,'tp'=4] {'tp'}, dimensions={0} | all-to-all | bytes 1048576 | tf_op jit(solution)/shard_map/all_to_all | solution.py:463
  52.4 0.0 copy-done.3
  52.5 0.0 copy-done.4
  52.5 0.0 copy-done.6
  52.5 0.9 %finish.1 = f32[64,1024]{1,0:T(8,128)} custom-call(s32[1]{0:T(128)} %bitcast.place, bf16[4,64,1024]{2,1,0:T(8,128)(2,1)S(1)} %all_to_all.5.received, bf16[256,1024]{1,0:T(8,128)(2,1)S(1)} %bitcast.13, f32[1,1024]{1,0:T(1,128)S(1)} %bitcast.17, bf16[256,1024]{1,0:T(8,128)(2,1)S(1)} %bitcast.15), custom_call_target="tpu_custom_call" | custom-call | tf_op jit(solution)/shard_map/finish/pallas_call | solution.py:53
Async XLA Ops:
  0.0 10.8 %copy-start = (bf16[768,448]{1,0:T(8,128)(2,1)S(1)}, bf16[768,448]{1,0:T(8,128)(2,1)}, u32[]{:S(2)}) copy-start(bf16[768,448]{1,0:T(8,128)(2,1)} %constant.21.clone.gather) | copy-start | bytes 2064388
  0.0 10.9 %copy-start.2 = (bf16[768,256]{1,0:T(8,128)(2,1)S(1)}, bf16[768,256]{1,0:T(8,128)(2,1)}, u32[]{:S(2)}) copy-start(bf16[768,256]{1,0:T(8,128)(2,1)} %constant.22.clone.spread) | copy-start | bytes 1179652
  0.0 10.9 %copy-start.5 = (f32[8,2304]{1,0:T(8,128)S(1)}, f32[8,2304]{1,0:T(8,128)}, u32[]{:S(2)}) copy-start(f32[8,2304]{1,0:T(8,128)} %constant.23.clone.points) | copy-start | bytes 221188
  3.2 15.1 %collective-permute-start = (bf16[144,512]{1,0:T(8,128)(2,1)S(1)}, bf16[144,512]{1,0:T(8,128)(2,1)S(1)}, u32[]{:S(2)}, u32[]{:S(2)}) collective-permute-start(bf16[144,512]{1,0:T(8,128)(2,1)S(1)} %get-tuple-element.23), channel_id=1, source_target_pairs={{32,64},{64,32},{96,128},{128,96},{160,192},{192,160},{224,256},{2... | collective-permute-start | bytes 442376 | tf_op jit(solution)/shard_map/ppermute | solution.py:375
  7.3 11.0 %collective-permute-start.1 = (bf16[144,512]{1,0:T(8,128)(2,1)S(1)}, bf16[144,512]{1,0:T(8,128)(2,1)S(1)}, u32[]{:S(2)}, u32[]{:S(2)}) collective-permute-start(bf16[144,512]{1,0:T(8,128)(2,1)S(1)} %get-tuple-element.24), channel_id=1, source_target_pairs={{0,32},{32,0},{64,96},{96,64},{128,160},{160,128},{192,224},{224,1... | collective-permute-start | bytes 442376 | tf_op jit(solution)/shard_map/ppermute | solution.py:375
  18.8 14.1 %copy-start.1 = (bf16[1024,3,256]{2,0,1:T(8,128)(2,1)S(1)}, bf16[1024,3,256]{2,0,1:T(8,128)(2,1)}, u32[]{:S(2)}) copy-start(bf16[1024,3,256]{2,0,1:T(8,128)(2,1)} %param.10) | copy-start | bytes 4718596
  18.8 11.0 %collective-permute-start.3 = (bf16[256,512]{1,0:T(8,128)(2,1)S(1)}, bf16[256,512]{1,0:T(8,128)(2,1)S(1)}, u32[]{:S(2)}, u32[]{:S(2)}) collective-permute-start(bf16[256,512]{1,0:T(8,128)(2,1)S(1)} %get-tuple-element.26.leftward), channel_id=1, source_target_pairs={{4,0},{8,4},{12,8},{16,12},{20,16},{24,20},{28,24},{5,1},{9,5},{13... | collective-permute-start | bytes 786440 | tf_op jit(solution)/shard_map/ppermute | solution.py:381
  20.8 12.1 %collective-permute-start.2 = (bf16[256,512]{1,0:T(8,128)(2,1)S(1)}, bf16[256,512]{1,0:T(8,128)(2,1)S(1)}, u32[]{:S(2)}, u32[]{:S(2)}) collective-permute-start(bf16[256,512]{1,0:T(8,128)(2,1)S(1)} %get-tuple-element.27.rightward), channel_id=1, source_target_pairs={{0,4},{4,8},{8,12},{12,16},{16,20},{20,24},{24,28},{1,5},{5,9},{9,... | collective-permute-start | bytes 786440 | tf_op jit(solution)/shard_map/ppermute | solution.py:381
  32.9 19.5 %copy-start.3 = (bf16[16,16,1024]{2,1,0:T(8,128)(2,1)S(1)}, bf16[16,16,1024]{2,1,0:T(8,128)(2,1)}, u32[]{:S(2)}) copy-start(bf16[16,16,1024]{2,1,0:T(8,128)(2,1)} %param.8) | copy-start | bytes 1572868
  32.9 19.5 %copy-start.4 = (bf16[16,16,1024]{2,1,0:T(8,128)(2,1)S(1)}, bf16[16,16,1024]{2,1,0:T(8,128)(2,1)}, u32[]{:S(2)}) copy-start(bf16[16,16,1024]{2,1,0:T(8,128)(2,1)} %param.12) | copy-start | bytes 1572868
  32.9 19.5 %copy-start.6 = (f32[1024]{0:T(1024)S(1)}, f32[1024]{0:T(1024)}, u32[]{:S(2)}) copy-start(f32[1024]{0:T(1024)} %param.9) | copy-start | bytes 12292

commit v9 on v8

--- a/solution.py
+++ b/solution.py
@@ -16,8 +16,8 @@
 TALL = SIDE + 2 * RADIUS
 KV_ROWS = REACH * SIDE
 QG_ROWS = RADIUS * SIDE
-KV_EDGE = 176
-QG_EDGE = 80
+KV_EDGE = 168
+QG_EDGE = 72
 INNER = range(RADIUS, SIDE - RADIUS)
 ALONG = range(SIDE)
 TOP = range(-RADIUS, RADIUS)
@@ -63,6 +63,10 @@
 
 def nt(a, b):
     return lax.dot_general(a, b, (((1,), (1,)), ((), ())), preferred_element_type=f32)
+
+
+def tn(a, b):
+    return lax.dot_general(a, b, (((0,), (0,)), ((), ())), preferred_element_type=f32)
 
 
 def nn(a, b):
@@ -267,7 +271,7 @@
     count = groups[0].shape[0]
     heads = width // HEAD_DIM
     used = -(-count * heads // LANES) * LANES
-    stacked = nn(key.astype(f32).T.astype(bf16), score_grads[:, :used]).T
+    stacked = tn(score_grads[:, :used], key)
     lanes = lax.broadcasted_iota(jnp.int32, (1, width), 1) // HEAD_DIM
     query_grad = stacked[:count]
     for head in range(1, heads):
@@ -322,24 +326,26 @@
         pair_out[:, first : first + width] = grad + core_pair[:, first : first + width]
 
 
+def side_grads(mine, theirs, bias):
+    own = slice(OWN_FROM, OWN_FROM + OWN_EDGE)
+    kv = jnp.concatenate([mine[:KV_EDGE], theirs[:KV_EDGE]], axis=0)
+    groups = [mine[KV_EDGE:], theirs[KV_EDGE:]]
+    query_grad, key_grad, value_grad = attention(bias[...], kv, groups, own)
+    return query_grad.astype(bf16), jnp.concatenate([key_grad, value_grad], axis=1)
+
+
+def right_kernel(rightward, from_right, right_bias, query_out, pair_out):
+    query_out[...], pair_out[...] = side_grads(rightward, from_right, right_bias)
+
+
 def sides_kernel(
-    leftward, from_left, rightward, from_right, query_mid, pair_mid, left_bias, right_bias,
-    spread, weight, partial
+    leftward, from_left, left_bias, right_query, right_pair, query_mid, pair_mid, spread, weight,
+    partial
 ):
     width = query_mid.shape[1]
-    own = slice(OWN_FROM, OWN_FROM + OWN_EDGE)
-    query_parts, pair_parts = [], []
-    for mine, theirs, bias in (
-        (leftward, from_left, left_bias),
-        (rightward, from_right, right_bias),
-    ):
-        kv = jnp.concatenate([mine[:KV_EDGE], theirs[:KV_EDGE]], axis=0)
-        groups = [mine[KV_EDGE:], theirs[KV_EDGE:]]
-        query_grad, key_grad, value_grad = attention(bias[...], kv, groups, own)
-        query_parts.append(query_grad)
-        pair_parts.append(jnp.concatenate([key_grad, value_grad], axis=1))
-    query_side = jnp.concatenate(query_parts, axis=0).astype(bf16)
-    pair_side = jnp.concatenate(pair_parts, axis=0)
+    left_query, left_pair = side_grads(leftward, from_left, left_bias)
+    query_side = jnp.concatenate([left_query, right_query[...]], axis=0)
+    pair_side = jnp.concatenate([left_pair, right_pair[...]], axis=0)
     coarse = pair_side.astype(bf16)
     fine = (pair_side - coarse.astype(f32)).astype(bf16)
     key_spread, query_spread = (part_of(spread, SPREADS[name]) for name in ("keys", "queries"))
@@ -452,13 +458,20 @@
         kv_tall, qg_tall, top_bias, bottom_bias, gather, spread, core_query, core_pair,
     )
     own = count // tp
+    right_query, right_pair = near_call(
+        right_kernel,
+        "right_side",
+        [shape((QG_EDGE, head_cols), bf16), shape((OWN_EDGE, 2 * head_cols), f32)],
+        [VMEM] * 3,
+        rightward, from_right, right_bias,
+    )
     partial = near_call(
         sides_kernel,
         "sides",
         shape((count, model_width), bf16),
-        [VMEM] * 10,
-        leftward, from_left, rightward, from_right, query_mid, pair_mid, left_bias, right_bias,
-        spread, weight,
+        [VMEM] * 9,
+        leftward, from_left, left_bias, right_query, right_pair, query_mid, pair_mid, spread,
+        weight,
     )
     received = lax.all_to_all(partial.reshape(tp, own, model_width), "tp", 0, 0)
     result = near_call(

time: 53.6 us -> 52.4 us (0.978)
  waiting for transfers between devices: 12.1 us -> 10.8 us
    ppermute x2, waiting for transfers between devices: 6.78 us -> 5.48 us  [moved(): return lax.ppermute(block, axis, route)]
    pallas_call x5 -> x6, Pallas kernels: 7.32 us -> 7.46 us  [near_call(): pl.pallas_call(kernel, out_shape=outs, in_specs=places, out_specs=jax.tre...]
  transfers between devices with their start and end apart: 4 -> 4, of which waited for: 3 -> 3; matrix products, arithmetic and copies ran while one was open for 0% -> 0% of each run, Pallas kernels for 7% -> 8%
where the time goes in v9:
time: 52.4 us; the launch traced here: 52.1 us
  blocking collectives  17.1 us (33%)
  starting transfers between devices  13.5 us (26%)
  waiting for transfers between devices  10.8 us (21%)
  Pallas kernels  10.6 us (20%)
    all_to_all x1, blocking collectives, per_device(): received = lax.all_to_all(partial.reshape(tp, own, model_width), 'tp', 0, 0)  17.1 us
    ppermute x2, starting transfers between devices, paired(): return lax.ppermute(block, axis, route)  7.66 us
    pallas_call x6, Pallas kernels, near_call(): pl.pallas_call(kernel, out_shape=outs, in_specs=places, out_specs=jax.tre...  7.46 us
    ppermute x2, starting transfers between devices, moved(): return lax.ppermute(block, axis, route)  5.84 us
    ppermute x2, waiting for transfers between devices, moved(): return lax.ppermute(block, axis, route)  5.48 us
    ppermute x2, waiting for transfers between devices, paired(): return lax.ppermute(block, axis, route)  5.28 us
    pallas_call x1, Pallas kernels, per_device(): pl.pallas_call(project_kernel, out_shape=[shape((count, 2 * head_cols), b...  3.15 us
  transfers between devices with their start and end apart: 4, of which 3 were waited for; matrix products, arithmetic and copies ran while one was open for 0% of the time, Pallas kernels for 8%

profile of v9, /device:TPU:314, one launch (start us, length us, event | category | flops | bytes accessed | tf_op | source)
XLA Modules:
  0.0 52.1 jit_solution(1939127546565134758)
XLA Ops:
  0.0 0.0 copy-start
  0.0 0.0 copy-start.2
  0.0 0.0 copy-start.5
  0.0 3.2 %project.1 = (bf16[256,512]{1,0:T(8,128)(2,1)S(1)}, bf16[256,512]{1,0:T(8,128)(2,1)S(1)}, bf16[144,512]{1,0:T(8,128)(2,1)S(1)}, bf16[144,512]{1,0:T(8,128)(2,1)S(1)}) custom-call(s32[1]{0:T(128)} %bitcast.1.row, s32[1]{0:T(128)} %bitcast.2.col, s32[1]{0:T(128)} %bitcast.place, bf16[256,1024]{1,0:T(8,128)(2,1)} %bitcast.11, f32[1,1024]{1,0:T(1,128)} %bitcast.16, ...), custom_call_target="tpu_custom_call" | custom-call | tf_op jit(solution)/shard_map/project/pallas_call | solution.py:406
  3.2 4.2 %collective-permute-start = (bf16[144,512]{1,0:T(8,128)(2,1)S(1)}, bf16[144,512]{1,0:T(8,128)(2,1)S(1)}, u32[]{:S(2)}, u32[]{:S(2)}) collective-permute-start(bf16[144,512]{1,0:T(8,128)(2,1)S(1)} %get-tuple-element.25), channel_id=1, source_target_pairs={{32,64},{64,32},{96,128},{128,96},{160,192},{192,160},{224,256},{2... | collective-permute-start | bytes 442376 | tf_op jit(solution)/shard_map/ppermute | solution.py:381
  7.3 3.5 %collective-permute-start.1 = (bf16[144,512]{1,0:T(8,128)(2,1)S(1)}, bf16[144,512]{1,0:T(8,128)(2,1)S(1)}, u32[]{:S(2)}, u32[]{:S(2)}) collective-permute-start(bf16[144,512]{1,0:T(8,128)(2,1)S(1)} %get-tuple-element.26), channel_id=1, source_target_pairs={{0,32},{32,0},{64,96},{96,64},{128,160},{160,128},{192,224},{224,1... | collective-permute-start | bytes 442376 | tf_op jit(solution)/shard_map/ppermute | solution.py:381
  10.8 0.0 copy-done
  10.9 0.0 copy-done.2
  10.9 0.0 copy-done.5
  10.9 2.1 %core.1 = (bf16[256,256]{1,0:T(8,128)(2,1)S(1)}, f32[256,512]{1,0:T(8,128)S(1)}, f32[192,256]{1,0:T(8,128)S(1)}, f32[192,256]{1,0:T(8,128)S(1)}, f32[336,576]{1,0:T(8,128)S(1)}, /*index=5*/f32[336,576]{1,0:T(8,128)S(1)}) custom-call(s32[1]{0:T(128)} %bitcast.1.row, s32[1]{0:T(128)} %bitcast.2.col, bf16[256,512]{1,0:T(8,128)(2,1)S(1)} %get-tuple-element.23.kv, ...), custom_call_target="tpu_custom_call" | custom-call | tf_op jit(solution)/shard_map/core/pallas_call | solution.py:53
  13.0 5.3 %collective-permute-done.far = bf16[144,512]{1,0:T(8,128)(2,1)S(1)} collective-permute-done((bf16[144,512]{1,0:T(8,128)(2,1)S(1)}, bf16[144,512]{1,0:T(8,128)(2,1)S(1)}, u32[]{:S(2)}, u32[]{:S(2)}) %collective-permute-start) | collective-permute-done | bytes 147488 | tf_op jit(solution)/shard_map/ppermute | solution.py:381
  18.3 0.0 collective-permute-done.1.near
  18.3 0.4 edges.1
  18.8 1.9 %collective-permute-start.3 = (bf16[240,512]{1,0:T(8,128)(2,1)S(1)}, bf16[240,512]{1,0:T(8,128)(2,1)S(1)}, u32[]{:S(2)}, u32[]{:S(2)}) collective-permute-start(bf16[240,512]{1,0:T(8,128)(2,1)S(1)} %get-tuple-element.28.leftward), channel_id=1, source_target_pairs={{4,0},{8,4},{12,8},{16,12},{20,16},{24,20},{28,24},{5,1},{9,5},{13... | collective-permute-start | bytes 737288 | tf_op jit(solution)/shard_map/ppermute | solution.py:387
  20.7 3.9 %collective-permute-start.2 = (bf16[240,512]{1,0:T(8,128)(2,1)S(1)}, bf16[240,512]{1,0:T(8,128)(2,1)S(1)}, u32[]{:S(2)}, u32[]{:S(2)}) collective-permute-start(bf16[240,512]{1,0:T(8,128)(2,1)S(1)} %get-tuple-element.29.rightward), channel_id=1, source_target_pairs={{0,4},{4,8},{8,12},{12,16},{16,20},{20,24},{24,28},{1,5},{5,9},{9,... | collective-permute-start | bytes 737288 | tf_op jit(solution)/shard_map/ppermute | solution.py:387
  24.6 0.0 copy-start.1
  24.6 1.3 %middle.1 = (bf16[256,256]{1,0:T(8,128)(2,1)S(1)}, f32[256,512]{1,0:T(8,128)S(1)}) custom-call(bf16[448,512]{1,0:T(8,128)(2,1)S(1)} %get-tuple-element.34.kv, bf16[352,512]{1,0:T(8,128)(2,1)S(1)} %get-tuple-element.35.qg, f32[192,256]{1,0:T(8,128)S(1)} %get-tuple-element.36.top_bias, f32[192,256]{1,0:T(8,128)S(1)} %get-tuple-element.37.bottom_bias, ...), custom_call_target="tpu_custom_call" | custom-call | tf_op jit(solution)/shard_map/middle/pallas_call | solution.py:53
  25.9 3.3 %collective-permute-done.3.from_right = bf16[240,512]{1,0:T(8,128)(2,1)S(1)} collective-permute-done((bf16[240,512]{1,0:T(8,128)(2,1)S(1)}, bf16[240,512]{1,0:T(8,128)(2,1)S(1)}, u32[]{:S(2)}, u32[]{:S(2)}) %collective-permute-start.3) | collective-permute-done | bytes 245792 | tf_op jit(solution)/shard_map/ppermute | solution.py:387
  29.3 1.0 %right_side.1 = (bf16[72,256]{1,0:T(8,128)(2,1)S(1)}, f32[112,512]{1,0:T(8,128)S(1)}) custom-call(bf16[240,512]{1,0:T(8,128)(2,1)S(1)} %get-tuple-element.29.rightward, bf16[240,512]{1,0:T(8,128)(2,1)S(1)} %collective-permute-done.3.from_right, f32[336,576]{1,0:T(8,128)S(1)} %get-tuple-element.31.right_bias), custom_call_target="tpu_custom_call" | custom-call | tf_op jit(solution)/shard_map/right_side/pallas_call | solution.py:53
  30.2 2.1 %collective-permute-done.2.from_left = bf16[240,512]{1,0:T(8,128)(2,1)S(1)} collective-permute-done((bf16[240,512]{1,0:T(8,128)(2,1)S(1)}, bf16[240,512]{1,0:T(8,128)(2,1)S(1)}, u32[]{:S(2)}, u32[]{:S(2)}) %collective-permute-start.2) | collective-permute-done | bytes 245792 | tf_op jit(solution)/shard_map/ppermute | solution.py:387
  32.4 0.0 copy-done.1
  32.4 0.0 copy-start.3
  32.4 0.0 copy-start.4
  32.4 0.0 copy-start.6
  32.4 1.7 %sides.1 = bf16[256,1024]{1,0:T(8,128)(2,1)S(1)} custom-call(bf16[240,512]{1,0:T(8,128)(2,1)S(1)} %get-tuple-element.28.leftward, bf16[240,512]{1,0:T(8,128)(2,1)S(1)} %collective-permute-done.2.from_left, f32[336,576]{1,0:T(8,128)S(1)} %get-tuple-element.30.left_bias, bf16[72,256]{1,0:T(8,128)(2,1)S(1)} %get-tuple-element.32.right_query, ...), custom_call_target="tpu_custom_call" | custom-call | tf_op jit(solution)/shard_map/sides/pallas_call | solution.py:53
  34.1 17.1 %all_to_all.5.received = bf16[4,64,1024]{2,1,0:T(8,128)(2,1)S(1)} all-to-all(bf16[4,64,1024]{2,1,0:T(8,128)(2,1)S(1)} %bitcast.15), channel_id=1, replica_groups=mesh['row'=16,'col'=8,'tp'=4] {'tp'}, dimensions={0} | all-to-all | bytes 1048576 | tf_op jit(solution)/shard_map/all_to_all | solution.py:476
  51.2 0.0 copy-done.3
  51.2 0.0 copy-done.4
  51.2 0.0 copy-done.6
  51.2 0.9 %finish.1 = f32[64,1024]{1,0:T(8,128)} custom-call(s32[1]{0:T(128)} %bitcast.place, bf16[4,64,1024]{2,1,0:T(8,128)(2,1)S(1)} %all_to_all.5.received, bf16[256,1024]{1,0:T(8,128)(2,1)S(1)} %bitcast.12, f32[1,1024]{1,0:T(1,128)S(1)} %bitcast.17, bf16[256,1024]{1,0:T(8,128)(2,1)S(1)} %bitcast.14), custom_call_target="tpu_custom_call" | custom-call | tf_op jit(solution)/shard_map/finish/pallas_call | solution.py:53
Async XLA Ops:
  0.0 10.8 %copy-start = (bf16[736,448]{1,0:T(8,128)(2,1)S(1)}, bf16[736,448]{1,0:T(8,128)(2,1)}, u32[]{:S(2)}) copy-start(bf16[736,448]{1,0:T(8,128)(2,1)} %constant.21.clone.gather) | copy-start | bytes 1978372
  0.0 10.9 %copy-start.2 = (bf16[768,256]{1,0:T(8,128)(2,1)S(1)}, bf16[768,256]{1,0:T(8,128)(2,1)}, u32[]{:S(2)}) copy-start(bf16[768,256]{1,0:T(8,128)(2,1)} %constant.22.clone.spread) | copy-start | bytes 1179652
  0.0 10.9 %copy-start.5 = (f32[8,2176]{1,0:T(8,128)S(1)}, f32[8,2176]{1,0:T(8,128)}, u32[]{:S(2)}) copy-start(f32[8,2176]{1,0:T(8,128)} %constant.23.clone.points) | copy-start | bytes 208900
  3.2 15.1 %collective-permute-start = (bf16[144,512]{1,0:T(8,128)(2,1)S(1)}, bf16[144,512]{1,0:T(8,128)(2,1)S(1)}, u32[]{:S(2)}, u32[]{:S(2)}) collective-permute-start(bf16[144,512]{1,0:T(8,128)(2,1)S(1)} %get-tuple-element.25), channel_id=1, source_target_pairs={{32,64},{64,32},{96,128},{128,96},{160,192},{192,160},{224,256},{2... | collective-permute-start | bytes 442376 | tf_op jit(solution)/shard_map/ppermute | solution.py:381
  7.3 11.0 %collective-permute-start.1 = (bf16[144,512]{1,0:T(8,128)(2,1)S(1)}, bf16[144,512]{1,0:T(8,128)(2,1)S(1)}, u32[]{:S(2)}, u32[]{:S(2)}) collective-permute-start(bf16[144,512]{1,0:T(8,128)(2,1)S(1)} %get-tuple-element.26), channel_id=1, source_target_pairs={{0,32},{32,0},{64,96},{96,64},{128,160},{160,128},{192,224},{224,1... | collective-permute-start | bytes 442376 | tf_op jit(solution)/shard_map/ppermute | solution.py:381
  18.8 10.5 %collective-permute-start.3 = (bf16[240,512]{1,0:T(8,128)(2,1)S(1)}, bf16[240,512]{1,0:T(8,128)(2,1)S(1)}, u32[]{:S(2)}, u32[]{:S(2)}) collective-permute-start(bf16[240,512]{1,0:T(8,128)(2,1)S(1)} %get-tuple-element.28.leftward), channel_id=1, source_target_pairs={{4,0},{8,4},{12,8},{16,12},{20,16},{24,20},{28,24},{5,1},{9,5},{13... | collective-permute-start | bytes 737288 | tf_op jit(solution)/shard_map/ppermute | solution.py:387
  20.7 11.7 %collective-permute-start.2 = (bf16[240,512]{1,0:T(8,128)(2,1)S(1)}, bf16[240,512]{1,0:T(8,128)(2,1)S(1)}, u32[]{:S(2)}, u32[]{:S(2)}) collective-permute-start(bf16[240,512]{1,0:T(8,128)(2,1)S(1)} %get-tuple-element.29.rightward), channel_id=1, source_target_pairs={{0,4},{4,8},{8,12},{12,16},{16,20},{20,24},{24,28},{1,5},{5,9},{9,... | collective-permute-start | bytes 737288 | tf_op jit(solution)/shard_map/ppermute | solution.py:387
  24.6 7.8 %copy-start.1 = (bf16[1024,3,256]{2,0,1:T(8,128)(2,1)S(1)}, bf16[1024,3,256]{2,0,1:T(8,128)(2,1)}, u32[]{:S(2)}) copy-start(bf16[1024,3,256]{2,0,1:T(8,128)(2,1)} %param.10) | copy-start | bytes 4718596
  32.4 18.8 %copy-start.3 = (bf16[16,16,1024]{2,1,0:T(8,128)(2,1)S(1)}, bf16[16,16,1024]{2,1,0:T(8,128)(2,1)}, u32[]{:S(2)}) copy-start(bf16[16,16,1024]{2,1,0:T(8,128)(2,1)} %param.8) | copy-start | bytes 1572868
  32.4 18.8 %copy-start.4 = (bf16[16,16,1024]{2,1,0:T(8,128)(2,1)S(1)}, bf16[16,16,1024]{2,1,0:T(8,128)(2,1)}, u32[]{:S(2)}) copy-start(bf16[16,16,1024]{2,1,0:T(8,128)(2,1)} %param.12) | copy-start | bytes 1572868
  32.4 18.8 %copy-start.6 = (f32[1024]{0:T(1024)S(1)}, f32[1024]{0:T(1024)}, u32[]{:S(2)}) copy-start(f32[1024]{0:T(1024)} %param.9) | copy-start | bytes 12292

commit v10 on v9

--- a/solution.py
+++ b/solution.py
@@ -73,13 +73,6 @@
     return jnp.dot(a, b, preferred_element_type=f32)
 
 
-def table(out_rows, in_rows, pairs):
-    filled = np.zeros((out_rows, in_rows), np.float32)
-    for target, source in pairs:
-        filled[target, source] = 1.0
-    return jnp.asarray(filled, bf16)
-
-
 def strip_pairs(lines, count, first):
     return [
         (line * count + step, line * SIDE + first + step)
@@ -124,7 +117,10 @@
     for part, rows in enumerate((TOP, BOTTOM)):
         for t, (y, x) in enumerate(cells(rows, INNER)):
             pairs.append((begin + part * RIM_QUERIES + t, (y + RADIUS) * SIDE + x))
-    return table(begin + 2 * RIM_QUERIES, WIDE * SIDE, pairs)
+    sources = np.full((begin + 2 * RIM_QUERIES,), -1.0, np.float32)
+    for target, source in pairs:
+        sources[target] = source
+    return sources
 
 
 def spreads():
@@ -145,7 +141,10 @@
     for part, first in enumerate((0, SIDE - RADIUS)):
         for t, f in strip_pairs(TALL, RADIUS, first):
             add("queries", part * QG_EDGE + t, f - QG_ROWS)
-    return table(3 * SIDE * SIDE, SIDE * SIDE, pairs)
+    targets = np.full((3, SIDE * SIDE), -1.0, np.float32)
+    for target, column in pairs:
+        targets[target // (SIDE * SIDE), column] = target % (SIDE * SIDE)
+    return targets
 
 
 def coords(rows, cols, total, pad):
@@ -172,7 +171,10 @@
     joined = np.full((8, queries.shape[1]), FAR, np.float32)
     joined[:2, : keys.shape[1]] = keys
     joined[2:4] = queries
-    return jnp.asarray(joined)
+    sources = gathers()
+    joined[4, : sources.shape[0]] = sources
+    joined[5:, : SIDE * SIDE] = spreads()
+    return jnp.asarray(joined), (sources.shape[0], WIDE * SIDE)
 
 
 def project_kernel(
@@ -226,7 +228,7 @@
     return kv_all, qg_all
 
 
-def edges_kernel(row, kv, qg, far, near, gather, after, left, right, kv_tall, qg_tall):
+def edges_kernel(row, kv, qg, far, near, gather, left, right, kv_tall, qg_tall):
     kv_all, qg_all = tall_blocks(row, kv, qg, far, near)
     kv_tall[...] = kv_all
     qg_tall[...] = qg_all
@@ -286,7 +288,16 @@
     count = kv.shape[0]
     width = kv.shape[1] // 2
     spot = (row[0], col[0])
-    keys, queries = points[...].T, points[2:4]
+    columns = points[...].T
+    keys, queries = columns[:, :2], points[2:4]
+    picked = columns[: gather.shape[0], 4:5].astype(jnp.int32)
+    sources = lax.broadcasted_iota(jnp.int32, gather.shape, 1)
+    gather[...] = jnp.where(sources == picked, 1.0, 0.0).astype(bf16)
+    tokens = lax.broadcasted_iota(jnp.int32, (count, count), 0)
+    for part in range(3):
+        targets = points[5 + part : 6 + part, :count].astype(jnp.int32)
+        hits = jnp.where(tokens == targets, 1.0, 0.0).astype(bf16)
+        spread[part * count : (part + 1) * count] = hits
 
     def mask(first_key, key_count, first_query, query_count):
         at_keys = keys[first_key : first_key + key_count]
@@ -431,13 +442,19 @@
     near = paired(near, "row", 0)
     bias = shape((2 * KV_EDGE, 2 * QG_EDGE * heads), f32)
     rim = shape((RIM_KEYS, RIM_QUERIES * heads), f32)
-    gather, spread = gathers(), spreads()
-    core_query, core_pair, top_bias, bottom_bias, left_bias, right_bias = near_call(
+    points, gather_shape = places(heads)
+    gather, spread, core_query, core_pair, top_bias, bottom_bias, left_bias, right_bias = near_call(
         functools.partial(core_kernel, extent),
         "core",
-        [shape((count, head_cols), bf16), shape((count, 2 * head_cols), f32), rim, rim, bias, bias],
-        [SMEM] * 2 + [VMEM] * 5,
-        row, col, kv, qg, places(heads), gather, spread,
+        [
+            shape(gather_shape, bf16),
+            shape((3 * count, count), bf16),
+            shape((count, head_cols), bf16),
+            shape((count, 2 * head_cols), f32),
+            rim, rim, bias, bias,
+        ],
+        [SMEM] * 2 + [VMEM] * 3,
+        row, col, kv, qg, points,
     )
     side = shape((KV_EDGE + QG_EDGE, 2 * head_cols), bf16)
     tall = [shape((lines * SIDE, 2 * head_cols), bf16) for lines in (WIDE, TALL)]
@@ -445,8 +462,8 @@
         edges_kernel,
         "edges",
         [side] * 2 + tall,
-        [SMEM] + [VMEM] * 6,
-        row, kv, qg, far, near, gather, core_query,
+        [SMEM] + [VMEM] * 5,
+        row, kv, qg, far, near, gather,
     )
     from_left = moved(rightward, "col", 1)
     from_right = moved(leftward, "col", -1)

time: 52.4 us -> 52.3 us (level)
  transfers between devices with their start and end apart: 4 -> 4, of which waited for: 3 -> 3; matrix products, arithmetic and copies ran while one was open for 0% -> 0% of each run, Pallas kernels for 8% -> 9%
where the time goes in v10:
time: 52.3 us; the launch traced here: 52 us
  blocking collectives  17.1 us (33%)
  starting transfers between devices  13.5 us (26%)
  Pallas kernels  10.7 us (20%)
  waiting for transfers between devices  10.6 us (20%)
    all_to_all x1, blocking collectives, per_device(): received = lax.all_to_all(partial.reshape(tp, own, model_width), 'tp', 0, 0)  17.1 us
    pallas_call x6, Pallas kernels, near_call(): pl.pallas_call(kernel, out_shape=outs, in_specs=places, out_specs=jax.tre...  7.66 us
    ppermute x2, starting transfers between devices, paired(): return lax.ppermute(block, axis, route)  7.66 us
    ppermute x2, starting transfers between devices, moved(): return lax.ppermute(block, axis, route)  5.84 us
    ppermute x2, waiting for transfers between devices, moved(): return lax.ppermute(block, axis, route)  5.48 us
    ppermute x2, waiting for transfers between devices, paired(): return lax.ppermute(block, axis, route)  5.09 us
    pallas_call x1, Pallas kernels, per_device(): pl.pallas_call(project_kernel, out_shape=[shape((count, 2 * head_cols), b...  3.08 us
  transfers between devices with their start and end apart: 4, of which 3 were waited for; matrix products, arithmetic and copies ran while one was open for 0% of the time, Pallas kernels for 9%

profile of v10, /device:TPU:314, one launch (start us, length us, event | category | flops | bytes accessed | tf_op | source)
XLA Modules:
  0.0 52.0 jit_solution(7453823374852917671)
XLA Ops:
  0.0 0.0 copy-start.3
  0.0 3.1 %project.1 = (bf16[256,512]{1,0:T(8,128)(2,1)S(1)}, bf16[256,512]{1,0:T(8,128)(2,1)S(1)}, bf16[144,512]{1,0:T(8,128)(2,1)S(1)}, bf16[144,512]{1,0:T(8,128)(2,1)S(1)}) custom-call(s32[1]{0:T(128)} %bitcast.1.row, s32[1]{0:T(128)} %bitcast.2.col, s32[1]{0:T(128)} %bitcast.place, bf16[256,1024]{1,0:T(8,128)(2,1)} %bitcast.11, f32[1,1024]{1,0:T(1,128)} %bitcast.16, ...), custom_call_target="tpu_custom_call" | custom-call | tf_op jit(solution)/shard_map/project/pallas_call | solution.py:417
  3.1 4.2 %collective-permute-start = (bf16[144,512]{1,0:T(8,128)(2,1)S(1)}, bf16[144,512]{1,0:T(8,128)(2,1)S(1)}, u32[]{:S(2)}, u32[]{:S(2)}) collective-permute-start(bf16[144,512]{1,0:T(8,128)(2,1)S(1)} %get-tuple-element.27), channel_id=1, source_target_pairs={{32,64},{64,32},{96,128},{128,96},{160,192},{192,160},{224,256},{2... | collective-permute-start | bytes 442376 | tf_op jit(solution)/shard_map/ppermute | solution.py:392
  7.3 3.5 %collective-permute-start.1 = (bf16[144,512]{1,0:T(8,128)(2,1)S(1)}, bf16[144,512]{1,0:T(8,128)(2,1)S(1)}, u32[]{:S(2)}, u32[]{:S(2)}) collective-permute-start(bf16[144,512]{1,0:T(8,128)(2,1)S(1)} %get-tuple-element.28), channel_id=1, source_target_pairs={{0,32},{32,0},{64,96},{96,64},{128,160},{160,128},{192,224},{224,1... | collective-permute-start | bytes 442376 | tf_op jit(solution)/shard_map/ppermute | solution.py:392
  10.8 0.0 copy-done.3
  10.8 2.4 %core.1 = (bf16[736,448]{1,0:T(8,128)(2,1)S(1)}, bf16[768,256]{1,0:T(8,128)(2,1)S(1)}, bf16[256,256]{1,0:T(8,128)(2,1)S(1)}, f32[256,512]{1,0:T(8,128)S(1)}, f32...) custom-call(s32[1]{0:T(128)} %bitcast.1.row, s32[1]{0:T(128)} %bitcast.2.col, ...), custom_call_target="tpu_custom_call" | custom-call | tf_op jit(solution)/shard_map/core/pallas_call | solution.py:53
  13.1 5.1 %collective-permute-done.far = bf16[144,512]{1,0:T(8,128)(2,1)S(1)} collective-permute-done((bf16[144,512]{1,0:T(8,128)(2,1)S(1)}, bf16[144,512]{1,0:T(8,128)(2,1)S(1)}, u32[]{:S(2)}, u32[]{:S(2)}) %collective-permute-start) | collective-permute-done | bytes 147488 | tf_op jit(solution)/shard_map/ppermute | solution.py:392
  18.2 0.0 collective-permute-done.1.near
  18.2 0.4 edges.1
  18.7 1.9 %collective-permute-start.3 = (bf16[240,512]{1,0:T(8,128)(2,1)S(1)}, bf16[240,512]{1,0:T(8,128)(2,1)S(1)}, u32[]{:S(2)}, u32[]{:S(2)}) collective-permute-start(bf16[240,512]{1,0:T(8,128)(2,1)S(1)} %get-tuple-element.30.leftward), channel_id=1, source_target_pairs={{4,0},{8,4},{12,8},{16,12},{20,16},{24,20},{28,24},{5,1},{9,5},{13... | collective-permute-start | bytes 737288 | tf_op jit(solution)/shard_map/ppermute | solution.py:398
  20.6 3.9 %collective-permute-start.2 = (bf16[240,512]{1,0:T(8,128)(2,1)S(1)}, bf16[240,512]{1,0:T(8,128)(2,1)S(1)}, u32[]{:S(2)}, u32[]{:S(2)}) collective-permute-start(bf16[240,512]{1,0:T(8,128)(2,1)S(1)} %get-tuple-element.31.rightward), channel_id=1, source_target_pairs={{0,4},{4,8},{8,12},{12,16},{16,20},{20,24},{24,28},{1,5},{5,9},{9,... | collective-permute-start | bytes 737288 | tf_op jit(solution)/shard_map/ppermute | solution.py:398
  24.5 0.0 copy-start
  24.5 1.3 %middle.1 = (bf16[256,256]{1,0:T(8,128)(2,1)S(1)}, f32[256,512]{1,0:T(8,128)S(1)}) custom-call(bf16[448,512]{1,0:T(8,128)(2,1)S(1)} %get-tuple-element.36.kv, bf16[352,512]{1,0:T(8,128)(2,1)S(1)} %get-tuple-element.37.qg, f32[192,256]{1,0:T(8,128)S(1)} %get-tuple-element.38.top_bias, f32[192,256]{1,0:T(8,128)S(1)} %get-tuple-element.39.bottom_bias, ...), custom_call_target="tpu_custom_call" | custom-call | tf_op jit(solution)/shard_map/middle/pallas_call | solution.py:53
  25.8 3.3 %collective-permute-done.3.from_right = bf16[240,512]{1,0:T(8,128)(2,1)S(1)} collective-permute-done((bf16[240,512]{1,0:T(8,128)(2,1)S(1)}, bf16[240,512]{1,0:T(8,128)(2,1)S(1)}, u32[]{:S(2)}, u32[]{:S(2)}) %collective-permute-start.3) | collective-permute-done | bytes 245792 | tf_op jit(solution)/shard_map/ppermute | solution.py:398
  29.2 1.0 %right_side.1 = (bf16[72,256]{1,0:T(8,128)(2,1)S(1)}, f32[112,512]{1,0:T(8,128)S(1)}) custom-call(bf16[240,512]{1,0:T(8,128)(2,1)S(1)} %get-tuple-element.31.rightward, bf16[240,512]{1,0:T(8,128)(2,1)S(1)} %collective-permute-done.3.from_right, f32[336,576]{1,0:T(8,128)S(1)} %get-tuple-element.33.right_bias), custom_call_target="tpu_custom_call" | custom-call | tf_op jit(solution)/shard_map/right_side/pallas_call | solution.py:53
  30.2 2.1 %collective-permute-done.2.from_left = bf16[240,512]{1,0:T(8,128)(2,1)S(1)} collective-permute-done((bf16[240,512]{1,0:T(8,128)(2,1)S(1)}, bf16[240,512]{1,0:T(8,128)(2,1)S(1)}, u32[]{:S(2)}, u32[]{:S(2)}) %collective-permute-start.2) | collective-permute-done | bytes 245792 | tf_op jit(solution)/shard_map/ppermute | solution.py:398
  32.3 0.0 copy-done
  32.3 0.0 copy-start.1
  32.3 0.0 copy-start.2
  32.3 0.0 copy-start.4
  32.3 1.7 %sides.1 = bf16[256,1024]{1,0:T(8,128)(2,1)S(1)} custom-call(bf16[240,512]{1,0:T(8,128)(2,1)S(1)} %get-tuple-element.30.leftward, bf16[240,512]{1,0:T(8,128)(2,1)S(1)} %collective-permute-done.2.from_left, f32[336,576]{1,0:T(8,128)S(1)} %get-tuple-element.32.left_bias, bf16[72,256]{1,0:T(8,128)(2,1)S(1)} %get-tuple-element.34.right_query, ...), custom_call_target="tpu_custom_call" | custom-call | tf_op jit(solution)/shard_map/sides/pallas_call | solution.py:53
  34.0 17.1 %all_to_all.5.received = bf16[4,64,1024]{2,1,0:T(8,128)(2,1)S(1)} all-to-all(bf16[4,64,1024]{2,1,0:T(8,128)(2,1)S(1)} %bitcast.15), channel_id=1, replica_groups=mesh['row'=16,'col'=8,'tp'=4] {'tp'}, dimensions={0} | all-to-all | bytes 1048576 | tf_op jit(solution)/shard_map/all_to_all | solution.py:493
  51.1 0.0 copy-done.1
  51.1 0.0 copy-done.2
  51.1 0.0 copy-done.4
  51.1 0.9 %finish.1 = f32[64,1024]{1,0:T(8,128)} custom-call(s32[1]{0:T(128)} %bitcast.place, bf16[4,64,1024]{2,1,0:T(8,128)(2,1)S(1)} %all_to_all.5.received, bf16[256,1024]{1,0:T(8,128)(2,1)S(1)} %bitcast.12, f32[1,1024]{1,0:T(1,128)S(1)} %bitcast.17, bf16[256,1024]{1,0:T(8,128)(2,1)S(1)} %bitcast.14), custom_call_target="tpu_custom_call" | custom-call | tf_op jit(solution)/shard_map/finish/pallas_call | solution.py:53
Async XLA Ops:
  0.0 10.8 %copy-start.3 = (f32[8,2176]{1,0:T(8,128)S(1)}, f32[8,2176]{1,0:T(8,128)}, u32[]{:S(2)}) copy-start(f32[8,2176]{1,0:T(8,128)} %constant.17.clone.points) | copy-start | bytes 208900
  3.1 15.1 %collective-permute-start = (bf16[144,512]{1,0:T(8,128)(2,1)S(1)}, bf16[144,512]{1,0:T(8,128)(2,1)S(1)}, u32[]{:S(2)}, u32[]{:S(2)}) collective-permute-start(bf16[144,512]{1,0:T(8,128)(2,1)S(1)} %get-tuple-element.27), channel_id=1, source_target_pairs={{32,64},{64,32},{96,128},{128,96},{160,192},{192,160},{224,256},{2... | collective-permute-start | bytes 442376 | tf_op jit(solution)/shard_map/ppermute | solution.py:392
  7.3 11.0 %collective-permute-start.1 = (bf16[144,512]{1,0:T(8,128)(2,1)S(1)}, bf16[144,512]{1,0:T(8,128)(2,1)S(1)}, u32[]{:S(2)}, u32[]{:S(2)}) collective-permute-start(bf16[144,512]{1,0:T(8,128)(2,1)S(1)} %get-tuple-element.28), channel_id=1, source_target_pairs={{0,32},{32,0},{64,96},{96,64},{128,160},{160,128},{192,224},{224,1... | collective-permute-start | bytes 442376 | tf_op jit(solution)/shard_map/ppermute | solution.py:392
  18.7 10.5 %collective-permute-start.3 = (bf16[240,512]{1,0:T(8,128)(2,1)S(1)}, bf16[240,512]{1,0:T(8,128)(2,1)S(1)}, u32[]{:S(2)}, u32[]{:S(2)}) collective-permute-start(bf16[240,512]{1,0:T(8,128)(2,1)S(1)} %get-tuple-element.30.leftward), channel_id=1, source_target_pairs={{4,0},{8,4},{12,8},{16,12},{20,16},{24,20},{28,24},{5,1},{9,5},{13... | collective-permute-start | bytes 737288 | tf_op jit(solution)/shard_map/ppermute | solution.py:398
  20.6 11.7 %collective-permute-start.2 = (bf16[240,512]{1,0:T(8,128)(2,1)S(1)}, bf16[240,512]{1,0:T(8,128)(2,1)S(1)}, u32[]{:S(2)}, u32[]{:S(2)}) collective-permute-start(bf16[240,512]{1,0:T(8,128)(2,1)S(1)} %get-tuple-element.31.rightward), channel_id=1, source_target_pairs={{0,4},{4,8},{8,12},{12,16},{16,20},{20,24},{24,28},{1,5},{5,9},{9,... | collective-permute-start | bytes 737288 | tf_op jit(solution)/shard_map/ppermute | solution.py:398
  24.5 7.8 %copy-start = (bf16[1024,3,256]{2,0,1:T(8,128)(2,1)S(1)}, bf16[1024,3,256]{2,0,1:T(8,128)(2,1)}, u32[]{:S(2)}) copy-start(bf16[1024,3,256]{2,0,1:T(8,128)(2,1)} %param.8) | copy-start | bytes 4718596
  32.3 18.8 %copy-start.1 = (bf16[16,16,1024]{2,1,0:T(8,128)(2,1)S(1)}, bf16[16,16,1024]{2,1,0:T(8,128)(2,1)}, u32[]{:S(2)}) copy-start(bf16[16,16,1024]{2,1,0:T(8,128)(2,1)} %param.6) | copy-start | bytes 1572868
  32.3 18.8 %copy-start.2 = (bf16[16,16,1024]{2,1,0:T(8,128)(2,1)S(1)}, bf16[16,16,1024]{2,1,0:T(8,128)(2,1)}, u32[]{:S(2)}) copy-start(bf16[16,16,1024]{2,1,0:T(8,128)(2,1)} %param.10) | copy-start | bytes 1572868
  32.3 18.8 %copy-start.4 = (f32[1024]{0:T(1024)S(1)}, f32[1024]{0:T(1024)}, u32[]{:S(2)}) copy-start(f32[1024]{0:T(1024)} %param.7) | copy-start | bytes 12292

commit v11 on v10

--- a/solution.py
+++ b/solution.py
@@ -228,16 +228,17 @@
     return kv_all, qg_all
 
 
-def edges_kernel(row, kv, qg, far, near, gather, left, right, kv_tall, qg_tall):
+def edges_kernel(row, col, kv, qg, far, near, gather, first, second, kv_tall, qg_tall):
     kv_all, qg_all = tall_blocks(row, kv, qg, far, near)
     kv_tall[...] = kv_all
     qg_tall[...] = qg_all
     kv_edges = nn(part_of(gather, GATHERS["kv_edges"]), kv_all).astype(bf16)
     qg_edges = nn(part_of(gather, GATHERS["qg_edges"]), qg_all).astype(bf16)
-    left[:KV_EDGE] = kv_edges[:KV_EDGE]
-    left[KV_EDGE:] = qg_edges[:QG_EDGE]
-    right[:KV_EDGE] = kv_edges[KV_EDGE:]
-    right[KV_EDGE:] = qg_edges[QG_EDGE:]
+    left = jnp.concatenate([kv_edges[:KV_EDGE], qg_edges[:QG_EDGE]], axis=0)
+    right = jnp.concatenate([kv_edges[KV_EDGE:], qg_edges[QG_EDGE:]], axis=0)
+    odd = lax.rem(col[0], 2) == 1
+    first[...] = jnp.where(odd, left, right)
+    second[...] = jnp.where(odd, right, left)
 
 
 def window_bias(spot, extent, keys, queries):
@@ -312,9 +313,19 @@
     pair_out[:, :width] = key_grad
     pair_out[:, width:] = value_grad
     first_key, first_query = count, lanes
-    for side in biases:
+    for side in biases[:2]:
         side[...] = mask(first_key, side.shape[0], first_query, side.shape[1])
         first_key, first_query = first_key + side.shape[0], first_query + side.shape[1]
+    key_count, query_count = biases[2].shape
+    left_keys = keys[first_key : first_key + key_count]
+    right_keys = keys[first_key + key_count : first_key + 2 * key_count]
+    left_queries = queries[:, first_query : first_query + query_count]
+    right_queries = queries[:, first_query + query_count : first_query + 2 * query_count]
+    odd = lax.rem(col[0], 2) == 1
+    for side, flip in ((biases[2], odd), (biases[3], jnp.logical_not(odd))):
+        at_keys = jnp.where(flip, left_keys, right_keys)
+        at_queries = jnp.where(flip, left_queries, right_queries)
+        side[...] = window_bias(spot, extent, at_keys, at_queries)
 
 
 def middle_kernel(
@@ -345,18 +356,20 @@
     return query_grad.astype(bf16), jnp.concatenate([key_grad, value_grad], axis=1)
 
 
-def right_kernel(rightward, from_right, right_bias, query_out, pair_out):
-    query_out[...], pair_out[...] = side_grads(rightward, from_right, right_bias)
+def first_side_kernel(mine, theirs, bias, query_out, pair_out):
+    query_out[...], pair_out[...] = side_grads(mine, theirs, bias)
 
 
 def sides_kernel(
-    leftward, from_left, left_bias, right_query, right_pair, query_mid, pair_mid, spread, weight,
-    partial
+    col, mine, theirs, bias, first_query, first_pair, query_mid, pair_mid, spread, weight, partial
 ):
     width = query_mid.shape[1]
-    left_query, left_pair = side_grads(leftward, from_left, left_bias)
-    query_side = jnp.concatenate([left_query, right_query[...]], axis=0)
-    pair_side = jnp.concatenate([left_pair, right_pair[...]], axis=0)
+    second_query, second_pair = side_grads(mine, theirs, bias)
+    odd = lax.rem(col[0], 2) == 1
+    queries = jnp.where(odd, first_query[...], second_query), jnp.where(odd, second_query, first_query[...])
+    pairs = jnp.where(odd, first_pair[...], second_pair), jnp.where(odd, second_pair, first_pair[...])
+    query_side = jnp.concatenate(queries, axis=0)
+    pair_side = jnp.concatenate(pairs, axis=0)
     coarse = pair_side.astype(bf16)
     fine = (pair_side - coarse.astype(f32)).astype(bf16)
     key_spread, query_spread = (part_of(spread, SPREADS[name]) for name in ("keys", "queries"))
@@ -389,12 +402,6 @@
     route = []
     for low in range(first, count - 1, 2):
         route += [(low, low + 1), (low + 1, low)]
-    return lax.ppermute(block, axis, route)
-
-
-def moved(block, axis, distance):
-    count = lax.axis_size(axis)
-    route = [(i, i + distance) for i in range(count) if 0 <= i + distance < count]
     return lax.ppermute(block, axis, route)
 
 
@@ -443,7 +450,7 @@
     bias = shape((2 * KV_EDGE, 2 * QG_EDGE * heads), f32)
     rim = shape((RIM_KEYS, RIM_QUERIES * heads), f32)
     points, gather_shape = places(heads)
-    gather, spread, core_query, core_pair, top_bias, bottom_bias, left_bias, right_bias = near_call(
+    gather, spread, core_query, core_pair, top_bias, bottom_bias, first_bias, second_bias = near_call(
         functools.partial(core_kernel, extent),
         "core",
         [
@@ -458,15 +465,15 @@
     )
     side = shape((KV_EDGE + QG_EDGE, 2 * head_cols), bf16)
     tall = [shape((lines * SIDE, 2 * head_cols), bf16) for lines in (WIDE, TALL)]
-    leftward, rightward, kv_tall, qg_tall = near_call(
+    first, second, kv_tall, qg_tall = near_call(
         edges_kernel,
         "edges",
         [side] * 2 + tall,
-        [SMEM] + [VMEM] * 5,
-        row, kv, qg, far, near, gather,
-    )
-    from_left = moved(rightward, "col", 1)
-    from_right = moved(leftward, "col", -1)
+        [SMEM] * 2 + [VMEM] * 5,
+        row, col, kv, qg, far, near, gather,
+    )
+    first_theirs = paired(first, "col", 0)
+    second_theirs = paired(second, "col", 1)
     query_mid, pair_mid = near_call(
         middle_kernel,
         "middle",
@@ -475,20 +482,20 @@
         kv_tall, qg_tall, top_bias, bottom_bias, gather, spread, core_query, core_pair,
     )
     own = count // tp
-    right_query, right_pair = near_call(
-        right_kernel,
-        "right_side",
+    first_query, first_pair = near_call(
+        first_side_kernel,
+        "first_side",
         [shape((QG_EDGE, head_cols), bf16), shape((OWN_EDGE, 2 * head_cols), f32)],
         [VMEM] * 3,
-        rightward, from_right, right_bias,
+        first, first_theirs, first_bias,
     )
     partial = near_call(
         sides_kernel,
         "sides",
         shape((count, model_width), bf16),
-        [VMEM] * 9,
-        leftward, from_left, left_bias, right_query, right_pair, query_mid, pair_mid, spread,
-        weight,
+        [SMEM] + [VMEM] * 9,
+        col, second, second_theirs, second_bias, first_query, first_pair, query_mid, pair_mid,
+        spread, weight,
     )
     received = lax.all_to_all(partial.reshape(tp, own, model_width), "tp", 0, 0)
     result = near_call(

time: 52.3 us -> 54.1 us (1.034)
  the two profiles are of different devices: /device:TPU:314 before, /device:TPU:250 now
where the time goes in v11:
time: 54.1 us; the launch traced here: 53.8 us
  blocking collectives  17 us (31%)
  starting transfers between devices  16.5 us (30%)
  Pallas kernels  10.7 us (20%)
  waiting for transfers between devices  9.38 us (17%)
    all_to_all x1, blocking collectives, per_device(): received = lax.all_to_all(partial.reshape(tp, own, model_width), 'tp', 0, 0)  17 us
    ppermute x4, starting transfers between devices, paired(): return lax.ppermute(block, axis, route)  16.5 us
    ppermute x4, waiting for transfers between devices, paired(): return lax.ppermute(block, axis, route)  9.38 us
    pallas_call x6, Pallas kernels, near_call(): pl.pallas_call(kernel, out_shape=outs, in_specs=places, out_specs=jax.tre...  7.61 us
    pallas_call x1, Pallas kernels, per_device(): pl.pallas_call(project_kernel, out_shape=[shape((count, 2 * head_cols), b...  3.08 us
  transfers between devices with their start and end apart: 4, of which 3 were waited for; matrix products, arithmetic and copies ran while one was open for 0% of the time, Pallas kernels for 9%

profile of v11, /device:TPU:250, one launch (start us, length us, event | category | flops | bytes accessed | tf_op | source)
XLA Modules:
  0.0 53.8 jit_solution(12295636007972575925)
XLA Ops:
  0.0 0.0 copy-start.3
  0.0 3.1 %project.1 = (bf16[256,512]{1,0:T(8,128)(2,1)S(1)}, bf16[256,512]{1,0:T(8,128)(2,1)S(1)}, bf16[144,512]{1,0:T(8,128)(2,1)S(1)}, bf16[144,512]{1,0:T(8,128)(2,1)S(1)}) custom-call(s32[1]{0:T(128)} %bitcast.2.row, s32[1]{0:T(128)} %bitcast.1.col, s32[1]{0:T(128)} %bitcast.place, bf16[256,1024]{1,0:T(8,128)(2,1)} %bitcast.11, f32[1,1024]{1,0:T(1,128)} %bitcast.16, ...), custom_call_target="tpu_custom_call" | custom-call | tf_op jit(solution)/shard_map/project/pallas_call | solution.py:424
  3.1 4.2 %collective-permute-start = (bf16[144,512]{1,0:T(8,128)(2,1)S(1)}, bf16[144,512]{1,0:T(8,128)(2,1)S(1)}, u32[]{:S(2)}, u32[]{:S(2)}) collective-permute-start(bf16[144,512]{1,0:T(8,128)(2,1)S(1)} %get-tuple-element.27), channel_id=1, source_target_pairs={{32,64},{64,32},{96,128},{128,96},{160,192},{192,160},{224,256},{2... | collective-permute-start | bytes 442376 | tf_op jit(solution)/shard_map/ppermute | solution.py:405
  7.3 3.5 %collective-permute-start.1 = (bf16[144,512]{1,0:T(8,128)(2,1)S(1)}, bf16[144,512]{1,0:T(8,128)(2,1)S(1)}, u32[]{:S(2)}, u32[]{:S(2)}) collective-permute-start(bf16[144,512]{1,0:T(8,128)(2,1)S(1)} %get-tuple-element.28), channel_id=1, source_target_pairs={{0,32},{32,0},{64,96},{96,64},{128,160},{160,128},{192,224},{224,1... | collective-permute-start | bytes 442376 | tf_op jit(solution)/shard_map/ppermute | solution.py:405
  10.8 0.0 copy-done.3
  10.8 2.4 %core.1 = (bf16[736,448]{1,0:T(8,128)(2,1)S(1)}, bf16[768,256]{1,0:T(8,128)(2,1)S(1)}, bf16[256,256]{1,0:T(8,128)(2,1)S(1)}, f32[256,512]{1,0:T(8,128)S(1)}, f32...) custom-call(s32[1]{0:T(128)} %bitcast.2.row, s32[1]{0:T(128)} %bitcast.1.col, ...), custom_call_target="tpu_custom_call" | custom-call | tf_op jit(solution)/shard_map/core/pallas_call | solution.py:53
  13.1 5.1 %collective-permute-done.far = bf16[144,512]{1,0:T(8,128)(2,1)S(1)} collective-permute-done((bf16[144,512]{1,0:T(8,128)(2,1)S(1)}, bf16[144,512]{1,0:T(8,128)(2,1)S(1)}, u32[]{:S(2)}, u32[]{:S(2)}) %collective-permute-start) | collective-permute-done | bytes 147488 | tf_op jit(solution)/shard_map/ppermute | solution.py:405
  18.2 0.0 collective-permute-done.1.near
  18.2 0.4 edges.1
  18.7 1.9 %collective-permute-start.3 = (bf16[240,512]{1,0:T(8,128)(2,1)S(1)}, bf16[240,512]{1,0:T(8,128)(2,1)S(1)}, u32[]{:S(2)}, u32[]{:S(2)}) collective-permute-start(bf16[240,512]{1,0:T(8,128)(2,1)S(1)} %get-tuple-element.32.mine), channel_id=1, source_target_pairs={{0,4},{4,0},{8,12},{12,8},{16,20},{20,16},{24,28},{28,24},{1,5},{5... | collective-permute-start | bytes 737288 | tf_op jit(solution)/shard_map/ppermute | solution.py:405
  20.6 7.0 %collective-permute-start.2 = (bf16[240,512]{1,0:T(8,128)(2,1)S(1)}, bf16[240,512]{1,0:T(8,128)(2,1)S(1)}, u32[]{:S(2)}, u32[]{:S(2)}) collective-permute-start(bf16[240,512]{1,0:T(8,128)(2,1)S(1)} %get-tuple-element.30.mine), channel_id=1, source_target_pairs={{4,8},{8,4},{12,16},{16,12},{20,24},{24,20},{5,9},{9,5},{13,17},{1... | collective-permute-start | bytes 737288 | tf_op jit(solution)/shard_map/ppermute | solution.py:405
  27.6 0.0 copy-start
  27.6 1.3 %middle.1 = (bf16[256,256]{1,0:T(8,128)(2,1)S(1)}, f32[256,512]{1,0:T(8,128)S(1)}) custom-call(bf16[448,512]{1,0:T(8,128)(2,1)S(1)} %get-tuple-element.36.kv, bf16[352,512]{1,0:T(8,128)(2,1)S(1)} %get-tuple-element.37.qg, f32[192,256]{1,0:T(8,128)S(1)} %get-tuple-element.38.top_bias, f32[192,256]{1,0:T(8,128)S(1)} %get-tuple-element.39.bottom_bias, ...), custom_call_target="tpu_custom_call" | custom-call | tf_op jit(solution)/shard_map/middle/pallas_call | solution.py:53
  28.9 0.3 collective-permute-done.3.theirs
  29.2 1.0 %first_side.1 = (bf16[72,256]{1,0:T(8,128)(2,1)S(1)}, f32[112,512]{1,0:T(8,128)S(1)}) custom-call(bf16[240,512]{1,0:T(8,128)(2,1)S(1)} %get-tuple-element.32.mine, bf16[240,512]{1,0:T(8,128)(2,1)S(1)} %collective-permute-done.3.theirs, f32[336,576]{1,0:T(8,128)S(1)} %get-tuple-element.33.bias), custom_call_target="tpu_custom_call" | custom-call | tf_op jit(solution)/shard_map/first_side/pallas_call | solution.py:53
  30.1 4.0 %collective-permute-done.2.theirs = bf16[240,512]{1,0:T(8,128)(2,1)S(1)} collective-permute-done((bf16[240,512]{1,0:T(8,128)(2,1)S(1)}, bf16[240,512]{1,0:T(8,128)(2,1)S(1)}, u32[]{:S(2)}, u32[]{:S(2)}) %collective-permute-start.2) | collective-permute-done | bytes 245792 | tf_op jit(solution)/shard_map/ppermute | solution.py:405
  34.1 0.0 copy-done
  34.1 0.0 copy-start.1
  34.1 0.0 copy-start.2
  34.1 0.0 copy-start.4
  34.1 1.6 %sides.1 = bf16[256,1024]{1,0:T(8,128)(2,1)S(1)} custom-call(s32[1]{0:T(128)} %bitcast.1.col, bf16[240,512]{1,0:T(8,128)(2,1)S(1)} %get-tuple-element.30.mine, bf16[240,512]{1,0:T(8,128)(2,1)S(1)} %collective-permute-done.2.theirs, f32[336,576]{1,0:T(8,128)S(1)} %get-tuple-element.31.bias, bf16[72,256]{1,0:T(8,128)(2,1)S(1)} %get-tuple-element.34.first_query, ...), custom_call_target="tpu_custom_call" | custom-call | tf_op jit(solution)/shard_map/sides/pallas_call | solution.py:53
  35.8 17.0 %all_to_all.5.received = bf16[4,64,1024]{2,1,0:T(8,128)(2,1)S(1)} all-to-all(bf16[4,64,1024]{2,1,0:T(8,128)(2,1)S(1)} %bitcast.15), channel_id=1, replica_groups=mesh['row'=16,'col'=8,'tp'=4] {'tp'}, dimensions={0} | all-to-all | bytes 1048576 | tf_op jit(solution)/shard_map/all_to_all | solution.py:500
  52.8 0.0 copy-done.1
  52.8 0.0 copy-done.2
  52.8 0.0 copy-done.4
  52.8 0.9 %finish.1 = f32[64,1024]{1,0:T(8,128)} custom-call(s32[1]{0:T(128)} %bitcast.place, bf16[4,64,1024]{2,1,0:T(8,128)(2,1)S(1)} %all_to_all.5.received, bf16[256,1024]{1,0:T(8,128)(2,1)S(1)} %bitcast.12, f32[1,1024]{1,0:T(1,128)S(1)} %bitcast.17, bf16[256,1024]{1,0:T(8,128)(2,1)S(1)} %bitcast.14), custom_call_target="tpu_custom_call" | custom-call | tf_op jit(solution)/shard_map/finish/pallas_call | solution.py:53
Async XLA Ops:
  0.0 10.8 %copy-start.3 = (f32[8,2176]{1,0:T(8,128)S(1)}, f32[8,2176]{1,0:T(8,128)}, u32[]{:S(2)}) copy-start(f32[8,2176]{1,0:T(8,128)} %constant.17.clone.points) | copy-start | bytes 208900
  3.1 15.1 %collective-permute-start = (bf16[144,512]{1,0:T(8,128)(2,1)S(1)}, bf16[144,512]{1,0:T(8,128)(2,1)S(1)}, u32[]{:S(2)}, u32[]{:S(2)}) collective-permute-start(bf16[144,512]{1,0:T(8,128)(2,1)S(1)} %get-tuple-element.27), channel_id=1, source_target_pairs={{32,64},{64,32},{96,128},{128,96},{160,192},{192,160},{224,256},{2... | collective-permute-start | bytes 442376 | tf_op jit(solution)/shard_map/ppermute | solution.py:405
  7.3 11.0 %collective-permute-start.1 = (bf16[144,512]{1,0:T(8,128)(2,1)S(1)}, bf16[144,512]{1,0:T(8,128)(2,1)S(1)}, u32[]{:S(2)}, u32[]{:S(2)}) collective-permute-start(bf16[144,512]{1,0:T(8,128)(2,1)S(1)} %get-tuple-element.28), channel_id=1, source_target_pairs={{0,32},{32,0},{64,96},{96,64},{128,160},{160,128},{192,224},{224,1... | collective-permute-start | bytes 442376 | tf_op jit(solution)/shard_map/ppermute | solution.py:405
  18.7 10.5 %collective-permute-start.3 = (bf16[240,512]{1,0:T(8,128)(2,1)S(1)}, bf16[240,512]{1,0:T(8,128)(2,1)S(1)}, u32[]{:S(2)}, u32[]{:S(2)}) collective-permute-start(bf16[240,512]{1,0:T(8,128)(2,1)S(1)} %get-tuple-element.32.mine), channel_id=1, source_target_pairs={{0,4},{4,0},{8,12},{12,8},{16,20},{20,16},{24,28},{28,24},{1,5},{5... | collective-permute-start | bytes 737288 | tf_op jit(solution)/shard_map/ppermute | solution.py:405
  20.6 13.5 %collective-permute-start.2 = (bf16[240,512]{1,0:T(8,128)(2,1)S(1)}, bf16[240,512]{1,0:T(8,128)(2,1)S(1)}, u32[]{:S(2)}, u32[]{:S(2)}) collective-permute-start(bf16[240,512]{1,0:T(8,128)(2,1)S(1)} %get-tuple-element.30.mine), channel_id=1, source_target_pairs={{4,8},{8,4},{12,16},{16,12},{20,24},{24,20},{5,9},{9,5},{13,17},{1... | collective-permute-start | bytes 737288 | tf_op jit(solution)/shard_map/ppermute | solution.py:405
  27.6 6.5 %copy-start = (bf16[1024,3,256]{2,0,1:T(8,128)(2,1)S(1)}, bf16[1024,3,256]{2,0,1:T(8,128)(2,1)}, u32[]{:S(2)}) copy-start(bf16[1024,3,256]{2,0,1:T(8,128)(2,1)} %param.8) | copy-start | bytes 4718596
  34.1 18.7 %copy-start.1 = (bf16[16,16,1024]{2,1,0:T(8,128)(2,1)S(1)}, bf16[16,16,1024]{2,1,0:T(8,128)(2,1)}, u32[]{:S(2)}) copy-start(bf16[16,16,1024]{2,1,0:T(8,128)(2,1)} %param.6) | copy-start | bytes 1572868
  34.1 18.7 %copy-start.2 = (bf16[16,16,1024]{2,1,0:T(8,128)(2,1)S(1)}, bf16[16,16,1024]{2,1,0:T(8,128)(2,1)}, u32[]{:S(2)}) copy-start(bf16[16,16,1024]{2,1,0:T(8,128)(2,1)} %param.10) | copy-start | bytes 1572868
  34.1 18.7 %copy-start.4 = (f32[1024]{0:T(1024)S(1)}, f32[1024]{0:T(1024)}, u32[]{:S(2)}) copy-start(f32[1024]{0:T(1024)} %param.7) | copy-start | bytes 12292

commit v12 on v10

--- a/solution.py
+++ b/solution.py
@@ -357,10 +357,8 @@
     left_query, left_pair = side_grads(leftward, from_left, left_bias)
     query_side = jnp.concatenate([left_query, right_query[...]], axis=0)
     pair_side = jnp.concatenate([left_pair, right_pair[...]], axis=0)
-    coarse = pair_side.astype(bf16)
-    fine = (pair_side - coarse.astype(f32)).astype(bf16)
     key_spread, query_spread = (part_of(spread, SPREADS[name]) for name in ("keys", "queries"))
-    pair = pair_mid[...] + (nn(key_spread, coarse) + nn(key_spread, fine))
+    pair = pair_mid[...] + nn(key_spread, pair_side.astype(bf16))
     query_grad = query_mid[...].astype(f32) + nn(query_spread, query_side)
     pair = pair.astype(bf16)
     total = nt(query_grad.astype(bf16), weight[0])

time: 52.3 us -> 52.2 us (level)
  no operation moved by 1% of the time
where the time goes in v12:
time: 52.2 us; the launch traced here: 52 us
  blocking collectives  17.1 us (33%)
  starting transfers between devices  13.5 us (26%)
  Pallas kernels  10.7 us (20%)
  waiting for transfers between devices  10.6 us (20%)
    all_to_all x1, blocking collectives, per_device(): received = lax.all_to_all(partial.reshape(tp, own, model_width), 'tp', 0, 0)  17.1 us
    ppermute x2, starting transfers between devices, paired(): return lax.ppermute(block, axis, route)  7.66 us
    pallas_call x6, Pallas kernels, near_call(): pl.pallas_call(kernel, out_shape=outs, in_specs=places, out_specs=jax.tre...  7.62 us
    ppermute x2, starting transfers between devices, moved(): return lax.ppermute(block, axis, route)  5.84 us
    ppermute x2, waiting for transfers between devices, moved(): return lax.ppermute(block, axis, route)  5.48 us
    ppermute x2, waiting for transfers between devices, paired(): return lax.ppermute(block, axis, route)  5.09 us
    pallas_call x1, Pallas kernels, per_device(): pl.pallas_call(project_kernel, out_shape=[shape((count, 2 * head_cols), b...  3.08 us
  transfers between devices with their start and end apart: 4, of which 3 were waited for; matrix products, arithmetic and copies ran while one was open for 0% of the time, Pallas kernels for 9%

profile of v12, /device:TPU:314, one launch (start us, length us, event | category | flops | bytes accessed | tf_op | source)
XLA Modules:
  0.0 52.0 jit_solution(3340775849183993899)
XLA Ops:
  0.0 0.0 copy-start.3
  0.0 3.1 %project.1 = (bf16[256,512]{1,0:T(8,128)(2,1)S(1)}, bf16[256,512]{1,0:T(8,128)(2,1)S(1)}, bf16[144,512]{1,0:T(8,128)(2,1)S(1)}, bf16[144,512]{1,0:T(8,128)(2,1)S(1)}) custom-call(s32[1]{0:T(128)} %bitcast.1.row, s32[1]{0:T(128)} %bitcast.2.col, s32[1]{0:T(128)} %bitcast.place, bf16[256,1024]{1,0:T(8,128)(2,1)} %bitcast.11, f32[1,1024]{1,0:T(1,128)} %bitcast.16, ...), custom_call_target="tpu_custom_call" | custom-call | tf_op jit(solution)/shard_map/project/pallas_call | solution.py:415
  3.1 4.2 %collective-permute-start = (bf16[144,512]{1,0:T(8,128)(2,1)S(1)}, bf16[144,512]{1,0:T(8,128)(2,1)S(1)}, u32[]{:S(2)}, u32[]{:S(2)}) collective-permute-start(bf16[144,512]{1,0:T(8,128)(2,1)S(1)} %get-tuple-element.27), channel_id=1, source_target_pairs={{32,64},{64,32},{96,128},{128,96},{160,192},{192,160},{224,256},{2... | collective-permute-start | bytes 442376 | tf_op jit(solution)/shard_map/ppermute | solution.py:390
  7.3 3.5 %collective-permute-start.1 = (bf16[144,512]{1,0:T(8,128)(2,1)S(1)}, bf16[144,512]{1,0:T(8,128)(2,1)S(1)}, u32[]{:S(2)}, u32[]{:S(2)}) collective-permute-start(bf16[144,512]{1,0:T(8,128)(2,1)S(1)} %get-tuple-element.28), channel_id=1, source_target_pairs={{0,32},{32,0},{64,96},{96,64},{128,160},{160,128},{192,224},{224,1... | collective-permute-start | bytes 442376 | tf_op jit(solution)/shard_map/ppermute | solution.py:390
  10.8 0.0 copy-done.3
  10.8 2.4 %core.1 = (bf16[736,448]{1,0:T(8,128)(2,1)S(1)}, bf16[768,256]{1,0:T(8,128)(2,1)S(1)}, bf16[256,256]{1,0:T(8,128)(2,1)S(1)}, f32[256,512]{1,0:T(8,128)S(1)}, f32...) custom-call(s32[1]{0:T(128)} %bitcast.1.row, s32[1]{0:T(128)} %bitcast.2.col, ...), custom_call_target="tpu_custom_call" | custom-call | tf_op jit(solution)/shard_map/core/pallas_call | solution.py:53
  13.1 5.1 %collective-permute-done.far = bf16[144,512]{1,0:T(8,128)(2,1)S(1)} collective-permute-done((bf16[144,512]{1,0:T(8,128)(2,1)S(1)}, bf16[144,512]{1,0:T(8,128)(2,1)S(1)}, u32[]{:S(2)}, u32[]{:S(2)}) %collective-permute-start) | collective-permute-done | bytes 147488 | tf_op jit(solution)/shard_map/ppermute | solution.py:390
  18.2 0.0 collective-permute-done.1.near
  18.2 0.4 edges.1
  18.7 1.9 %collective-permute-start.3 = (bf16[240,512]{1,0:T(8,128)(2,1)S(1)}, bf16[240,512]{1,0:T(8,128)(2,1)S(1)}, u32[]{:S(2)}, u32[]{:S(2)}) collective-permute-start(bf16[240,512]{1,0:T(8,128)(2,1)S(1)} %get-tuple-element.30.leftward), channel_id=1, source_target_pairs={{4,0},{8,4},{12,8},{16,12},{20,16},{24,20},{28,24},{5,1},{9,5},{13... | collective-permute-start | bytes 737288 | tf_op jit(solution)/shard_map/ppermute | solution.py:396
  20.6 3.9 %collective-permute-start.2 = (bf16[240,512]{1,0:T(8,128)(2,1)S(1)}, bf16[240,512]{1,0:T(8,128)(2,1)S(1)}, u32[]{:S(2)}, u32[]{:S(2)}) collective-permute-start(bf16[240,512]{1,0:T(8,128)(2,1)S(1)} %get-tuple-element.31.rightward), channel_id=1, source_target_pairs={{0,4},{4,8},{8,12},{12,16},{16,20},{20,24},{24,28},{1,5},{5,9},{9,... | collective-permute-start | bytes 737288 | tf_op jit(solution)/shard_map/ppermute | solution.py:396
  24.5 0.0 copy-start
  24.5 1.3 %middle.1 = (bf16[256,256]{1,0:T(8,128)(2,1)S(1)}, f32[256,512]{1,0:T(8,128)S(1)}) custom-call(bf16[448,512]{1,0:T(8,128)(2,1)S(1)} %get-tuple-element.36.kv, bf16[352,512]{1,0:T(8,128)(2,1)S(1)} %get-tuple-element.37.qg, f32[192,256]{1,0:T(8,128)S(1)} %get-tuple-element.38.top_bias, f32[192,256]{1,0:T(8,128)S(1)} %get-tuple-element.39.bottom_bias, ...), custom_call_target="tpu_custom_call" | custom-call | tf_op jit(solution)/shard_map/middle/pallas_call | solution.py:53
  25.8 3.3 %collective-permute-done.3.from_right = bf16[240,512]{1,0:T(8,128)(2,1)S(1)} collective-permute-done((bf16[240,512]{1,0:T(8,128)(2,1)S(1)}, bf16[240,512]{1,0:T(8,128)(2,1)S(1)}, u32[]{:S(2)}, u32[]{:S(2)}) %collective-permute-start.3) | collective-permute-done | bytes 245792 | tf_op jit(solution)/shard_map/ppermute | solution.py:396
  29.2 1.0 %right_side.1 = (bf16[72,256]{1,0:T(8,128)(2,1)S(1)}, f32[112,512]{1,0:T(8,128)S(1)}) custom-call(bf16[240,512]{1,0:T(8,128)(2,1)S(1)} %get-tuple-element.31.rightward, bf16[240,512]{1,0:T(8,128)(2,1)S(1)} %collective-permute-done.3.from_right, f32[336,576]{1,0:T(8,128)S(1)} %get-tuple-element.33.right_bias), custom_call_target="tpu_custom_call" | custom-call | tf_op jit(solution)/shard_map/right_side/pallas_call | solution.py:53
  30.2 2.1 %collective-permute-done.2.from_left = bf16[240,512]{1,0:T(8,128)(2,1)S(1)} collective-permute-done((bf16[240,512]{1,0:T(8,128)(2,1)S(1)}, bf16[240,512]{1,0:T(8,128)(2,1)S(1)}, u32[]{:S(2)}, u32[]{:S(2)}) %collective-permute-start.2) | collective-permute-done | bytes 245792 | tf_op jit(solution)/shard_map/ppermute | solution.py:396
  32.3 0.0 copy-done
  32.3 0.0 copy-start.1
  32.3 0.0 copy-start.2
  32.3 0.0 copy-start.4
  32.3 1.6 %sides.1 = bf16[256,1024]{1,0:T(8,128)(2,1)S(1)} custom-call(bf16[240,512]{1,0:T(8,128)(2,1)S(1)} %get-tuple-element.30.leftward, bf16[240,512]{1,0:T(8,128)(2,1)S(1)} %collective-permute-done.2.from_left, f32[336,576]{1,0:T(8,128)S(1)} %get-tuple-element.32.left_bias, bf16[72,256]{1,0:T(8,128)(2,1)S(1)} %get-tuple-element.34.right_query, ...), custom_call_target="tpu_custom_call" | custom-call | tf_op jit(solution)/shard_map/sides/pallas_call | solution.py:53
  34.0 17.1 %all_to_all.5.received = bf16[4,64,1024]{2,1,0:T(8,128)(2,1)S(1)} all-to-all(bf16[4,64,1024]{2,1,0:T(8,128)(2,1)S(1)} %bitcast.15), channel_id=1, replica_groups=mesh['row'=16,'col'=8,'tp'=4] {'tp'}, dimensions={0} | all-to-all | bytes 1048576 | tf_op jit(solution)/shard_map/all_to_all | solution.py:491
  51.0 0.0 copy-done.1
  51.0 0.0 copy-done.2
  51.0 0.0 copy-done.4
  51.0 0.9 %finish.1 = f32[64,1024]{1,0:T(8,128)} custom-call(s32[1]{0:T(128)} %bitcast.place, bf16[4,64,1024]{2,1,0:T(8,128)(2,1)S(1)} %all_to_all.5.received, bf16[256,1024]{1,0:T(8,128)(2,1)S(1)} %bitcast.12, f32[1,1024]{1,0:T(1,128)S(1)} %bitcast.17, bf16[256,1024]{1,0:T(8,128)(2,1)S(1)} %bitcast.14), custom_call_target="tpu_custom_call" | custom-call | tf_op jit(solution)/shard_map/finish/pallas_call | solution.py:53
Async XLA Ops:
  0.0 10.8 %copy-start.3 = (f32[8,2176]{1,0:T(8,128)S(1)}, f32[8,2176]{1,0:T(8,128)}, u32[]{:S(2)}) copy-start(f32[8,2176]{1,0:T(8,128)} %constant.17.clone.points) | copy-start | bytes 208900
  3.1 15.1 %collective-permute-start = (bf16[144,512]{1,0:T(8,128)(2,1)S(1)}, bf16[144,512]{1,0:T(8,128)(2,1)S(1)}, u32[]{:S(2)}, u32[]{:S(2)}) collective-permute-start(bf16[144,512]{1,0:T(8,128)(2,1)S(1)} %get-tuple-element.27), channel_id=1, source_target_pairs={{32,64},{64,32},{96,128},{128,96},{160,192},{192,160},{224,256},{2... | collective-permute-start | bytes 442376 | tf_op jit(solution)/shard_map/ppermute | solution.py:390
  7.3 11.0 %collective-permute-start.1 = (bf16[144,512]{1,0:T(8,128)(2,1)S(1)}, bf16[144,512]{1,0:T(8,128)(2,1)S(1)}, u32[]{:S(2)}, u32[]{:S(2)}) collective-permute-start(bf16[144,512]{1,0:T(8,128)(2,1)S(1)} %get-tuple-element.28), channel_id=1, source_target_pairs={{0,32},{32,0},{64,96},{96,64},{128,160},{160,128},{192,224},{224,1... | collective-permute-start | bytes 442376 | tf_op jit(solution)/shard_map/ppermute | solution.py:390
  18.7 10.5 %collective-permute-start.3 = (bf16[240,512]{1,0:T(8,128)(2,1)S(1)}, bf16[240,512]{1,0:T(8,128)(2,1)S(1)}, u32[]{:S(2)}, u32[]{:S(2)}) collective-permute-start(bf16[240,512]{1,0:T(8,128)(2,1)S(1)} %get-tuple-element.30.leftward), channel_id=1, source_target_pairs={{4,0},{8,4},{12,8},{16,12},{20,16},{24,20},{28,24},{5,1},{9,5},{13... | collective-permute-start | bytes 737288 | tf_op jit(solution)/shard_map/ppermute | solution.py:396
  20.6 11.7 %collective-permute-start.2 = (bf16[240,512]{1,0:T(8,128)(2,1)S(1)}, bf16[240,512]{1,0:T(8,128)(2,1)S(1)}, u32[]{:S(2)}, u32[]{:S(2)}) collective-permute-start(bf16[240,512]{1,0:T(8,128)(2,1)S(1)} %get-tuple-element.31.rightward), channel_id=1, source_target_pairs={{0,4},{4,8},{8,12},{12,16},{16,20},{20,24},{24,28},{1,5},{5,9},{9,... | collective-permute-start | bytes 737288 | tf_op jit(solution)/shard_map/ppermute | solution.py:396
  24.5 7.8 %copy-start = (bf16[1024,3,256]{2,0,1:T(8,128)(2,1)S(1)}, bf16[1024,3,256]{2,0,1:T(8,128)(2,1)}, u32[]{:S(2)}) copy-start(bf16[1024,3,256]{2,0,1:T(8,128)(2,1)} %param.8) | copy-start | bytes 4718596
  32.3 18.7 %copy-start.1 = (bf16[16,16,1024]{2,1,0:T(8,128)(2,1)S(1)}, bf16[16,16,1024]{2,1,0:T(8,128)(2,1)}, u32[]{:S(2)}) copy-start(bf16[16,16,1024]{2,1,0:T(8,128)(2,1)} %param.6) | copy-start | bytes 1572868
  32.3 18.7 %copy-start.2 = (bf16[16,16,1024]{2,1,0:T(8,128)(2,1)S(1)}, bf16[16,16,1024]{2,1,0:T(8,128)(2,1)}, u32[]{:S(2)}) copy-start(bf16[16,16,1024]{2,1,0:T(8,128)(2,1)} %param.10) | copy-start | bytes 1572868
  32.3 18.7 %copy-start.4 = (f32[1024]{0:T(1024)S(1)}, f32[1024]{0:T(1024)}, u32[]{:S(2)}) copy-start(f32[1024]{0:T(1024)} %param.7) | copy-start | bytes 12292
